TPU v7x, 32 devices: a whole 2x2x4 slice. The times are simulated.
32 devices in a mesh: dp: 8 (over z, x), tensor: 4 (over y, core).
Axes of the slice: x: 2, y: 2, z: 4, core: 2. Of those that a mesh axis runs over, the one named last changes fastest.
Arguments:
- images: bfloat16 [128, 196, 768], P('dp'), may hold values from -6 to 6
- keep_index: int32 [128, 49], P('dp'), may hold values from 0 to 195, as said below
- unshuffle: int32 [128, 196], P('dp'), may hold values from 0 to 195, as said below
- masked: int32 [128, 196], P('dp'), may hold values from 0 to 1, as said below
- image_valid: int32 [128], P('dp'), may hold values from 0 to 1
- encoder_in: float32 [768, 4, 1344], P('dp', 'tensor'), may hold values from -0.21875 to 0.21875
- encoder_out: float32 [4, 960, 768], P('tensor', 'dp'), may hold values from -0.21875 to 0.21875
- decoder_in: float32 [512, 4, 896], P('dp', 'tensor'), may hold values from -0.25 to 0.25
- decoder_out: float32 [4, 640, 512], P('tensor', 'dp'), may hold values from -0.25 to 0.25
- pixel_maps: float32 [1280, 768], P('dp'), may hold values from -0.21875 to 0.21875
- bridge_map: float32 [768, 512], P('dp'), may hold values from -0.21875 to 0.21875
- vector_pack: float32 [7, 1280], P(None, 'dp')
- first_encoder_in: float32 [768, 4, 1344], P('dp', 'tensor'), may hold values from -1.9073486e-05 to 1.9073486e-05
- first_encoder_out: float32 [4, 960, 768], P('tensor', 'dp'), may hold values from -1.9073486e-05 to 1.9073486e-05
- first_decoder_in: float32 [512, 4, 896], P('dp', 'tensor'), may hold values from -1.9073486e-05 to 1.9073486e-05
- first_decoder_out: float32 [4, 640, 512], P('tensor', 'dp'), may hold values from -1.9073486e-05 to 1.9073486e-05
- first_pixel_maps: float32 [1280, 768], P('dp'), may hold values from -1.9073486e-05 to 1.9073486e-05
- first_bridge_map: float32 [768, 512], P('dp'), may hold values from -1.9073486e-05 to 1.9073486e-05
- first_vector_pack: float32 [7, 1280], P(None, 'dp'), may hold values from -1.9073486e-05 to 1.9073486e-05
- second_encoder_in: float32 [768, 4, 1344], P('dp', 'tensor'), may hold values from 9.934108e-13 to 3.973643e-12
- second_encoder_out: float32 [4, 960, 768], P('tensor', 'dp'), may hold values from 9.934108e-13 to 3.973643e-12
- second_decoder_in: float32 [512, 4, 896], P('dp', 'tensor'), may hold values from 9.934108e-13 to 3.973643e-12
- second_decoder_out: float32 [4, 640, 512], P('tensor', 'dp'), may hold values from 9.934108e-13 to 3.973643e-12
- second_pixel_maps: float32 [1280, 768], P('dp'), may hold values from 9.934108e-13 to 3.973643e-12
- second_bridge_map: float32 [768, 512], P('dp'), may hold values from 9.934108e-13 to 3.973643e-12
- second_vector_pack: float32 [7, 1280], P(None, 'dp'), may hold values from 9.934108e-13 to 3.973643e-12
Outputs:
- loss_value: float32 [], replicated
- norm_pairs: float32 [2, 7], replicated
- next_first_encoder_in: float32 [768, 4, 1344], P('dp', 'tensor')
- next_first_encoder_out: float32 [4, 960, 768], P('tensor', 'dp')
- next_first_decoder_in: float32 [512, 4, 896], P('dp', 'tensor')
- next_first_decoder_out: float32 [4, 640, 512], P('tensor', 'dp')
- next_first_pixel_maps: float32 [1280, 768], P('dp')
- next_first_bridge_map: float32 [768, 512], P('dp')
- next_first_vector_pack: float32 [7, 1280], P(None, 'dp')
- next_second_encoder_in: float32 [768, 4, 1344], P('dp', 'tensor')
- next_second_encoder_out: float32 [4, 960, 768], P('tensor', 'dp')
- next_second_decoder_in: float32 [512, 4, 896], P('dp', 'tensor')
- next_second_decoder_out: float32 [4, 640, 512], P('tensor', 'dp')
- next_second_pixel_maps: float32 [1280, 768], P('dp')
- next_second_bridge_map: float32 [768, 512], P('dp')
- next_second_vector_pack: float32 [7, 1280], P(None, 'dp')
- next_encoder_in: float32 [768, 4, 1344], P('dp', 'tensor')
- next_encoder_out: float32 [4, 960, 768], P('tensor', 'dp')
- next_decoder_in: float32 [512, 4, 896], P('dp', 'tensor')
- next_decoder_out: float32 [4, 640, 512], P('tensor', 'dp')
- next_pixel_maps: float32 [1280, 768], P('dp')
- next_bridge_map: float32 [768, 512], P('dp')
- next_vector_pack: float32 [7, 1280], P(None, 'dp')
Inputs may be any that keep to these rules, and one draw needn't show every extreme that they name: `keep_index`: each row names 49 different patches, in the image's shuffled order. `unshuffle`: each row is a permutation of the patches' places, with unshuffle[b, keep_index[b, j]] = j. masked[b, p] = 1 exactly where unshuffle[b, p] >= 49.
All inputs are finite; a program needn't handle non-finite values.
Results may differ from a plain program's by a relative error of at most 0.0035.
The roundings to bfloat16 on the way count: a program that leaves them out, or rounds other values in their place, can miss the bound.
Values may be sent and summed in bfloat16 or wider, within the bound.
A program may use at most 192 MiB of HBM per device.

v0:
```python
import jax
import jax.numpy as jnp
from jax import lax
from jax.sharding import PartitionSpec as P

ENCODER_WIDTH = 768
H_E = 12
HD_E = 64
D_D = 512
H_D = 16
HD_D = 32
PATCH_DIM = 768
GRID_PATCHES = 14
IMAGE_PATCHES = 196
KEEP = 49


eps_norm = 1e-06
beta_one = 0.9
beta_two = 0.999
step_count = 7.0
learn_rate = 0.3
decay_matrix = 0.05
eps_moment = 1e-06
highest_precision = lax.Precision.HIGHEST


def sinusoid_table(feature_width, grid_side, patch_count):
    position = jnp.arange(patch_count, dtype=jnp.int32)
    quarter = feature_width // 4
    omegas = 1.0 / 10000.0 ** (jnp.arange(quarter, dtype=jnp.float32) / quarter)

    def half_table(coords):
        angles = coords.astype(jnp.float32)[:, None] * omegas[None, :]
        return jnp.concatenate([jnp.sin(angles), jnp.cos(angles)], axis=1)

    return jnp.concatenate(
        [half_table(position % grid_side), half_table(position // grid_side)], axis=1
    )


def norm_forward(stream, gain_row, shift_row):
    centred = stream - jnp.mean(stream, axis=-1, keepdims=True)
    inverse = lax.rsqrt(jnp.mean(centred * centred, axis=-1, keepdims=True) + eps_norm)
    unit_values = centred * inverse
    return (unit_values * gain_row + shift_row, unit_values, inverse)


def norm_backward(incoming, unit_values, inverse, gain_row):
    scaled = incoming * gain_row
    inner_part = (
        scaled
        - jnp.mean(scaled, axis=-1, keepdims=True)
        - unit_values * jnp.mean(scaled * unit_values, axis=-1, keepdims=True)
    )
    width = incoming.shape[-1]
    gain_grad = jnp.sum((incoming * unit_values).reshape(-1, width), axis=0)
    shift_grad = jnp.sum(incoming.reshape(-1, width), axis=0)
    return (inverse * inner_part, gain_grad, shift_grad)


def tensor_sum(partial_out):
    return lax.psum(partial_out.astype(jnp.bfloat16), "tensor").astype(jnp.float32)


def input_sum(partial_grad):
    return lax.psum(partial_grad.astype(jnp.bfloat16), "tensor").astype(jnp.float32)


def layer_forward(stream, w_input, w_output, vectors, head_count, head_dim):
    image_count, token_count, model_width = stream.shape
    inner_width = head_count * head_dim
    normed_one, unit_one, inverse_one = norm_forward(stream, vectors[0], vectors[1])
    input_one = normed_one.astype(jnp.bfloat16)
    raw_heads = jnp.einsum(
        "bsd,dc->bsc", input_one, w_input[:, : 3 * inner_width], preferred_element_type=jnp.float32
    )
    triple = raw_heads.astype(jnp.bfloat16).reshape(
        image_count, token_count, 3, head_count, head_dim
    )
    scores = jnp.einsum(
        "bqhd,bkhd->bhqk", triple[:, :, 0], triple[:, :, 1], preferred_element_type=jnp.float32
    ) * head_dim ** (-0.5)
    shifted = jnp.exp(scores - jnp.max(scores, axis=-1, keepdims=True))
    attention = shifted / jnp.sum(shifted, axis=-1, keepdims=True)
    mixed_heads = jnp.einsum(
        "bhqk,bkhd->bqhd",
        attention.astype(jnp.bfloat16),
        triple[:, :, 2],
        preferred_element_type=jnp.float32,
    )
    mixed_low = mixed_heads.reshape(image_count, token_count, inner_width).astype(jnp.bfloat16)
    attn_part = jnp.einsum(
        "bsc,cd->bsd", mixed_low, w_output[:inner_width], preferred_element_type=jnp.float32
    )
    after_attn = stream + tensor_sum(attn_part)
    normed_two, unit_two, inverse_two = norm_forward(after_attn, vectors[2], vectors[3])
    input_two = normed_two.astype(jnp.bfloat16)
    hidden = jnp.einsum(
        "bsd,dc->bsc", input_two, w_input[:, 3 * inner_width :], preferred_element_type=jnp.float32
    )
    active = jax.nn.gelu(hidden, approximate=False).astype(jnp.bfloat16)
    ffn_part = jnp.einsum(
        "bsc,cd->bsd", active, w_output[inner_width:], preferred_element_type=jnp.float32
    )
    result = after_attn + tensor_sum(ffn_part)
    saved_state = (
        unit_one,
        inverse_one,
        input_one,
        triple,
        attention,
        mixed_low,
        unit_two,
        inverse_two,
        input_two,
        hidden,
        active,
    )
    return (result, saved_state)


def layer_backward(stream_grad, saved_state, w_input, w_output, vectors, head_count, head_dim):
    (
        unit_one,
        inverse_one,
        input_one,
        triple,
        attention,
        mixed_low,
        unit_two,
        inverse_two,
        input_two,
        hidden,
        active,
    ) = saved_state
    image_count, token_count, model_width = stream_grad.shape
    inner_width = head_count * head_dim
    score_scale = head_dim ** (-0.5)
    grad_low = stream_grad.astype(jnp.bfloat16)
    grad_down = jnp.einsum("bsc,bsd->cd", active, grad_low, preferred_element_type=jnp.float32)
    grad_active = jnp.einsum(
        "bsd,cd->bsc", grad_low, w_output[inner_width:], preferred_element_type=jnp.float32
    )
    gelu_back = jax.vjp(lambda values: jax.nn.gelu(values, approximate=False), hidden)[1]
    grad_hidden = gelu_back(grad_active)[0].astype(jnp.bfloat16)
    grad_up = jnp.einsum("bsd,bsc->dc", input_two, grad_hidden, preferred_element_type=jnp.float32)
    grad_two_part = jnp.einsum(
        "bsc,dc->bsd",
        grad_hidden,
        w_input[:, 3 * inner_width :],
        preferred_element_type=jnp.float32,
    )
    grad_mid, gain_two, shift_two = norm_backward(
        input_sum(grad_two_part), unit_two, inverse_two, vectors[2]
    )
    grad_mid = grad_mid + stream_grad
    mid_low = grad_mid.astype(jnp.bfloat16)
    grad_attn_rows = jnp.einsum(
        "bsc,bsd->cd", mixed_low, mid_low, preferred_element_type=jnp.float32
    )
    grad_mixed = jnp.einsum(
        "bsd,cd->bsc", mid_low, w_output[:inner_width], preferred_element_type=jnp.float32
    )
    grad_mixed = grad_mixed.astype(jnp.bfloat16).reshape(
        image_count, token_count, head_count, head_dim
    )
    grad_values = jnp.einsum(
        "bhqk,bqhd->bkhd",
        attention.astype(jnp.bfloat16),
        grad_mixed,
        preferred_element_type=jnp.float32,
    )
    grad_attention = jnp.einsum(
        "bqhd,bkhd->bhqk", grad_mixed, triple[:, :, 2], preferred_element_type=jnp.float32
    )
    grad_scores = attention * (
        grad_attention - jnp.sum(attention * grad_attention, axis=-1, keepdims=True)
    )
    scores_low = grad_scores.astype(jnp.bfloat16)
    grad_queries = (
        jnp.einsum(
            "bhqk,bkhd->bqhd", scores_low, triple[:, :, 1], preferred_element_type=jnp.float32
        )
        * score_scale
    )
    grad_keys = (
        jnp.einsum(
            "bhqk,bqhd->bkhd", scores_low, triple[:, :, 0], preferred_element_type=jnp.float32
        )
        * score_scale
    )
    grad_raw = (
        jnp.stack([grad_queries, grad_keys, grad_values], axis=2)
        .reshape(image_count, token_count, 3 * inner_width)
        .astype(jnp.bfloat16)
    )
    grad_triple = jnp.einsum("bsd,bsc->dc", input_one, grad_raw, preferred_element_type=jnp.float32)
    grad_normed_one = input_sum(
        jnp.einsum(
            "bsc,dc->bsd",
            grad_raw,
            w_input[:, : 3 * inner_width],
            preferred_element_type=jnp.float32,
        )
    )
    grad_stream, gain_one, shift_one = norm_backward(
        grad_normed_one, unit_one, inverse_one, vectors[0]
    )
    grad_in_cols = jnp.concatenate([grad_triple, grad_up], axis=1)
    grad_out_rows = jnp.concatenate([grad_attn_rows, grad_down], axis=0)
    return (
        grad_stream + grad_mid,
        grad_in_cols,
        grad_out_rows,
        jnp.stack([gain_one, shift_one, gain_two, shift_two]),
    )


def shards(
    images,
    keep_index,
    unshuffle,
    masked,
    image_valid,
    encoder_in,
    encoder_out,
    decoder_in,
    decoder_out,
    pixel_maps,
    bridge_map,
    vector_pack,
    first_encoder_in,
    first_encoder_out,
    first_decoder_in,
    first_decoder_out,
    first_pixel_maps,
    first_bridge_map,
    first_vector_pack,
    second_encoder_in,
    second_encoder_out,
    second_decoder_in,
    second_decoder_out,
    second_pixel_maps,
    second_bridge_map,
    second_vector_pack,
):
    copies = (
        lax.all_gather(encoder_in.astype(jnp.bfloat16), "dp", axis=0, tiled=True),
        lax.all_gather(encoder_out.astype(jnp.bfloat16), "dp", axis=1, tiled=True),
        lax.all_gather(decoder_in.astype(jnp.bfloat16), "dp", axis=0, tiled=True),
        lax.all_gather(decoder_out.astype(jnp.bfloat16), "dp", axis=1, tiled=True),
        lax.all_gather(pixel_maps.astype(jnp.bfloat16), "dp", axis=0, tiled=True),
        lax.all_gather(bridge_map.astype(jnp.bfloat16), "dp", axis=0, tiled=True),
        lax.all_gather(vector_pack.astype(jnp.bfloat16), "dp", axis=1, tiled=True),
    )
    tensor_count = lax.axis_size("tensor")
    enc_in_w = copies[0].reshape(ENCODER_WIDTH, -1)
    enc_out_w = copies[1].reshape(-1, ENCODER_WIDTH)
    dec_in_w = copies[2].reshape(D_D, -1)
    dec_out_w = copies[3].reshape(-1, D_D)
    embedding_weight = copies[4][:PATCH_DIM]
    head_w = copies[4][PATCH_DIM:]
    bridge_w = copies[5]
    vectors_all = copies[6].astype(jnp.float32)
    enc_vectors = vectors_all[:, :ENCODER_WIDTH]
    dec_vectors = vectors_all[:, ENCODER_WIDTH:]
    enc_heads = H_E // tensor_count
    dec_heads = H_D // tensor_count
    patch_flags = masked.astype(jnp.float32) * image_valid.astype(jnp.float32)[:, None]
    patch_total = lax.psum(jnp.sum(patch_flags), "dp")
    image_count = images.shape[0]
    patch_ids = jnp.arange(IMAGE_PATCHES, dtype=jnp.int32)
    selection_matrix = (keep_index[:, :, None] == patch_ids[None, None, :]).astype(jnp.float32)
    retained_pixels = jnp.einsum(
        "bkp,bpc->bkc",
        selection_matrix.astype(jnp.bfloat16),
        images,
        preferred_element_type=jnp.float32,
    ).astype(jnp.bfloat16)
    kept_pos = jnp.einsum(
        "nau,uc->nac",
        selection_matrix,
        sinusoid_table(ENCODER_WIDTH, GRID_PATCHES, IMAGE_PATCHES),
        precision=highest_precision,
    )
    embedded = (
        jnp.einsum(
            "fzh,hg->fzg", retained_pixels, embedding_weight, preferred_element_type=jnp.float32
        )
        + kept_pos
    )
    enc_start = jnp.concatenate(
        [jnp.broadcast_to(enc_vectors[0], (image_count, 1, ENCODER_WIDTH)), embedded], axis=1
    )
    enc_end, enc_saved = layer_forward(
        enc_start, enc_in_w, enc_out_w, enc_vectors[1:5], enc_heads, HD_E
    )
    enc_normed, enc_unit, enc_inverse = norm_forward(enc_end, enc_vectors[5], enc_vectors[6])
    enc_low = enc_normed.astype(jnp.bfloat16)
    projected = jnp.einsum("bsd,de->bse", enc_low, bridge_w, preferred_element_type=jnp.float32)
    placer = (unshuffle[:, :, None] == jnp.arange(KEEP, dtype=jnp.int32)[None, None, :]).astype(
        jnp.float32
    )
    mask_column = masked.astype(jnp.float32)[:, :, None]
    filled = (
        jnp.einsum("bpk,bke->bpe", placer, projected[:, 1:], precision=highest_precision)
        + mask_column * dec_vectors[0]
        + sinusoid_table(D_D, GRID_PATCHES, IMAGE_PATCHES)
    )
    dec_start = jnp.concatenate([projected[:, :1], filled], axis=1)
    dec_end, dec_saved = layer_forward(
        dec_start, dec_in_w, dec_out_w, dec_vectors[1:5], dec_heads, HD_D
    )
    dec_normed, dec_unit, dec_inverse = norm_forward(dec_end, dec_vectors[5], dec_vectors[6])
    dec_low = dec_normed.astype(jnp.bfloat16)
    predicted = jnp.einsum(
        "bpe,ec->bpc", dec_low[:, 1:], head_w, preferred_element_type=jnp.float32
    )
    pixels = images.astype(jnp.float32)
    pix_centred = pixels - jnp.mean(pixels, axis=-1, keepdims=True)
    variance = jnp.sum(pix_centred * pix_centred, axis=-1, keepdims=True) / (PATCH_DIM - 1)
    target = pix_centred * lax.rsqrt(variance + eps_norm)
    errors = predicted - target
    patch_weight = patch_flags / patch_total
    loss_part = jnp.sum(jnp.mean(errors * errors, axis=-1) * patch_weight)
    grad_pred = (errors * (2.0 / PATCH_DIM) * patch_weight[:, :, None]).astype(jnp.bfloat16)
    grad_head = jnp.einsum(
        "bpe,bpc->ec", dec_low[:, 1:], grad_pred, preferred_element_type=jnp.float32
    )
    grad_dec_rows = jnp.einsum("bpc,ec->bpe", grad_pred, head_w, preferred_element_type=jnp.float32)
    grad_dec_norm = jnp.concatenate(
        [jnp.zeros((image_count, 1, D_D), jnp.float32), grad_dec_rows], axis=1
    )
    grad_dec_end, dec_gain, dec_shift = norm_backward(
        grad_dec_norm, dec_unit, dec_inverse, dec_vectors[5]
    )
    dec_state = layer_forward(dec_start, dec_in_w, dec_out_w, dec_vectors[1:5], dec_heads, HD_D)[1]
    grad_dec_start, grad_dec_in, grad_dec_out, grad_dec_vectors = layer_backward(
        grad_dec_end, dec_state, dec_in_w, dec_out_w, dec_vectors[1:5], dec_heads, HD_D
    )
    grad_mask = jnp.sum(grad_dec_start[:, 1:] * mask_column, axis=(0, 1))
    grad_rest = jnp.einsum(
        "bpk,bpe->bke", placer, grad_dec_start[:, 1:], precision=highest_precision
    )
    grad_projected = jnp.concatenate([grad_dec_start[:, :1], grad_rest], axis=1).astype(
        jnp.bfloat16
    )
    grad_bridge = jnp.einsum(
        "bsd,bse->de", enc_low, grad_projected, preferred_element_type=jnp.float32
    )
    grad_enc_norm = jnp.einsum(
        "bse,de->bsd", grad_projected, bridge_w, preferred_element_type=jnp.float32
    )
    grad_enc_end, enc_gain, enc_shift = norm_backward(
        grad_enc_norm, enc_unit, enc_inverse, enc_vectors[5]
    )
    enc_state = layer_forward(enc_start, enc_in_w, enc_out_w, enc_vectors[1:5], enc_heads, HD_E)[1]
    grad_enc_start, grad_enc_in, grad_enc_out, grad_enc_vectors = layer_backward(
        grad_enc_end, enc_state, enc_in_w, enc_out_w, enc_vectors[1:5], enc_heads, HD_E
    )
    grad_class = jnp.sum(grad_enc_start[:, 0], axis=0)
    grad_embed = jnp.einsum(
        "wmx,wmg->xg",
        retained_pixels,
        grad_enc_start[:, 1:].astype(jnp.bfloat16),
        preferred_element_type=jnp.float32,
    )
    grad_vectors = jnp.concatenate(
        [
            jnp.concatenate(
                [grad_class[None], grad_enc_vectors, enc_gain[None], enc_shift[None]], axis=0
            ),
            jnp.concatenate(
                [grad_mask[None], grad_dec_vectors, dec_gain[None], dec_shift[None]], axis=0
            ),
        ],
        axis=1,
    )
    grad_one = grad_enc_in.reshape(ENCODER_WIDTH, 1, -1)
    grad_two = grad_enc_out.reshape(1, -1, ENCODER_WIDTH)
    grad_three = grad_dec_in.reshape(D_D, 1, -1)
    grad_four = grad_dec_out.reshape(1, -1, D_D)
    grad_five = jnp.concatenate([grad_embed, grad_head], axis=0)
    masters = (
        encoder_in,
        encoder_out,
        decoder_in,
        decoder_out,
        pixel_maps,
        bridge_map,
        vector_pack,
    )
    reduced = (
        lax.psum_scatter(grad_one, "dp", scatter_dimension=0, tiled=True),
        lax.psum_scatter(grad_two, "dp", scatter_dimension=1, tiled=True),
        lax.psum_scatter(grad_three, "dp", scatter_dimension=0, tiled=True),
        lax.psum_scatter(grad_four, "dp", scatter_dimension=1, tiled=True),
        lax.psum_scatter(grad_five, "dp", scatter_dimension=0, tiled=True),
        lax.psum_scatter(grad_bridge, "dp", scatter_dimension=0, tiled=True),
        lax.psum_scatter(grad_vectors, "dp", scatter_dimension=1, tiled=True),
    )
    firsts = (
        first_encoder_in,
        first_encoder_out,
        first_decoder_in,
        first_decoder_out,
        first_pixel_maps,
        first_bridge_map,
        first_vector_pack,
    )
    seconds = (
        second_encoder_in,
        second_encoder_out,
        second_decoder_in,
        second_decoder_out,
        second_pixel_maps,
        second_bridge_map,
        second_vector_pack,
    )
    decays = (decay_matrix,) * 6 + (0.0,)
    share_counts = (
        1.0,
        1.0,
        1.0,
        1.0,
        float(tensor_count),
        float(tensor_count),
        float(tensor_count),
    )
    bias_one = 1.0 - beta_one**step_count
    bias_two = 1.0 - beta_two**step_count
    new_firsts, new_seconds, updates = ([], [], [])
    for gradient, master, moment_one, moment_two, decay_value in zip(
        reduced, masters, firsts, seconds, decays
    ):
        next_one = beta_one * moment_one + (1.0 - beta_one) * gradient
        next_two = beta_two * moment_two + (1.0 - beta_two) * gradient * gradient
        new_firsts.append(next_one)
        new_seconds.append(next_two)
        updates.append(
            next_one / bias_one / (jnp.sqrt(next_two / bias_two) + eps_moment)
            + decay_value * master
        )
    weight_sq = jnp.stack(
        [
            jnp.sum(master * master) / share_value
            for master, share_value in zip(masters, share_counts)
        ]
    )
    update_sq = jnp.stack(
        [
            jnp.sum(update * update) / share_value
            for update, share_value in zip(updates, share_counts)
        ]
    )
    totals = lax.psum((weight_sq, update_sq, loss_part / tensor_count), ("dp", "tensor"))
    weight_norm = jnp.sqrt(totals[0])
    update_norm = jnp.sqrt(totals[1])
    step_ratio = learn_rate * weight_norm / update_norm
    news = [
        master - step_ratio[position] * update
        for position, (master, update) in enumerate(zip(masters, updates))
    ]
    return tuple(
        [totals[2], jnp.stack([weight_norm, update_norm])] + new_firsts + new_seconds + news
    )


def solution(mesh):
    in_specs = (
        P("dp", None, None),
        P("dp", None),
        P("dp", None),
        P("dp", None),
        P("dp"),
        P("dp", "tensor", None),
        P("tensor", "dp", None),
        P("dp", "tensor", None),
        P("tensor", "dp", None),
        P("dp", None),
        P("dp", None),
        P(None, "dp"),
        P("dp", "tensor", None),
        P("tensor", "dp", None),
        P("dp", "tensor", None),
        P("tensor", "dp", None),
        P("dp", None),
        P("dp", None),
        P(None, "dp"),
        P("dp", "tensor", None),
        P("tensor", "dp", None),
        P("dp", "tensor", None),
        P("tensor", "dp", None),
        P("dp", None),
        P("dp", None),
        P(None, "dp"),
    )
    out_specs = (
        P(),
        P(),
        P("dp", "tensor", None),
        P("tensor", "dp", None),
        P("dp", "tensor", None),
        P("tensor", "dp", None),
        P("dp", None),
        P("dp", None),
        P(None, "dp"),
        P("dp", "tensor", None),
        P("tensor", "dp", None),
        P("dp", "tensor", None),
        P("tensor", "dp", None),
        P("dp", None),
        P("dp", None),
        P(None, "dp"),
        P("dp", "tensor", None),
        P("tensor", "dp", None),
        P("dp", "tensor", None),
        P("tensor", "dp", None),
        P("dp", None),
        P("dp", None),
        P(None, "dp"),
    )
    return jax.shard_map(shards, mesh=mesh, in_specs=in_specs, out_specs=out_specs, check_vma=False)
```

profile of v0, /device:TPU:0, one launch (start us, length us, event | category | flops | bytes accessed | tf_op | source)
XLA Modules:
  0.0 1510.2 jit_solution(6791526144642053541)
XLA Ops:
  13.0 32.6 %all-gather = bf16[8,160,7]{1,2,0:T(8,128)(2,1)S(1)} all-gather(bf16[1,160,7]{1,2,0:T(8,128)(2,1)S(1)} %convert_bitcast_fusion), channel_id=1, replica_groups=mesh['dp'=8,'tensor'=4] {'dp'}, dimensions={0}, use_global_device_ids=true | all-gather | bytes 20160 | tf_op jit(solution)/shard_map/all_gather | solution.py:255
  66.6 46.4 %all-gather.7.cloned.1.call-done = bf16[768,1,1344]{2,0,1:T(8,128)(2,1)} async-done(((bf16[96,1,1344]{2,0,1:T(8,128)(2,1)}), bf16[768,1,1344]{2,0,1:T(8,128)(2,1)}) %all-gather.7.cloned.1.call-update) | async-done | bytes 2064400 | tf_op jit(solution)/shard_map/all_gather | solution.py:249
  139.2 18.8 %all-gather.9.cloned.1.call-done = bf16[1,960,768]{2,1,0:T(8,128)(2,1)} async-done(((bf16[1,120,768]{2,1,0:T(8,128)(2,1)}), bf16[1,960,768]{2,1,0:T(8,128)(2,1)}) %all-gather.9.cloned.1.call-update) | async-done | bytes 1474576 | tf_op jit(solution)/shard_map/all_gather | solution.py:250
  160.6 34.1 %all_gather.27 = bf16[1,640,512]{2,1,0:T(8,128)(2,1)} all-gather(bf16[1,80,512]{2,1,0:T(8,128)(2,1)} %convert_element_type.271), channel_id=1, replica_groups=mesh['dp'=8,'tensor'=4] {'dp'}, dimensions={1}, use_global_device_ids=true | all-gather | bytes 737280 | tf_op jit(solution)/shard_map/all_gather | solution.py:252
  194.7 34.1 %all_gather.25 = bf16[768,512]{1,0:T(8,128)(2,1)} all-gather(bf16[96,512]{1,0:T(8,128)(2,1)S(1)} %copy-done.76), channel_id=1, replica_groups=mesh['dp'=8,'tensor'=4] {'dp'}, dimensions={0}, use_global_device_ids=true | all-gather | bytes 884736 | tf_op jit(solution)/shard_map/all_gather | solution.py:254
  246.3 34.6 %all_gather.26 = bf16[512,1,896]{2,0,1:T(8,128)(2,1)} all-gather(bf16[64,1,896]{2,0,1:T(8,128)(2,1)S(1)} %copy.318), channel_id=1, replica_groups=mesh['dp'=8,'tensor'=4] {'dp'}, dimensions={0}, use_global_device_ids=true | all-gather | bytes 1032192 | tf_op jit(solution)/shard_map/all_gather | solution.py:251
  303.7 7.7 fusion.183
  323.7 22.4 %psum.94 = f32[]{:T(128)} all-reduce(f32[]{:T(128)} %multiply_reduce_fusion.30), channel_id=1, replica_groups=mesh['dp'=8,'tensor'=4] {'dp'}, use_global_device_ids=true, to_apply=%region_24.25 | all-reduce | flops 1 | bytes 8 | tf_op jit(solution)/shard_map/psum | solution.py:271
  346.0 47.1 %all-reduce.19.cloned.1.call-done = bf16[16,197,512]{2,1,0:T(8,128)(2,1)} async-done(((bf16[16,197,512]{2,1,0:T(8,128)(2,1)}), bf16[16,197,512]{2,1,0:T(8,128)(2,1)}) %all-reduce.19.cloned.1.call-update) | async-done | bytes 3227664 | tf_op jit(solution)/shard_map/psum | solution.py:63
  405.2 15.4 %multiply_convert_fusion.2 = (bf16[16,197,512]{2,1,0:T(8,128)(2,1)S(1)}, f32[16,197,512]{2,1,0:T(8,128)}) fusion(f32[16,197,512]{2,1,0:T(8,128)S(1)} %get-tuple-element.209, u16[197,512]{1,0:T(8,128)(2,1)S(1)} %get-tuple-element.101, u16[197,512]{1,0:T(8,128)(2,1)S(1)} %get-tuple-element.100), kind=kLoop, calls=%fused_computation.55 | loop fusion | flops 112967680 | bytes 16541696 | tf_op jit(solution)/shard_map/convert_element_type | solution.py:102
  437.2 59.6 %all-reduce.21.cloned.1.call-done = bf16[16,197,512]{2,1,0:T(8,128)(2,1)} async-done(((bf16[16,197,512]{2,1,0:T(8,128)(2,1)}), bf16[16,197,512]{2,1,0:T(8,128)(2,1)}) %all-reduce.21.cloned.1.call-update) | async-done | bytes 3227664 | tf_op jit(solution)/shard_map/psum | solution.py:63
  507.9 7.6 multiply_convert_fusion.1
  539.8 70.8 %all-reduce.23.cloned.1.call-done = bf16[16,197,512]{2,1,0:T(8,128)(2,1)} async-done(((bf16[16,197,512]{2,1,0:T(8,128)(2,1)}), bf16[16,197,512]{2,1,0:T(8,128)(2,1)}) %all-reduce.23.cloned.1.call-update) | async-done | bytes 3227664 | tf_op jit(solution)/shard_map/psum | solution.py:67
  661.6 70.8 %all-reduce.25.cloned.1.call-done = bf16[16,197,512]{2,1,0:T(8,128)(2,1)} async-done(((bf16[16,197,512]{2,1,0:T(8,128)(2,1)}), bf16[16,197,512]{2,1,0:T(8,128)(2,1)}) %all-reduce.25.cloned.1.call-update) | async-done | bytes 3227664 | tf_op jit(solution)/shard_map/psum | solution.py:67
  739.1 7.5 fusion.17
  762.1 40.1 %all-reduce.27.cloned.1.call-done = bf16[16,50,768]{2,1,0:T(8,128)(2,1)} async-done(((bf16[16,50,768]{2,1,0:T(8,128)(2,1)}), bf16[16,50,768]{2,1,0:T(8,128)(2,1)}) %all-reduce.27.cloned.1.call-update) | async-done | bytes 1228816 | tf_op jit(solution)/shard_map/psum | solution.py:67
  837.6 26.3 %all-reduce.29.cloned.1.call-done = bf16[16,50,768]{2,1,0:T(8,128)(2,1)} async-done(((bf16[16,50,768]{2,1,0:T(8,128)(2,1)}), bf16[16,50,768]{2,1,0:T(8,128)(2,1)}) %all-reduce.29.cloned.1.call-update) | async-done | bytes 1228816 | tf_op jit(solution)/shard_map/psum | solution.py:67
  910.1 12.2 copy.210
  943.1 52.8 %reduce-scatter.16.cloned.1.call-done = f32[160,7]{1,0:T(8,128)} async-done(((f32[1280,7]{1,0:T(8,128)}), f32[160,7]{1,0:T(8,128)}) %reduce-scatter.16.cloned.1.call-update) | async-done | bytes 4496
  998.9 64.7 %reduce-scatter.14.cloned.1.call-done = f32[96,512]{1,0:T(8,128)} async-done(((f32[768,512]{1,0:T(8,128)}), f32[96,512]{1,0:T(8,128)}) %reduce-scatter.14.cloned.1.call-update) | async-done | bytes 196624 | tf_op jit(solution)/shard_map/reduce_scatter | solution.py:400
  1067.3 71.0 %reduce-scatter.8.cloned.1.call-done = f32[1,120,768]{2,1,0:T(8,128)} async-done(((f32[1,960,768]{2,1,0:T(8,128)}), f32[1,120,768]{2,1,0:T(8,128)}) %reduce-scatter.8.cloned.1.call-update) | async-done | bytes 368656 | tf_op jit(solution)/shard_map/reduce_scatter | solution.py:396
  1141.0 210.0 %all-reduce.31.cloned.1.call-done = (f32[768,1,1344]{2,1,0:T(1,128)}, f32[512,1,896]{2,1,0:T(1,128)}) async-done(((f32[768,1,1344]{2,1,0:T(1,128)}, f32[512,1,896]{2,1,0:T(1,128)}), (f32[768,1,1344]{2,1,0:T(1,128)}, f32[512,1,896]{2,1,0:T(1,128)})) %all-reduce.31.cloned.1.call-update) | async-done | bytes 5963792
  1360.2 77.4 %reduce-scatter.12.cloned.1.call-done = f32[160,768]{1,0:T(8,128)} async-done(((f32[1280,768]{1,0:T(8,128)}), f32[160,768]{1,0:T(8,128)}) %reduce-scatter.12.cloned.1.call-update) | async-done | bytes 491536 | tf_op jit(solution)/shard_map/reduce_scatter | solution.py:399
  1448.7 40.3 %all-reduce.3 = (f32[]{:T(128)}, f32[7]{0:T(128)S(1)}, f32[7]{0:T(128)S(1)}) all-reduce(f32[]{:T(128)S(6)} %div.337, f32[7]{0:T(128)S(1)} %stack.145, f32[7]{0:T(128)S(1)} %stack.120), channel_id=1, replica_groups=mesh['dp'=8,'tensor'=4] {'dp','tensor'}, use_global_device_ids=true, to_apply=%region_26.27 | all-reduce | flops 15 | bytes 120 | tf_op jit(solution)/shard_map/psum | solution.py:457
  (557 shorter events, 383.7 us)
Async XLA Ops:
  7.3 54.0 %all-gather.5.cloned.1.call-start = ((), (), s32[]{:S(2)}) async-start(), calls=%async_computation.5 | async-start | bytes 2211840 | tf_op jit(solution)/shard_map/all_gather | solution.py:253
  9.2 103.8 %all-gather.7.cloned.1.call-start = ((), (), s32[]{:S(2)}) async-start(), calls=%async_computation.6 | async-start | bytes 2433024 | tf_op jit(solution)/shard_map/all_gather | solution.py:249
  11.1 146.8 %all-gather.9.cloned.1.call-start = ((), (), s32[]{:S(2)}) async-start(), calls=%async_computation.7 | async-start | bytes 1658880 | tf_op jit(solution)/shard_map/all_gather | solution.py:250
  12.8 216.0 %all-reduce.15.cloned.1.call-start = ((), (), s32[]{:S(2)}) async-start(), calls=%async_computation.8 | async-start | bytes 2752512 | tf_op jit(solution)/shard_map/psum | solution.py:63
  13.0 276.2 %copy-start.90 = (f32[16,196]{1,0:T(8,128)}, f32[16,196]{1,0:T(8,128)S(1)}, u32[]{:S(2)}) copy-start(f32[16,196]{1,0:T(8,128)S(1)} %convert_element_type.263) | copy-start | bytes 37636
  160.5 123.8 %all-reduce.17.cloned.1.call-start = ((), (), s32[]{:S(2)}) async-start(), calls=%async_computation.9 | async-start | bytes 2752512 | tf_op jit(solution)/shard_map/psum | solution.py:63
  246.1 147.0 %all-reduce.19.cloned.1.call-start = ((), (), s32[]{:S(2)}) async-start(), calls=%async_computation.10 | async-start | bytes 6553600 | tf_op jit(solution)/shard_map/psum | solution.py:63
  246.2 278.7 %copy-start.120 = (f32[1,512]{1,0:T(1,128)}, f32[1,512]{1,0:T(1,128)S(1)}, u32[]{:S(2)}) copy-start(f32[1,512]{1,0:T(1,128)S(1)} %get-tuple-element.175) | copy-start | bytes 6148
  246.2 371.0 %copy-start.124 = (f32[1,512]{1,0:T(1,128)}, f32[1,512]{1,0:T(1,128)S(1)}, u32[]{:S(2)}) copy-start(f32[1,512]{1,0:T(1,128)S(1)} %get-tuple-element.179) | copy-start | bytes 6148
  322.4 174.4 %all-reduce.21.cloned.1.call-start = ((), (), s32[]{:S(2)}) async-start(), calls=%async_computation.11 | async-start | bytes 6553600 | tf_op jit(solution)/shard_map/psum | solution.py:63
  426.0 184.6 %all-reduce.23.cloned.1.call-start = ((), (), s32[]{:S(2)}) async-start(), calls=%async_computation.12 | async-start | bytes 6553600 | tf_op jit(solution)/shard_map/psum | solution.py:67
  539.7 192.7 %all-reduce.25.cloned.1.call-start = ((), (), s32[]{:S(2)}) async-start(), calls=%async_computation.13 | async-start | bytes 6553600 | tf_op jit(solution)/shard_map/psum | solution.py:67
  661.6 140.6 %all-reduce.27.cloned.1.call-start = ((), (), s32[]{:S(2)}) async-start(), calls=%async_computation.14 | async-start | bytes 2752512 | tf_op jit(solution)/shard_map/psum | solution.py:67
  762.1 101.8 %all-reduce.29.cloned.1.call-start = ((), (), s32[]{:S(2)}) async-start(), calls=%async_computation.17 | async-start | bytes 2752512 | tf_op jit(solution)/shard_map/psum | solution.py:67
  823.9 116.8 %reduce-scatter.10.cloned.1.call-start = ((), (), s32[]{:S(2)}) async-start(), calls=%async_computation.16 | async-start | bytes 1474560 | tf_op jit(solution)/shard_map/reduce_scatter | solution.py:398
  833.7 162.2 %reduce-scatter.16.cloned.1.call-start = ((), (), s32[]{:S(2)}) async-start(), calls=%async_computation.20 | async-start | bytes 737280
  871.0 192.5 %reduce-scatter.14.cloned.1.call-start = ((), (), s32[]{:S(2)}) async-start(), calls=%async_computation.19 | async-start | bytes 1769472 | tf_op jit(solution)/shard_map/reduce_scatter | solution.py:400
  876.1 262.2 %reduce-scatter.8.cloned.1.call-start = ((), (), s32[]{:S(2)}) async-start(), calls=%async_computation.15 | async-start | bytes 3317760 | tf_op jit(solution)/shard_map/reduce_scatter | solution.py:396
  882.3 468.7 %all-reduce.31.cloned.1.call-start = ((), (), s32[]{:S(2)}) async-start(), calls=%async_computation.21 | async-start | bytes 12320768
  922.3 515.3 %reduce-scatter.12.cloned.1.call-start = ((), (), s32[]{:S(2)}) async-start(), calls=%async_computation.18 | async-start | bytes 4423680 | tf_op jit(solution)/shard_map/reduce_scatter | solution.py:399
  936.9 415.2 %copy-start.85 = (f32[64,1,896]{2,1,0:T(1,128)S(1)}, f32[64,1,896]{2,1,0:T(1,128)}, u32[]{:S(2)}) copy-start(f32[64,1,896]{2,1,0:T(1,128)} %param.40) | copy-start | bytes 688132
  936.9 415.2 %copy-start.86 = (f32[64,1,896]{2,1,0:T(1,128)S(1)}, f32[64,1,896]{2,1,0:T(1,128)}, u32[]{:S(2)}) copy-start(f32[64,1,896]{2,1,0:T(1,128)} %param.47) | copy-start | bytes 688132
  997.5 497.4 %copy-start.118 = (f32[7,160]{1,0:T(8,128)}, f32[7,160]{1,0:T(8,128)S(1)}, u32[]{:S(2)}) copy-start(f32[7,160]{1,0:T(8,128)S(1)} %get-tuple-element.142) | copy-start | bytes 13444
  997.5 497.4 %copy-start.119 = (f32[7,160]{1,0:T(8,128)}, f32[7,160]{1,0:T(8,128)S(1)}, u32[]{:S(2)}) copy-start(f32[7,160]{1,0:T(8,128)S(1)} %get-tuple-element.143) | copy-start | bytes 13444
  (156 other events, 3903.3 us)
Sparse Core Ops, SparseCore 0:
  10.9 50.3 all-gather.4
  64.0 49.0 all-gather.6
  115.8 42.0 all-gather.8
  160.6 38.1 all-reduce.14
  246.2 38.0 all-reduce.16
  322.5 70.6 all-reduce.18
  426.1 70.6 all-reduce.20
  539.9 70.6 all-reduce.22
  661.7 70.6 all-reduce.24
  762.2 39.9 all-reduce.26
  824.0 39.8 all-reduce.28
  867.2 64.3 reduce-scatter.9
  934.8 61.0 reduce-scatter.15
  999.6 63.8 reduce-scatter.13
  1066.9 71.2 reduce-scatter.7
  1142.9 208.1 all-reduce.30
  1354.5 82.9 reduce-scatter.11
where the time goes:
time: 1520 us; the launch traced here: 1510 us
  waiting for transfers between devices  864 us (57%)
  blocking collectives  198 us (13%)
  matrix products  170 us (11%)
  other arithmetic  161 us (11%)
  local copies, waits for them, and re-layouts  94.5 us (6%)
  between operations  22.3 us (1%)
    unnamed x19, waiting for transfers between devices  263 us
    psum x4, waiting for transfers between devices, input_sum(): lax.psum(partial_grad.astype(jnp.bfloat16), 'tensor').astype(jnp.float32)  208 us
    psum x4, waiting for transfers between devices, tensor_sum(): lax.psum(partial_out.astype(jnp.bfloat16), 'tensor').astype(jnp.float32)  110 us
    reduce_scatter x1, waiting for transfers between devices, shards(): lax.psum_scatter(grad_five, 'dp', scatter_dimension=0, tiled=True)  77.4 us
    reduce_scatter x1, waiting for transfers between devices, shards(): lax.psum_scatter(grad_two, 'dp', scatter_dimension=1, tiled=True)  71 us
    reduce_scatter x1, waiting for transfers between devices, shards(): lax.psum_scatter(grad_bridge, 'dp', scatter_dimension=0, tiled=True)  64.7 us
    all_gather x1, waiting for transfers between devices, shards(): lax.all_gather(encoder_in.astype(jnp.bfloat16), 'dp', axis=0, tiled=True)  46.4 us
    unnamed x339, local copies, waits for them, and re-layouts  44.2 us
  transfers between devices with their start and end apart: 17, of which 15 were waited for; matrix products, arithmetic and copies ran while one was open for 11% of the time, Pallas kernels for 0%

commit v1 on v0

v1 whole, which is shorter than its diff:
```python
import functools

import jax
import jax.numpy as jnp
from jax import lax
from jax.experimental import pallas as pl
from jax.experimental.pallas import tpu as pltpu
from jax.sharding import PartitionSpec as P

ENCODER_WIDTH = 768
H_E = 12
HD_E = 64
D_D = 512
H_D = 16
HD_D = 32
PATCH_DIM = 768
GRID_PATCHES = 14
IMAGE_PATCHES = 196
KEEP = 49

eps_norm = 1e-06
beta_one = 0.9
beta_two = 0.999
step_count = 7.0
learn_rate = 0.3
decay_matrix = 0.05
eps_moment = 1e-06
highest_precision = lax.Precision.HIGHEST
f32 = jnp.float32
bf16 = jnp.bfloat16
EVERY = ("dp", "tensor")
GROUPED = ("tensor", "dp")


MESH_ID = pl.DeviceIdType.MESH
PIX, EIN, EOUT, BRI, DIN, DOUT, VEC = range(7)


def place():
    dp_at = lax.axis_index("dp")
    group = lax.axis_index("tensor")
    z, x = lax.div(dp_at, 2), lax.rem(dp_at, 2)
    y, c = lax.div(group, 2), lax.rem(group, 2)
    return z, x, y, c


def device(z, x, y, c):
    return (z * 2 + x, y * 2 + c)


def flip(z, m):
    low = lax.rem(z, 2)
    high = lax.div(z, 2)
    if m % 2:
        low = 1 - low
    if m // 2:
        high = 1 - high
    return high * 2 + low


def greet(z, x, y, c):
    barrier = pltpu.get_barrier_semaphore()
    peers = [
        device(z, x, y, 1 - c),
        device(z, x, 1 - y, c),
        device(z, 1 - x, y, c),
        device(flip(z, 1), x, y, c),
        device(flip(z, 2), x, y, c),
        device(flip(z, 3), x, y, c),
    ]
    for peer in peers:
        pl.semaphore_signal(barrier, inc=1, device_id=peer, device_id_type=MESH_ID)
    pl.semaphore_wait(barrier, 6)


SHARED = (PIX, BRI)


def spot(array, y, c, z, x):
    return (z, x, y, c) if array in SHARED else (y, c, z, x)


def half_spot(array, y, z, x):
    return (z, x, y) if array in SHARED else (y, z, x)


def whole_shape(array, part):
    return ((4, 2, 2, 2) if array in SHARED else (2, 2, 4, 2)) + part


GATHER_STEPS = (
    ((VEC, 0, 8, 0), (PIX, 0, 24, 0), (PIX, 24, 16, 1)),
    ((EIN, 0, 32, 0), (EIN, 32, 16, 1)),
    ((EIN, 48, 16, 0), (EIN, 64, 32, 1)),
    ((EOUT, 0, 32, 0), (EOUT, 32, 32, 1)),
    ((EOUT, 64, 32, 0), (EOUT, 96, 24, 1)),
    ((BRI, 0, 8, 0), (BRI, 8, 16, 1), (DIN, 0, 32, 0), (DIN, 32, 32, 1)),
    ((DOUT, 0, 48, 0), (DOUT, 48, 32, 1)),
)


def gather_kernel(*refs):
    count = 7
    parts = refs[:count]
    outs = refs[count : 2 * count]
    send, recv, local = refs[2 * count :]
    z, x, y, c = place()
    units = []
    for at, step in enumerate(GATHER_STEPS):
        for unit in step:
            units.append((at,) + unit)
    copies = {}

    def rows(array, region, first, size):
        ref = outs[array]
        return ref.at[region + (pl.ds(first, size),)]

    def plan(number, stage):
        at, array, first, size, turn = units[number]
        every = slice(None)
        if stage < 3:
            src = parts[array].at[pl.ds(first, size)]
            dst = rows(array, spot(array, y, c, z, x), first, size)
            peer = device(flip(z, stage + 1), x, y, c)
        else:
            if stage == 3:
                region = spot(array, y, c, every, x)
                peer = device(z, x, 1 - y, c) if turn == 0 else device(z, 1 - x, y, c)
            elif stage == 4 and turn == 0:
                region = spot(array, every, c, every, x)
                peer = device(z, 1 - x, y, c)
            elif stage == 4:
                region = spot(array, y, c, every, every)
                peer = device(z, x, 1 - y, c)
            else:
                region = spot(array, every, c, every, every)
                peer = device(z, x, y, 1 - c)
            src = dst = rows(array, region, first, size)
        return pltpu.make_async_remote_copy(
            src_ref=src,
            dst_ref=dst,
            send_sem=send.at[number, stage],
            recv_sem=recv.at[number, stage],
            device_id=peer,
            device_id_type=MESH_ID,
        )

    def start(number, stage):
        copies[number, stage] = plan(number, stage)
        copies[number, stage].start()

    own = []
    for array in range(count):
        own.append(
            pltpu.make_async_copy(parts[array], outs[array].at[spot(array, y, c, z, x)], local.at[array])
        )
        own[-1].start()
    greet(z, x, y, c)
    steps = len(GATHER_STEPS)
    waited = set()
    for tick in range(steps + 4):
        for number, unit in enumerate(units):
            if unit[0] == tick:
                for stage in range(3):
                    start(number, stage)
        for number, unit in enumerate(units):
            if unit[0] == tick - 1:
                if unit[1] not in waited:
                    waited.add(unit[1])
                    own[unit[1]].wait()
                for stage in range(3):
                    copies[number, stage].wait_recv()
                start(number, 3)
        for back in (2, 3):
            for number, unit in enumerate(units):
                if unit[0] == tick - back:
                    copies[number, back + 1].wait_recv()
                    start(number, back + 2)
        for number, unit in enumerate(units):
            if unit[0] == tick - 4:
                copies[number, 5].wait_recv()
    for key in copies:
        copies[key].wait_send()


def gather_weights(parts):
    count = 7
    units = sum(len(step) for step in GATHER_STEPS)
    outs = [
        jax.ShapeDtypeStruct(whole_shape(array, part.shape), part.dtype)
        for array, part in enumerate(parts)
    ]
    total = sum(int(part.size) * 32 * part.dtype.itemsize for part in parts)
    return pl.pallas_call(
        gather_kernel,
        out_shape=outs,
        in_specs=[pl.BlockSpec(memory_space=pltpu.VMEM)] * count,
        out_specs=[pl.BlockSpec(memory_space=pl.ANY)] * count,
        scratch_shapes=[
            pltpu.SemaphoreType.DMA((units, 6)),
            pltpu.SemaphoreType.DMA((units, 6)),
            pltpu.SemaphoreType.DMA((count,)),
        ],
        compiler_params=pltpu.CompilerParams(collective_id=0, has_side_effects=True),
        cost_estimate=pl.CostEstimate(flops=0, bytes_accessed=2 * total, transcendentals=0),
        name="gather_weights",
    )(*parts)


SCATTER_STEPS = (
    ((DOUT, 0, 48, 0), (DOUT, 48, 32, 1)),
    ((BRI, 0, 8, 0), (BRI, 8, 16, 1), (DIN, 0, 32, 0), (DIN, 32, 32, 1)),
    ((PIX, 0, 24, 0), (PIX, 24, 16, 1)),
    ((EOUT, 0, 32, 0), (EOUT, 32, 32, 1)),
    ((EOUT, 64, 32, 0), (EOUT, 96, 24, 1)),
    ((EIN, 0, 32, 0), (EIN, 32, 16, 1)),
    ((EIN, 48, 16, 0), (EIN, 64, 32, 1)),
)
def scatter_kernel(shapes, units, *refs):
    grads = refs[:7]
    outs = refs[7:14]
    refs = refs[14:]
    n = len(units)
    own, one, two, three, four = (refs[k * n : (k + 1) * n] for k in range(5))
    vec_one, vec_two, vec_three, vec_four, vec_sum = refs[5 * n : 5 * n + 5]
    send, recv, local, vsend, vrecv, tsend, trecv = refs[5 * n + 5 :]
    z, x, y, c = place()
    every = slice(None)
    copies = {}

    def remote(src, dst, key, send_sem, recv_sem, peer):
        copies[key] = pltpu.make_async_remote_copy(
            src_ref=src,
            dst_ref=dst,
            send_sem=send_sem,
            recv_sem=recv_sem,
            device_id=peer,
            device_id_type=MESH_ID,
        )
        copies[key].start()

    def start(number, stage):
        at, array, first, size, turn = units[number]
        mine = own[number]
        if stage == 0:
            peer = device(z, x, y, 1 - c)
            src = grads[array].at[
                spot(array, every, 1 - c, every, every) + (pl.ds(first, size),)
            ]
            dst = one[number]
        elif stage == 1 and turn == 0:
            peer = device(z, 1 - x, y, c)
            src, dst = mine.at[half_spot(array, every, every, 1 - x)], two[number]
        elif stage == 1:
            peer = device(z, x, 1 - y, c)
            src, dst = mine.at[half_spot(array, 1 - y, every, every)], two[number]
        elif stage == 2 and turn == 0:
            peer = device(z, x, 1 - y, c)
            src, dst = mine.at[half_spot(array, 1 - y, every, x)], three[number]
        elif stage == 2:
            peer = device(z, 1 - x, y, c)
            src, dst = mine.at[half_spot(array, y, every, 1 - x)], three[number]
        else:
            other = flip(z, stage - 2)
            peer = device(other, x, y, c)
            src, dst = mine.at[half_spot(array, y, other, x)], four[number].at[stage - 3]
        remote(src, dst, (number, stage), send.at[number, stage], recv.at[number, stage], peer)

    def add(number, stage):
        at, array, first, size, turn = units[number]
        mine = own[number]

        def pair(here, there):
            mine[here] = (mine[here].astype(f32) + there.astype(f32)).astype(bf16)

        if stage == 0:

            @pl.loop(0, 16)
            def _(k):
                iy, iz, ix = k // 8, (k // 2) % 4, k % 2
                here = half_spot(array, iy, iz, ix)
                pair(here, one[number][here])

        elif stage == 1 and turn == 0:

            @pl.loop(0, 8)
            def _(k):
                iy, iz = k // 4, k % 4
                there = (iz, iy) if array in SHARED else (iy, iz)
                pair(half_spot(array, iy, iz, x), two[number][there])

        elif stage == 1:

            @pl.loop(0, 8)
            def _(k):
                iz, ix = k // 2, k % 2
                pair(half_spot(array, y, iz, ix), two[number][iz, ix])

        elif stage == 2:

            @pl.loop(0, 4)
            def _(k):
                pair(half_spot(array, y, k, x), three[number][k])

        else:
            total = mine[half_spot(array, y, z, x)].astype(f32)
            for slot in range(3):
                total = total + four[number][slot].astype(f32)
            if array in SHARED:
                outs[array][y * 2 + c, pl.ds(first, size)] = total
            else:
                outs[array][pl.ds(first, size)] = total

    loads = []
    for number, (at, array, first, size, turn) in enumerate(units):
        loads.append(
            pltpu.make_async_copy(
                grads[array].at[spot(array, every, c, every, every) + (pl.ds(first, size),)],
                own[number],
                local.at[number],
            )
        )
    greet(z, x, y, c)
    steps = units[-1][0] + 1

    def step_units(tick):
        return [number for number in range(n) if units[number][0] == tick]

    vec_dst = (vec_one, vec_two, vec_three)
    vec_peer = (device(z, x, y, 1 - c), device(z, 1 - x, y, c), device(z, x, 1 - y, c))

    for tick in range(steps + 4):
        for number in step_units(tick):
            loads[number].start()
            start(number, 0)
        for number in step_units(tick - 1):
            loads[number].wait()
            copies[number, 0].wait_recv()
            add(number, 0)
            start(number, 1)
        for number in step_units(tick - 2):
            copies[number, 1].wait()
            add(number, 1)
            start(number, 2)
        for number in step_units(tick - 3):
            copies[number, 2].wait()
            add(number, 2)
            for stage in (3, 4, 5):
                start(number, stage)
        for number in step_units(tick - 4):
            for stage in (3, 4, 5):
                copies[number, stage].wait()
            add(number, 3)
        if tick < 4:
            if tick == 0:
                vec_sum[...] = grads[6][...]
            if tick < 3:
                remote(vec_sum.at[...], vec_dst[tick], ("v", tick), vsend.at[tick], vrecv.at[tick], vec_peer[tick])
            else:
                vec_four[z] = vec_sum[...]
                for m in (1, 2, 3):
                    remote(vec_sum.at[...], vec_four.at[z], ("v", 2 + m), vsend.at[2 + m], vrecv.at[2 + m], device(flip(z, m), x, y, c))
        if 1 <= tick <= 3:
            pass
        if tick < 3:
            copies["v", tick].wait()
            vec_sum[...] = vec_sum[...] + vec_dst[tick][...]
        if tick == 4:
            for m in (1, 2, 3):
                copies["v", 2 + m].wait()
            outs[6][...] = ((vec_four[0] + vec_four[1]) + (vec_four[2] + vec_four[3]))
        for array in SHARED:
            last = max(units[number][0] for number in range(n) if units[number][1] == array)
            if tick == last + 4:
                here = y * 2 + c
                for k, peer in enumerate((device(z, x, y, 1 - c), device(z, x, 1 - y, c), device(z, x, 1 - y, 1 - c))):
                    slot = SHARED.index(array) * 3 + k
                    remote(outs[array].at[here], outs[array].at[here], ("t", slot), tsend.at[slot], trecv.at[slot], peer)
    for slot in range(6):
        copies["t", slot].wait()
    for number in range(n):
        copies[number, 0].wait_send()


def scatter_gradients(grads):
    units = [(at,) + unit for at, step in enumerate(SCATTER_STEPS) for unit in step]
    n = len(units)
    shapes = [grad.shape for grad in grads]
    outs = []
    for array in range(6):
        rows, columns = shapes[array][4:]
        if array in SHARED:
            outs.append(jax.ShapeDtypeStruct((4, rows, columns), f32))
        else:
            outs.append(jax.ShapeDtypeStruct((rows, columns), f32))
    outs.append(jax.ShapeDtypeStruct(grads[6].shape, f32))
    scratch = []
    for stage in range(5):
        for at, array, first, size, turn in units:
            shared = array in SHARED
            lead = ((4, 2, 2) if shared else (2, 4, 2), (4,), (3,))
            if stage < 2:
                lead = lead[0]
            elif stage == 2:
                lead = ((4, 2) if shared else (2, 4)) if turn == 0 else (4, 2)
            else:
                lead = lead[stage - 2]
            scratch.append(pltpu.VMEM(lead + (size, shapes[array][5]), bf16))
    vec = grads[6].shape
    scratch += [pltpu.VMEM(vec, f32)] * 3 + [pltpu.VMEM((4,) + vec, f32), pltpu.VMEM(vec, f32)]
    scratch += [
        pltpu.SemaphoreType.DMA((n, 6)),
        pltpu.SemaphoreType.DMA((n, 6)),
        pltpu.SemaphoreType.DMA((n,)),
        pltpu.SemaphoreType.DMA((6,)),
        pltpu.SemaphoreType.DMA((6,)),
        pltpu.SemaphoreType.DMA((6,)),
        pltpu.SemaphoreType.DMA((6,)),
    ]
    total = sum(int(grad.size) * grad.dtype.itemsize for grad in grads)
    return pl.pallas_call(
        functools.partial(scatter_kernel, shapes, units),
        out_shape=outs,
        in_specs=[pl.BlockSpec(memory_space=pl.ANY)] * 6 + [pl.BlockSpec(memory_space=pltpu.VMEM)],
        out_specs=[pl.BlockSpec(memory_space=pltpu.VMEM)] * 7,
        scratch_shapes=scratch,
        compiler_params=pltpu.CompilerParams(
            collective_id=1, has_side_effects=True, vmem_limit_bytes=60 * 1024 * 1024
        ),
        cost_estimate=pl.CostEstimate(flops=0, bytes_accessed=2 * total, transcendentals=0),
        name="scatter_gradients",
    )(*grads)


def mm(spec, left, right):
    return jnp.einsum(spec, left, right, preferred_element_type=f32)


def sinusoid_table(feature_width, grid_side, patch_count):
    position = jnp.arange(patch_count, dtype=jnp.int32)
    quarter = feature_width // 4
    omegas = 1.0 / 10000.0 ** (jnp.arange(quarter, dtype=f32) / quarter)

    def half_table(coords):
        angles = coords.astype(f32)[:, None] * omegas[None, :]
        return jnp.concatenate([jnp.sin(angles), jnp.cos(angles)], axis=1)

    return jnp.concatenate(
        [half_table(position % grid_side), half_table(position // grid_side)], axis=1
    )


def norm_forward(stream, gain_row, shift_row):
    centred = stream - jnp.mean(stream, axis=-1, keepdims=True)
    inverse = lax.rsqrt(jnp.mean(centred * centred, axis=-1, keepdims=True) + eps_norm)
    unit_values = centred * inverse
    return (unit_values * gain_row + shift_row, unit_values, inverse)


def norm_backward(incoming, unit_values, inverse, gain_row):
    scaled = incoming * gain_row
    inner_part = (
        scaled
        - jnp.mean(scaled, axis=-1, keepdims=True)
        - unit_values * jnp.mean(scaled * unit_values, axis=-1, keepdims=True)
    )
    width = incoming.shape[-1]
    gain_grad = jnp.sum((incoming * unit_values).reshape(-1, width), axis=0)
    shift_grad = jnp.sum(incoming.reshape(-1, width), axis=0)
    return (inverse * inner_part, gain_grad, shift_grad)


def layer_forward(stream, w_input, w_output, vectors, group_heads, head_dim):
    image_count, token_count, model_width = stream.shape
    groups = w_input.shape[0]
    inner = group_heads * head_dim
    normed_one, unit_one, inverse_one = norm_forward(stream, vectors[0], vectors[1])
    input_one = normed_one.astype(bf16)
    raw_heads = mm("bsd,tdc->btsc", input_one, w_input[:, :, : 3 * inner]).astype(bf16)
    triple = raw_heads.reshape(image_count, groups, token_count, 3, group_heads, head_dim)
    scores = mm("btqhd,btkhd->bthqk", triple[:, :, :, 0], triple[:, :, :, 1]) * head_dim ** (-0.5)
    shifted = jnp.exp(scores - jnp.max(scores, axis=-1, keepdims=True))
    attention = shifted / jnp.sum(shifted, axis=-1, keepdims=True)
    mixed = mm("bthqk,btkhd->btqhd", attention.astype(bf16), triple[:, :, :, 2])
    mixed_low = mixed.reshape(image_count, groups, token_count, inner).astype(bf16)
    after_attn = stream + mm("btsc,tcd->bsd", mixed_low, w_output[:, :inner])
    normed_two, unit_two, inverse_two = norm_forward(after_attn, vectors[2], vectors[3])
    input_two = normed_two.astype(bf16)
    hidden = mm("bsd,tdc->btsc", input_two, w_input[:, :, 3 * inner :])
    active = jax.nn.gelu(hidden, approximate=False).astype(bf16)
    result = after_attn + mm("btsc,tcd->bsd", active, w_output[:, inner:])
    saved_state = (
        unit_one,
        inverse_one,
        input_one,
        triple,
        attention,
        mixed_low,
        unit_two,
        inverse_two,
        input_two,
        hidden,
        active,
    )
    return (result, saved_state)


def layer_backward(stream_grad, saved_state, w_input, w_output, vectors, group_heads, head_dim):
    (
        unit_one,
        inverse_one,
        input_one,
        triple,
        attention,
        mixed_low,
        unit_two,
        inverse_two,
        input_two,
        hidden,
        active,
    ) = saved_state
    image_count, token_count, model_width = stream_grad.shape
    groups = w_input.shape[0]
    inner = group_heads * head_dim
    score_scale = head_dim ** (-0.5)
    grad_low = stream_grad.astype(bf16)
    grad_down = mm("btsc,bsd->tcd", active, grad_low)
    grad_active = mm("bsd,tcd->btsc", grad_low, w_output[:, inner:])
    gelu_back = jax.vjp(lambda values: jax.nn.gelu(values, approximate=False), hidden)[1]
    grad_hidden = gelu_back(grad_active)[0].astype(bf16)
    grad_up = mm("bsd,btsc->tdc", input_two, grad_hidden)
    grad_two = mm("btsc,tdc->bsd", grad_hidden, w_input[:, :, 3 * inner :])
    grad_mid, gain_two, shift_two = norm_backward(grad_two, unit_two, inverse_two, vectors[2])
    grad_mid = grad_mid + stream_grad
    mid_low = grad_mid.astype(bf16)
    grad_attn_rows = mm("btsc,bsd->tcd", mixed_low, mid_low)
    grad_mixed = mm("bsd,tcd->btsc", mid_low, w_output[:, :inner]).astype(bf16)
    grad_mixed = grad_mixed.reshape(image_count, groups, token_count, group_heads, head_dim)
    grad_values = mm("bthqk,btqhd->btkhd", attention.astype(bf16), grad_mixed)
    grad_attention = mm("btqhd,btkhd->bthqk", grad_mixed, triple[:, :, :, 2])
    grad_scores = attention * (
        grad_attention - jnp.sum(attention * grad_attention, axis=-1, keepdims=True)
    )
    scores_low = grad_scores.astype(bf16)
    grad_queries = mm("bthqk,btkhd->btqhd", scores_low, triple[:, :, :, 1]) * score_scale
    grad_keys = mm("bthqk,btqhd->btkhd", scores_low, triple[:, :, :, 0]) * score_scale
    grad_raw = (
        jnp.stack([grad_queries, grad_keys, grad_values], axis=3)
        .reshape(image_count, groups, token_count, 3 * inner)
        .astype(bf16)
    )
    grad_triple = mm("bsd,btsc->tdc", input_one, grad_raw)
    grad_one = mm("btsc,tdc->bsd", grad_raw, w_input[:, :, : 3 * inner])
    grad_stream, gain_one, shift_one = norm_backward(grad_one, unit_one, inverse_one, vectors[0])
    grad_in_cols = jnp.concatenate([grad_triple, grad_up], axis=2)
    grad_out_rows = jnp.concatenate([grad_attn_rows, grad_down], axis=1)
    return (
        grad_stream + grad_mid,
        grad_in_cols,
        grad_out_rows,
        jnp.stack([gain_one, shift_one, gain_two, shift_two]),
    )


def gather_grouped(part, groups):
    whole = lax.all_gather(part, GROUPED, axis=0, tiled=True)
    return whole.reshape(groups, -1, whole.shape[-1])


def scatter_grouped(gradient):
    flat = gradient.reshape(-1, gradient.shape[-1])
    return lax.psum_scatter(flat, GROUPED, scatter_dimension=0, tiled=True)


def ringed(tensor_count):
    return tensor_count == 4 and lax.axis_size("dp") == 8


def gather_all(masters, counted):
    tensor_count = lax.axis_size("tensor")
    columns = masters[6].shape[1]
    flat = [
        master.reshape(-1, master.shape[-1]).astype(bf16) for master in masters[:4]
    ]
    vectors_low = masters[6].astype(bf16).astype(f32)
    if ringed(tensor_count):
        at = lax.axis_index("tensor")
        quarters = [
            lax.dynamic_slice_in_dim(
                master, at * (master.shape[0] // tensor_count), master.shape[0] // tensor_count
            ).astype(bf16)
            for master in masters[4:6]
        ]
        lanes = 256
        vec_part = jnp.concatenate(
            [
                jnp.pad(vectors_low, ((0, 0), (0, lanes - columns))),
                jnp.broadcast_to(counted, (1, lanes)),
            ],
            axis=0,
        )
        wholes = gather_weights([quarters[0], flat[0], flat[1], quarters[1], flat[2], flat[3], vec_part])
        grouped = [
            wholes[k].reshape(tensor_count, -1, wholes[k].shape[-1]) for k in (EIN, EOUT, DIN, DOUT)
        ]
        pixel_w = wholes[PIX].reshape(-1, wholes[PIX].shape[-1])
        bridge_w = wholes[BRI].reshape(-1, wholes[BRI].shape[-1])
        vec_parts = wholes[VEC][0, 0].reshape(8, 8, lanes)
        vectors_all = vec_parts[:, :7, :columns].transpose(1, 0, 2).reshape(7, -1)
        patch_total = jnp.sum(vec_parts[:, 7, 0])
        return grouped, pixel_w, bridge_w, vectors_all, patch_total
    grouped = [gather_grouped(part, tensor_count) for part in flat]
    pixel_w = lax.all_gather(masters[4].astype(bf16), "dp", axis=0, tiled=True)
    bridge_w = lax.all_gather(masters[5].astype(bf16), "dp", axis=0, tiled=True)
    vectors_all = lax.all_gather(vectors_low, "dp", axis=1, tiled=True)
    return grouped, pixel_w, bridge_w, vectors_all, lax.psum(counted, "dp")


def reduce_all(gradients, loss_part, masters):
    tensor_count = lax.axis_size("tensor")
    columns = masters[6].shape[1]
    dp_at = lax.axis_index("dp")
    grouped, grad_pixel, grad_bridge, grad_vectors = gradients
    packed = jnp.concatenate(
        [grad_vectors, jnp.broadcast_to(loss_part, (1, grad_vectors.shape[1]))], axis=0
    )
    if ringed(tensor_count):
        shapes = {
            EIN: masters[0].reshape(-1, masters[0].shape[-1]).shape,
            EOUT: masters[1].reshape(-1, masters[1].shape[-1]).shape,
            DIN: masters[2].reshape(-1, masters[2].shape[-1]).shape,
            DOUT: masters[3].reshape(-1, masters[3].shape[-1]).shape,
            PIX: (masters[4].shape[0] // tensor_count, masters[4].shape[1]),
            BRI: (masters[5].shape[0] // tensor_count, masters[5].shape[1]),
        }
        sources = {PIX: grad_pixel, EIN: grouped[0], EOUT: grouped[1], BRI: grad_bridge, DIN: grouped[2], DOUT: grouped[3]}
        operands = [
            sources[array].astype(bf16).reshape(whole_shape(array, shapes[array]))
            for array in range(6)
        ]
        sums = scatter_gradients(operands + [packed])
        reduced = [sums[EIN], sums[EOUT], sums[DIN], sums[DOUT], sums[PIX], sums[BRI]]
        vector_sum = sums[VEC]
    else:

        def scatter_shared(gradient):
            part = lax.psum_scatter(gradient, EVERY, scatter_dimension=0, tiled=True)
            return lax.all_gather(part, "tensor", axis=0, tiled=True)

        reduced = [scatter_grouped(gradient) for gradient in grouped]
        reduced += [scatter_shared(grad_pixel), scatter_shared(grad_bridge)]
        vector_sum = lax.psum(packed, EVERY)
    own = lax.dynamic_slice_in_dim(vector_sum[:7], dp_at * columns, columns, axis=1)
    reduced = [gradient.reshape(master.shape) for gradient, master in zip(reduced + [own], masters)]
    return reduced, vector_sum[7, 0]


def shards(
    images,
    keep_index,
    unshuffle,
    masked,
    image_valid,
    *state,
):
    masters, firsts, seconds = state[:7], state[7:14], state[14:21]
    encoder_in, encoder_out, decoder_in, decoder_out, pixel_maps, bridge_map, vector_pack = masters
    tensor_count = lax.axis_size("tensor")
    tensor_at = lax.axis_index("tensor")
    counted = jnp.sum(masked.astype(f32) * image_valid.astype(f32)[:, None])
    grouped_w, pixel_w, bridge_w, vectors_all, patch_total = gather_all(masters, counted)
    enc_in_w, enc_out_w, dec_in_w, dec_out_w = grouped_w
    embedding_weight = pixel_w[:PATCH_DIM]
    head_w = pixel_w[PATCH_DIM:]
    enc_vectors = vectors_all[:, :ENCODER_WIDTH]
    dec_vectors = vectors_all[:, ENCODER_WIDTH:]
    enc_heads = H_E // tensor_count
    dec_heads = H_D // tensor_count
    image_count = images.shape[0] // tensor_count

    def own(member):
        return lax.dynamic_slice_in_dim(member, tensor_at * image_count, image_count, axis=0)

    images, keep_index, unshuffle, masked, image_valid = map(
        own, (images, keep_index, unshuffle, masked, image_valid)
    )
    patch_flags = masked.astype(f32) * image_valid.astype(f32)[:, None]
    patch_ids = jnp.arange(IMAGE_PATCHES, dtype=jnp.int32)
    selection_matrix = (keep_index[:, :, None] == patch_ids[None, None, :]).astype(f32)
    retained_pixels = mm("bkp,bpc->bkc", selection_matrix.astype(bf16), images).astype(bf16)
    kept_pos = jnp.einsum(
        "nau,uc->nac",
        selection_matrix,
        sinusoid_table(ENCODER_WIDTH, GRID_PATCHES, IMAGE_PATCHES),
        precision=highest_precision,
    )
    embedded = mm("fzh,hg->fzg", retained_pixels, embedding_weight) + kept_pos
    enc_start = jnp.concatenate(
        [jnp.broadcast_to(enc_vectors[0], (image_count, 1, ENCODER_WIDTH)), embedded], axis=1
    )
    enc_end, enc_saved = layer_forward(
        enc_start, enc_in_w, enc_out_w, enc_vectors[1:5], enc_heads, HD_E
    )
    enc_normed, enc_unit, enc_inverse = norm_forward(enc_end, enc_vectors[5], enc_vectors[6])
    enc_low = enc_normed.astype(bf16)
    projected = mm("bsd,de->bse", enc_low, bridge_w)
    placer = (unshuffle[:, :, None] == jnp.arange(KEEP, dtype=jnp.int32)[None, None, :]).astype(f32)
    mask_column = masked.astype(f32)[:, :, None]
    filled = (
        jnp.einsum("bpk,bke->bpe", placer, projected[:, 1:], precision=highest_precision)
        + mask_column * dec_vectors[0]
        + sinusoid_table(D_D, GRID_PATCHES, IMAGE_PATCHES)
    )
    dec_start = jnp.concatenate([projected[:, :1], filled], axis=1)
    dec_end, dec_saved = layer_forward(
        dec_start, dec_in_w, dec_out_w, dec_vectors[1:5], dec_heads, HD_D
    )
    dec_normed, dec_unit, dec_inverse = norm_forward(dec_end, dec_vectors[5], dec_vectors[6])
    dec_low = dec_normed.astype(bf16)
    predicted = mm("bpe,ec->bpc", dec_low[:, 1:], head_w)
    pixels = images.astype(f32)
    pix_centred = pixels - jnp.mean(pixels, axis=-1, keepdims=True)
    variance = jnp.sum(pix_centred * pix_centred, axis=-1, keepdims=True) / (PATCH_DIM - 1)
    target = pix_centred * lax.rsqrt(variance + eps_norm)
    errors = predicted - target
    patch_weight = patch_flags / patch_total
    loss_part = jnp.sum(jnp.mean(errors * errors, axis=-1) * patch_weight)
    grad_pred = (errors * (2.0 / PATCH_DIM) * patch_weight[:, :, None]).astype(bf16)
    grad_head = mm("bpe,bpc->ec", dec_low[:, 1:], grad_pred)
    grad_dec_rows = mm("bpc,ec->bpe", grad_pred, head_w)
    grad_dec_norm = jnp.concatenate([jnp.zeros((image_count, 1, D_D), f32), grad_dec_rows], axis=1)
    grad_dec_end, dec_gain, dec_shift = norm_backward(
        grad_dec_norm, dec_unit, dec_inverse, dec_vectors[5]
    )
    grad_dec_start, grad_dec_in, grad_dec_out, grad_dec_vectors = layer_backward(
        grad_dec_end, dec_saved, dec_in_w, dec_out_w, dec_vectors[1:5], dec_heads, HD_D
    )
    grad_mask = jnp.sum(grad_dec_start[:, 1:] * mask_column, axis=(0, 1))
    grad_rest = jnp.einsum(
        "bpk,bpe->bke", placer, grad_dec_start[:, 1:], precision=highest_precision
    )
    grad_projected = jnp.concatenate([grad_dec_start[:, :1], grad_rest], axis=1).astype(bf16)
    grad_bridge = mm("bsd,bse->de", enc_low, grad_projected)
    grad_enc_norm = mm("bse,de->bsd", grad_projected, bridge_w)
    grad_enc_end, enc_gain, enc_shift = norm_backward(
        grad_enc_norm, enc_unit, enc_inverse, enc_vectors[5]
    )
    grad_enc_start, grad_enc_in, grad_enc_out, grad_enc_vectors = layer_backward(
        grad_enc_end, enc_saved, enc_in_w, enc_out_w, enc_vectors[1:5], enc_heads, HD_E
    )
    grad_class = jnp.sum(grad_enc_start[:, 0], axis=0)
    grad_embed = mm("wmx,wmg->xg", retained_pixels, grad_enc_start[:, 1:].astype(bf16))
    grad_vectors = jnp.concatenate(
        [
            jnp.concatenate(
                [grad_class[None], grad_enc_vectors, enc_gain[None], enc_shift[None]], axis=0
            ),
            jnp.concatenate(
                [grad_mask[None], grad_dec_vectors, dec_gain[None], dec_shift[None]], axis=0
            ),
        ],
        axis=1,
    )
    grad_pixel = jnp.concatenate([grad_embed, grad_head], axis=0)

    reduced, loss_value = reduce_all(
        ([grad_enc_in, grad_enc_out, grad_dec_in, grad_dec_out], grad_pixel, grad_bridge, grad_vectors),
        loss_part,
        masters,
    )
    decays = (decay_matrix,) * 6 + (0.0,)
    share_counts = (1.0,) * 4 + (float(tensor_count),) * 3
    bias_one = 1.0 - beta_one**step_count
    bias_two = 1.0 - beta_two**step_count
    new_firsts, new_seconds, updates = ([], [], [])
    for gradient, master, moment_one, moment_two, decay_value in zip(
        reduced, masters, firsts, seconds, decays
    ):
        next_one = beta_one * moment_one + (1.0 - beta_one) * gradient
        next_two = beta_two * moment_two + (1.0 - beta_two) * gradient * gradient
        new_firsts.append(next_one)
        new_seconds.append(next_two)
        updates.append(
            next_one / bias_one / (jnp.sqrt(next_two / bias_two) + eps_moment)
            + decay_value * master
        )

    def squares(members):
        return jnp.stack(
            [jnp.sum(member * member) / count for member, count in zip(members, share_counts)]
        )

    totals = lax.psum((squares(masters), squares(updates)), EVERY)
    weight_norm = jnp.sqrt(totals[0])
    update_norm = jnp.sqrt(totals[1])
    step_ratio = learn_rate * weight_norm / update_norm
    news = [
        master - step_ratio[position] * update
        for position, (master, update) in enumerate(zip(masters, updates))
    ]
    return tuple(
        [loss_value, jnp.stack([weight_norm, update_norm])] + new_firsts + new_seconds + news
    )


def solution(mesh):
    state_specs = (
        P("dp", "tensor", None),
        P("tensor", "dp", None),
        P("dp", "tensor", None),
        P("tensor", "dp", None),
        P("dp", None),
        P("dp", None),
        P(None, "dp"),
    )
    in_specs = (
        P("dp", None, None),
        P("dp", None),
        P("dp", None),
        P("dp", None),
        P("dp"),
    ) + state_specs * 3
    out_specs = (P(), P()) + state_specs * 3
    return jax.shard_map(shards, mesh=mesh, in_specs=in_specs, out_specs=out_specs, check_vma=False)
```

time: 1520 us -> 628 us (0.41)
  waiting for transfers between devices: 864 us -> 0 us
  Pallas kernels: 0 us -> 272 us
  blocking collectives: 198 us -> 39.5 us
  other arithmetic: 161 us -> 84.8 us
  local copies, waits for them, and re-layouts: 94.5 us -> 66.5 us
  matrix products: 170 us -> 148 us
  between operations: 22.3 us -> 6.91 us
    psum x8 -> x0, waiting for transfers between devices: 318 us -> none  [the longest x4 208 us: input_sum(): lax.psum(partial_grad.astype(jnp.bfloat16), 'tensor').astype(jnp.float32)]
    pallas_call x0 -> x2, Pallas kernels: none -> 272 us  [the longest x1 142 us: scatter_gradients(): pl.pallas_call(functools.partial(scatter_kernel, shapes, units), out_shap...]
    unnamed x19 -> x0, waiting for transfers between devices: 263 us -> none
    reduce_scatter x4 -> x0, waiting for transfers between devices: 213 us -> none  [the longest x1 77.4 us: shards(): lax.psum_scatter(grad_five, 'dp', scatter_dimension=0, tiled=True)]
    all_gather x4 -> x0, blocking collectives: 135 us -> none  [the longest x1 34.6 us: shards(): lax.all_gather(decoder_in.astype(jnp.bfloat16), 'dp', axis=0, tiled=True)]
    all_gather x3 -> x0, waiting for transfers between devices: 69.3 us -> none  [the longest x1 46.4 us: shards(): lax.all_gather(encoder_in.astype(jnp.bfloat16), 'dp', axis=0, tiled=True)]
    unnamed x339 -> x271, local copies, waits for them, and re-layouts: 44.2 us -> 19.4 us
    psum x2 -> x1, blocking collectives: 62.6 us -> 39.5 us  [shards(): totals = lax.psum((squares(masters), squares(updates)), EVERY)]
  transfers between devices with their start and end apart: 17 -> 0, of which waited for: 15 -> 0; matrix products, arithmetic and copies ran while one was open for 11% -> 0% of each run, Pallas kernels for 0% -> 0%
where the time goes in v1:
time: 628 us; the launch traced here: 618 us
  Pallas kernels  272 us (43%)
  matrix products  148 us (24%)
  other arithmetic  84.8 us (14%)
  local copies, waits for them, and re-layouts  66.5 us (11%)
  blocking collectives  39.5 us (6%)
  between operations  6.91 us (1%)
    pallas_call x1, Pallas kernels, scatter_gradients(): pl.pallas_call(functools.partial(scatter_kernel, shapes, units), out_shap...  142 us
    dot_general x43, matrix products, mm(): return jnp.einsum(spec, left, right, preferred_element_type=f32)  131 us
    pallas_call x1, Pallas kernels, gather_weights(): pl.pallas_call(gather_kernel, out_shape=outs, in_specs=[pl.BlockSpec(memo...  130 us
    psum x1, blocking collectives, shards(): totals = lax.psum((squares(masters), squares(updates)), EVERY)  39.5 us
    reduce_sum x9, other arithmetic, squares(): jnp.sum(member * member) / count  21.9 us
    unnamed x271, local copies, waits for them, and re-layouts  19.4 us
    concatenate x2, other arithmetic, layer_backward(): grad_in_cols = jnp.concatenate([grad_triple, grad_up], axis=2)  14.8 us
    sub x2, matrix products, layer_forward(): shifted = jnp.exp(scores - jnp.max(scores, axis=-1, keepdims=True))  13.6 us

profile of v1, /device:TPU:0, one launch (start us, length us, event | category | flops | bytes accessed | tf_op | source)
XLA Modules:
  0.0 618.4 jit_solution(8752546288318669760)
XLA Ops:
  28.3 129.9 %gather_weights.1 = (bf16[4,2,2,2,40,768]{5,4,3,2,1,0:T(8,128)(2,1)}, bf16[2,2,4,2,96,1344]{5,4,3,2,1,0:T(8,128)(2,1)}, bf16[2,2,4,2,120,768]{5,4,3,2,1,0:T(8,12...) custom-call(bf16[40,768]{1,0:T(8,128)(2,1)} %dynamic-slice_convert_f, ...), custom_call_target="tpu_custom_call" | custom-call | bytes 46923776 | tf_op jit(solution)/shard_map/gather_weights/pallas_call | solution.py:194
  166.0 3.2 fusion.97
  172.3 3.4 fusion.227
  183.6 11.4 %fusion.54 = (bf16[4,4,50,768]{3,2,0,1:T(8,128)(2,1)S(1)}, f32[4,4,50,768]{3,2,0,1:T(8,128)}, f32[4,768,4,50]{1,3,2,0:T(8,128)}) fusion(f32[4,50,768]{2,1,0:T(8,128)S(1)} %get-tuple-element.199, f32[768]{0:T(1024)S(1)} %copy-done.87, f32[768]{0:T(1024)S(1)} %get-tuple-element.132, f32[4,50]{1,0:T(4,128)S(1)} %add_rsqrt_fusion.5, ...), kind=kOutput, calls=%fused_computation.88 | convolution fusion | flops 984422400 | bytes 11484736 | tf_op jit(solution)/shard_map/bsd,tdc->btsc/dot_general | solution.py:436
  199.8 4.5 convert_bitcast_fusion
  204.3 4.5 copy.107
  208.8 11.0 %fusion.233 = (f32[4,4,4,197]{3,2,1,0:T(4,128)S(1)}, f32[4,4,4,197,197]{3,4,2,1,0:T(8,128)}) fusion(bf16[4,4,197,3,4,32]{2,5,4,3,1,0:T(8,128)(2,1)} %bitcast.649), kind=kOutput, calls=%fused_computation.448 | convolution fusion | flops 166413184 | bytes 12082688 | tf_op jit(solution)/shard_map/sub | solution.py:482
  219.8 6.7 %fusion.87 = bf16[4,4,4,32,197]{4,3,2,1,0:T(8,128)(2,1)S(1)} fusion(bf16[4,4,197,3,4,32]{2,5,4,3,1,0:T(8,128)(2,1)} %bitcast.650, f32[4,4,4,197,197]{3,4,2,1,0:T(8,128)} %get-tuple-element.204, f32[4,4,4,197]{3,2,1,0:T(4,128)S(1)} %get-tuple-element.203), kind=kOutput, calls=%fused_computation.160 | convolution fusion | flops 164332672 | bytes 15013120 | tf_op jit(solution)/shard_map/bthqk,btkhd->btqhd/dot_general | solution.py:436
  228.6 18.9 %fusion.14 = (bf16[4,4,197,512]{3,2,0,1:T(8,128)(2,1)S(1)}, f32[4,4,197,512]{3,2,0,1:T(8,128)}, f32[4,512,4,197]{1,3,2,0:T(8,128)}) fusion(f32[4,197,512]{2,1,0:T(8,128)S(1)} %get-tuple-element.206, f32[512]{0:T(512)S(1)} %bitcast.696, f32[512]{0:T(512)S(1)} %bitcast.686, f32[4,197]{1,0:T(4,128)S(1)} %add_rsqrt_fusion.2, ...), kind=kOutput, calls=%fused_computation.28 | convolution fusion | flops 1759471616 | bytes 19886080 | tf_op jit(solution)/shard_map/bsd,tdc->btsc/dot_general | solution.py:436
  258.1 7.2 %fusion.11 = bf16[4,4,197,512]{3,2,0,1:T(8,128)(2,1)S(1)} fusion(f32[4,4,197,512]{3,2,0,1:T(8,128)} %get-tuple-element.161, f32[4,512,4,197]{1,3,2,0:T(8,128)} %get-tuple-element.207, bf16[4,640,512]{2,1,0:T(8,128)(2,1)S(1)} %bitcast.673, f32[4,197,512]{2,1,0:T(8,128)S(1)} %subtract_multiply_fusion), kind=kOutput, calls=%fused_computation.20 | convolution fusion | flops 1675552768 | bytes 19873792 | tf_op jit(solution)/shard_map/bsd,tcd->btsc/dot_general | solution.py:436
  270.1 4.0 bitcast_convert_fusion.4
  281.0 7.3 %fusion.102 = bf16[4,4,197,1,4,32]{2,5,4,1,0,3:T(8,128)(2,1)S(1)} fusion(bf16[4,4,197,4,32]{2,4,3,1,0:T(8,128)(2,1)} %bitcast.663, f32[4,4,4,197,197]{3,4,2,1,0:T(8,128)} %get-tuple-element.204, f32[4,4,4,197]{3,2,1,0:T(4,128)S(1)} %get-tuple-element.203), kind=kOutput, calls=%fused_computation.176 | convolution fusion | flops 164332672 | bytes 11599360 | tf_op jit(solution)/shard_map/bthqk,btqhd->btkhd/dot_general | solution.py:436
  290.8 5.9 multiply_reduce_fusion
  296.7 6.6 %multiply_convert_fusion = bf16[4,4,4,197,197]{3,4,2,1,0:T(8,128)(2,1)S(1)} fusion(f32[4,4,4,197,197]{3,4,2,1,0:T(8,128)} %get-tuple-element.212, f32[4,4,4,197]{3,2,1,0:T(4,128)S(1)} %get-tuple-element.211, f32[4,4,4,197,197]{3,4,2,1,0:T(8,128)S(1)} %bitcast.647, f32[4,4,4,197]{3,2,1,0:T(4,128)S(1)} %get-tuple-element.203), kind=kLoop, calls=%fused_computation.2 | loop fusion | flops 9935104 | bytes 24938624 | tf_op jit(solution)/shard_map/convert_element_type | solution.py:544
  308.2 4.9 fusion.73
  319.0 4.6 pad_maximum_fusion.2.refs_4_
  330.5 5.2 fusion.51
  349.0 3.3 convert_element_type.274
  352.4 4.0 multiply_reduce_fusion.15
  365.9 6.1 copy.129
  372.0 3.7 bitcast_convert_fusion.1
  375.7 10.3 %pad_maximum_fusion.refs_1_ = bf16[2,2,4,2,96,1344]{5,4,3,2,1,0:T(8,128)(2,1)} fusion(bf16[2,2,4,2,96,768]{5,4,3,2,1,0:T(8,128)(2,1)} %bitcast.644, bf16[2,2,4,2,96,576]{5,4,3,2,1,0:T(8,128)(2,1)} %bitcast.645), kind=kLoop, calls=%fused_computation.10 | loop fusion | flops 16515072 | bytes 16515072 | tf_op jit(solution)/shard_map/concatenate | solution.py:555
  390.5 142.3 %scatter_gradients.1 = (f32[4,40,768]{2,1,0:T(8,128)}, f32[96,1344]{1,0:T(8,128)}, f32[120,768]{1,0:T(8,128)}, f32[4,24,512]{2,1,0:T(8,128)}, f32[64,896]{1,0:T(...) custom-call(bf16[4,2,2,2,40,768]{5,4,3,2,1,0:T(8,128)(2,1)} %bitcast.654, ...), custom_call_target="tpu_custom_call" | custom-call | bytes 46481408 | tf_op jit(solution)/shard_map/scatter_gradients/pallas_call | solution.py:421
  562.4 39.5 %all-reduce.4 = (f32[7]{0:T(128)S(1)}, f32[7]{0:T(128)S(1)}) all-reduce(f32[7]{0:T(128)S(1)} %stack.145, f32[7]{0:T(128)S(1)} %stack.136), channel_id=1, replica_groups=mesh['dp'=8,'tensor'=4] {'dp','tensor'}, use_global_device_ids=true, to_apply=%region_65.66 | all-reduce | flops 14 | bytes 112 | tf_op jit(solution)/shard_map/psum | solution.py:793
  (429 shorter events, 163.0 us)
Async XLA Ops:
  6.2 153.6 %copy-start.115 = (f32[4]{0:T(128)}, f32[4]{0:T(128)S(1)}, u32[]{:S(2)}) copy-start(f32[4]{0:T(128)S(1)} %dynamic-slice_convert_fusion.3) | copy-start | bytes 52
  26.8 136.3 %copy-start.93 = (f32[4,196]{1,0:T(4,128)}, f32[4,196]{1,0:T(4,128)S(1)}, u32[]{:S(2)}) copy-start(f32[4,196]{1,0:T(4,128)S(1)} %broadcast_multiply_fusion.1) | copy-start | bytes 9412
  28.3 134.8 %copy-start.36 = (bf16[4,49,768]{2,1,0:T(8,128)(2,1)}, bf16[4,49,768]{2,1,0:T(8,128)(2,1)S(1)}, u32[]{:S(2)}) copy-start(bf16[4,49,768]{2,1,0:T(8,128)(2,1)S(1)} %convolution_convert_fusion.4) | copy-start | bytes 903172
  163.1 20.5 %copy-start.65 = (f32[768]{0:T(1024)}, f32[768]{0:T(1024)S(1)}, u32[]{:S(2)}) copy-start(f32[768]{0:T(1024)S(1)} %get-tuple-element.132) | copy-start | bytes 9220
  163.1 33.7 %copy-start.67 = (f32[768]{0:T(1024)}, f32[768]{0:T(1024)S(1)}, u32[]{:S(2)}) copy-start(f32[768]{0:T(1024)S(1)} %get-tuple-element.129) | copy-start | bytes 9220
  163.1 18.1 %copy-start.58 = (f32[4,1,768]{2,1,0:T(1,128)}, f32[4,1,768]{2,1,0:T(1,128)S(1)}, u32[]{:S(2)}) copy-start(f32[4,1,768]{2,1,0:T(1,128)S(1)} %broadcast_in_dim.14) | copy-start | bytes 36868
  165.5 15.7 %copy-start.5 = (f32[4,49,768]{2,1,0:T(8,128)}, f32[4,49,768]{2,1,0:T(8,128)S(1)}, u32[]{:S(2)}) copy-start(f32[4,49,768]{2,1,0:T(8,128)S(1)} %convolution_add_fusion) | copy-start | bytes 1806340
  181.2 13.8 %copy-start.55 = (bf16[4,4,50,192]{3,1,2,0:T(4,128)(2,1)}, bf16[4,4,50,192]{3,1,2,0:T(4,128)(2,1)S(1)}, u32[]{:S(2)}) copy-start(bf16[4,4,50,192]{3,1,2,0:T(4,128)(2,1)S(1)} %convert_element_type.243) | copy-start | bytes 921604
  181.2 13.8 %slice-start.7 = ((s8[5898240]{0:T(1024)(128)(4,1)}), s8[4194304]{0:T(1024)(128)(4,1)S(1)}, s32[]{:S(2)}) async-start(s8[5898240]{0:T(1024)(128)(4,1)} %bitcast.714), calls=%async_computation.7 | async-start | bytes 8388608
  183.3 11.8 %copy-start.9 = (f32[4,50,768]{2,1,0:T(8,128)}, f32[4,50,768]{2,1,0:T(8,128)S(1)}, u32[]{:S(2)}) copy-start(f32[4,50,768]{2,1,0:T(8,128)S(1)} %get-tuple-element.199) | copy-start | bytes 1843204
  390.4 143.7 %copy-start.64 = (f32[7,160]{1,0:T(8,128)S(1)}, f32[7,160]{1,0:T(8,128)}, u32[]{:S(2)}) copy-start(f32[7,160]{1,0:T(8,128)} %param.37) | copy-start | bytes 13444
  390.4 143.7 %copy-start.103 = (f32[7,160]{1,0:T(8,128)S(1)}, f32[7,160]{1,0:T(8,128)}, u32[]{:S(2)}) copy-start(f32[7,160]{1,0:T(8,128)} %param.44) | copy-start | bytes 13444
  390.4 143.7 %copy-start.104 = (f32[7,160]{1,0:T(8,128)S(1)}, f32[7,160]{1,0:T(8,128)}, u32[]{:S(2)}) copy-start(f32[7,160]{1,0:T(8,128)} %param.51) | copy-start | bytes 13444
  390.4 146.4 %copy-start.34 = (f32[1,80,512]{2,1,0:T(8,128)S(1)}, f32[1,80,512]{2,1,0:T(8,128)}, u32[]{:S(2)}) copy-start(f32[1,80,512]{2,1,0:T(8,128)} %param.34) | copy-start | bytes 491524
  390.4 146.4 %copy-start.62 = (f32[1,80,512]{2,1,0:T(8,128)S(1)}, f32[1,80,512]{2,1,0:T(8,128)}, u32[]{:S(2)}) copy-start(f32[1,80,512]{2,1,0:T(8,128)} %param.41) | copy-start | bytes 491524
  390.5 146.4 %copy-start.63 = (f32[1,80,512]{2,1,0:T(8,128)S(1)}, f32[1,80,512]{2,1,0:T(8,128)}, u32[]{:S(2)}) copy-start(f32[1,80,512]{2,1,0:T(8,128)} %param.48) | copy-start | bytes 491524
  390.5 148.8 %copy-start.40 = (f32[96,512]{1,0:T(8,128)S(1)}, f32[96,512]{1,0:T(8,128)}, u32[]{:S(2)}) copy-start(f32[96,512]{1,0:T(8,128)} %param.36) | copy-start | bytes 589828
  390.5 148.8 %copy-start.60 = (f32[96,512]{1,0:T(8,128)S(1)}, f32[96,512]{1,0:T(8,128)}, u32[]{:S(2)}) copy-start(f32[96,512]{1,0:T(8,128)} %param.43) | copy-start | bytes 589828
  390.5 148.8 %copy-start.61 = (f32[96,512]{1,0:T(8,128)S(1)}, f32[96,512]{1,0:T(8,128)}, u32[]{:S(2)}) copy-start(f32[96,512]{1,0:T(8,128)} %param.50) | copy-start | bytes 589828
  390.5 152.6 %copy-start.16 = (f32[64,1,896]{2,1,0:T(1,128)S(1)}, f32[64,1,896]{2,1,0:T(1,128)}, u32[]{:S(2)}) copy-start(f32[64,1,896]{2,1,0:T(1,128)} %param.33) | copy-start | bytes 688132
  390.5 152.6 %copy-start.57 = (f32[64,1,896]{2,1,0:T(1,128)S(1)}, f32[64,1,896]{2,1,0:T(1,128)}, u32[]{:S(2)}) copy-start(f32[64,1,896]{2,1,0:T(1,128)} %param.40) | copy-start | bytes 688132
  532.9 14.7 %copy-start.17 = (f32[1,120,768]{2,1,0:T(8,128)S(1)}, f32[1,120,768]{2,1,0:T(8,128)}, u32[]{:S(2)}) copy-start(f32[1,120,768]{2,1,0:T(8,128)} %param.32) | copy-start | bytes 1105924
  535.5 72.3 %copy-start.74 = (f32[7,160]{1,0:T(8,128)}, f32[7,160]{1,0:T(8,128)S(1)}, u32[]{:S(2)}) copy-start(f32[7,160]{1,0:T(8,128)S(1)} %get-tuple-element.140) | copy-start | bytes 13444
  535.5 72.3 %copy-start.75 = (f32[7,160]{1,0:T(8,128)}, f32[7,160]{1,0:T(8,128)S(1)}, u32[]{:S(2)}) copy-start(f32[7,160]{1,0:T(8,128)S(1)} %get-tuple-element.141) | copy-start | bytes 13444
  (107 other events, 491.0 us)

commit v2 on v1

--- a/solution.py
+++ b/solution.py
@@ -6,6 +6,7 @@
 from jax.experimental import pallas as pl
 from jax.experimental.pallas import tpu as pltpu
 from jax.sharding import PartitionSpec as P
+import numpy as np
 
 ENCODER_WIDTH = 768
 H_E = 12
@@ -25,7 +26,6 @@
 learn_rate = 0.3
 decay_matrix = 0.05
 eps_moment = 1e-06
-highest_precision = lax.Precision.HIGHEST
 f32 = jnp.float32
 bf16 = jnp.bfloat16
 EVERY = ("dp", "tensor")
@@ -432,134 +432,483 @@
     )(*grads)
 
 
-def mm(spec, left, right):
-    return jnp.einsum(spec, left, right, preferred_element_type=f32)
-
-
-def sinusoid_table(feature_width, grid_side, patch_count):
-    position = jnp.arange(patch_count, dtype=jnp.int32)
+def sinusoid_table(feature_width, grid_side, patch_count, padded):
+    position = np.arange(patch_count)
     quarter = feature_width // 4
-    omegas = 1.0 / 10000.0 ** (jnp.arange(quarter, dtype=f32) / quarter)
-
-    def half_table(coords):
-        angles = coords.astype(f32)[:, None] * omegas[None, :]
-        return jnp.concatenate([jnp.sin(angles), jnp.cos(angles)], axis=1)
-
-    return jnp.concatenate(
-        [half_table(position % grid_side), half_table(position // grid_side)], axis=1
+    omegas = 1.0 / 10000.0 ** (np.arange(quarter) / quarter)
+    parts = []
+    for coords in (position % grid_side, position // grid_side):
+        angles = coords[:, None] * omegas[None, :]
+        parts += [np.sin(angles), np.cos(angles)]
+    table = np.concatenate(parts, axis=1).astype(np.float32)
+    return jnp.asarray(np.pad(table, ((0, padded - patch_count), (0, 0))))
+
+
+GROUPS = 4
+ENC = dict(step=128, images=4, block=64, tokens=50, width=768, heads=3, head=64, hidden=768, spans=1)
+DEC = dict(step=208, images=4, block=208, tokens=197, width=512, heads=4, head=32, hidden=512, spans=4)
+CLASS_ROW = 49
+MASK_ROW = 50
+
+
+def dot(left, right, dims=((1,), (0,)), precision=None):
+    return lax.dot_general(
+        left, right, (dims, ((), ())), preferred_element_type=f32, precision=precision
     )
 
 
-def norm_forward(stream, gain_row, shift_row):
-    centred = stream - jnp.mean(stream, axis=-1, keepdims=True)
-    inverse = lax.rsqrt(jnp.mean(centred * centred, axis=-1, keepdims=True) + eps_norm)
-    unit_values = centred * inverse
-    return (unit_values * gain_row + shift_row, unit_values, inverse)
-
-
-def norm_backward(incoming, unit_values, inverse, gain_row):
-    scaled = incoming * gain_row
-    inner_part = (
-        scaled
-        - jnp.mean(scaled, axis=-1, keepdims=True)
-        - unit_values * jnp.mean(scaled * unit_values, axis=-1, keepdims=True)
+def dot_t(left, right):
+    return dot(left, right, ((0,), (0,)))
+
+
+def dot_nt(left, right):
+    return dot(left, right, ((1,), (1,)))
+
+
+def exact_dot(left, right, dims):
+    return dot(left, right, dims, lax.Precision.HIGHEST)
+
+
+def row_loop(count, step, body):
+    @pl.loop(0, count // step)
+    def _(k):
+        body(pl.ds(pl.multiple_of(k * step, step), step))
+
+
+def fold(values):
+    step, width = values.shape
+    return jnp.sum(values.reshape(step // 8, 8, width), axis=0)
+
+
+def norm_rows(source, gain, shift, unit, inverse, low, step):
+    def body(rows):
+        values = source[rows]
+        centred = values - jnp.mean(values, axis=-1, keepdims=True)
+        scale = lax.rsqrt(jnp.mean(centred * centred, axis=-1, keepdims=True) + eps_norm)
+        normed = centred * scale
+        unit[rows] = normed
+        inverse[rows] = scale
+        low[rows] = (normed * gain + shift).astype(bf16)
+
+    row_loop(source.shape[0], step, body)
+
+
+def norm_back_rows(incoming, unit, inverse, gain, result, residual, sums, at, step):
+    width = incoming.shape[-1]
+
+    def body(rows):
+        given = incoming[rows]
+        normed = unit[rows]
+        scaled = given * gain
+        inner = (
+            scaled
+            - jnp.mean(scaled, axis=-1, keepdims=True)
+            - normed * jnp.mean(scaled * normed, axis=-1, keepdims=True)
+        )
+        value = inverse[rows] * inner
+        if residual is not None:
+            value = value + residual[rows]
+        sums[at] = sums[at] + fold(given * normed)
+        sums[at + 1] = sums[at + 1] + fold(given)
+        result[rows] = value
+
+    row_loop(incoming.shape[0], step, body)
+
+
+def attend_mask(dims):
+    size = dims["block"] * dims["images"] // dims["spans"]
+    key = lax.broadcasted_iota(jnp.int32, (size, size), 1)
+    if dims["spans"] == 1:
+        query = lax.broadcasted_iota(jnp.int32, (size, size), 0)
+        return ((key // dims["block"]) == (query // dims["block"])) & (
+            (key % dims["block"]) < dims["tokens"]
+        )
+    return key < dims["tokens"]
+
+
+def layer_forward_rows(dims, stream, w_in, w_out, vectors, saved):
+    unit_one, inv_one, low_one, qkv, probs, mixed, unit_two, inv_two, low_two, active, slope = saved
+    count, width = stream.shape
+    inner = dims["heads"] * dims["head"]
+    span = count // dims["spans"]
+    norm_rows(stream, vectors[1:2, :], vectors[2:3, :], unit_one, inv_one, low_one, dims["step"])
+
+    @pl.loop(0, GROUPS)
+    def _(t):
+        weights = w_in[t, :, : 3 * inner] if inner % 128 == 0 else w_in[t][:, : 3 * inner]
+
+        def body(rows):
+            qkv[t, rows] = dot(low_one[rows], weights).astype(bf16)
+
+        body(slice(None))
+
+    scale = dims["head"] ** (-0.5)
+
+    @pl.loop(0, GROUPS * dims["spans"])
+    def _(k):
+        t = k // dims["spans"]
+        b = k % dims["spans"]
+        rows = pl.ds(pl.multiple_of(b * span, span), span)
+        triple = qkv[t, rows]
+        allowed = attend_mask(dims)
+        results = []
+        for head in range(dims["heads"]):
+            q, key, v = (
+                triple[:, part * inner + head * dims["head"] : part * inner + (head + 1) * dims["head"]]
+                for part in range(3)
+            )
+            scores = jnp.where(allowed, dot_nt(q, key) * scale, -1e30)
+            shifted = jnp.exp(scores - jnp.max(scores, axis=-1, keepdims=True))
+            share = shifted / jnp.sum(shifted, axis=-1, keepdims=True)
+            probs[k * dims["heads"] + head] = share
+            results.append(dot(share.astype(bf16), v))
+        mixed[t, rows] = jnp.concatenate(results, axis=1).astype(bf16)
+
+    @pl.loop(0, GROUPS)
+    def _(t):
+        weights = w_out[t, :inner]
+
+        def body(rows):
+            stream[rows] = stream[rows] + dot(mixed[t, rows], weights)
+
+        body(slice(None))
+
+    norm_rows(stream, vectors[3:4, :], vectors[4:5, :], unit_two, inv_two, low_two, dims["step"])
+
+    @pl.loop(0, GROUPS)
+    def _(t):
+        up = w_in[t, :, 3 * inner :] if inner % 128 == 0 else w_in[t][:, 3 * inner :]
+        down = w_out[t, inner:]
+
+        def body(rows):
+            slope[t, rows] = dot(low_two[rows], up)
+
+        body(slice(None))
+
+        def bend(rows):
+            hidden = slope[t, rows]
+            level = 0.5 + 0.5 * lax.erf(hidden * (0.5**0.5))
+            active[t, rows] = (hidden * level).astype(bf16)
+            slope[t, rows] = level + hidden * (
+                jnp.exp(-0.5 * hidden * hidden) * (0.5 / np.pi) ** 0.5
+            )
+
+        row_loop(count, 32, bend)
+
+        def body_two(rows):
+            stream[rows] = stream[rows] + dot(active[t, rows], down)
+
+        body_two(slice(None))
+
+
+def layer_backward_rows(dims, given, spare, w_in, w_out, vectors, saved, low, flow, grad_in, grad_out, sums):
+    unit_one, inv_one, low_one, qkv, probs, mixed, unit_two, inv_two, low_two, active, slope = saved
+    count, width = given.shape
+    inner = dims["heads"] * dims["head"]
+    span = count // dims["spans"]
+    aligned = inner % 128 == 0
+
+    def lower(rows):
+        low[rows] = given[rows].astype(bf16)
+        spare[rows] = jnp.zeros_like(spare[rows])
+
+    row_loop(count, 32, lower)
+
+    @pl.loop(0, GROUPS)
+    def _(t):
+        down = w_out[t, inner:]
+        up = w_in[t, :, 3 * inner :] if aligned else w_in[t][:, 3 * inner :]
+        grad_out[t, inner:] = dot_t(active[t], low[...]).astype(bf16)
+
+        def body(rows):
+            flow[rows] = (slope[t, rows] * dot_nt(low[rows], down)).astype(bf16)
+            spare[rows] = spare[rows] + dot_nt(flow[rows], up)
+
+        body(slice(None))
+        grad_up = dot_t(low_two[...], flow[...]).astype(bf16)
+        if aligned:
+            grad_in[t, :, 3 * inner :] = grad_up
+        else:
+            grad_in[t] = jnp.concatenate([jnp.zeros((width, 3 * inner), bf16), grad_up], axis=1)
+
+    norm_back_rows(spare, unit_two, inv_two, vectors[3:4, :], given, given, sums, 3, dims["step"])
+    row_loop(count, 32, lower)
+
+    @pl.loop(0, GROUPS)
+    def _(t):
+        weights = w_out[t, :inner]
+        grad_out[t, :inner] = dot_t(mixed[t], low[...]).astype(bf16)
+
+        def body(rows):
+            mixed[t, rows] = dot_nt(low[rows], weights).astype(bf16)
+
+        body(slice(None))
+
+    scale = dims["head"] ** (-0.5)
+
+    @pl.loop(0, GROUPS * dims["spans"])
+    def _(k):
+        t = k // dims["spans"]
+        b = k % dims["spans"]
+        rows = pl.ds(pl.multiple_of(b * span, span), span)
+        triple = qkv[t, rows]
+        back = mixed[t, rows]
+        parts = ([], [], [])
+        for head in range(dims["heads"]):
+            q, key, v = (
+                triple[:, part * inner + head * dims["head"] : part * inner + (head + 1) * dims["head"]]
+                for part in range(3)
+            )
+            grad_o = back[:, head * dims["head"] : (head + 1) * dims["head"]]
+            share = probs[k * dims["heads"] + head]
+            grad_p = dot_nt(grad_o, v)
+            grad_s = share * (grad_p - jnp.sum(share * grad_p, axis=-1, keepdims=True))
+            low_s = grad_s.astype(bf16)
+            parts[0].append(dot(low_s, key) * scale)
+            parts[1].append(dot_t(low_s, q) * scale)
+            parts[2].append(dot_t(share.astype(bf16), grad_o))
+        qkv[t, rows] = jnp.concatenate(parts[0] + parts[1] + parts[2], axis=1).astype(bf16)
+
+    @pl.loop(0, GROUPS)
+    def _(t):
+        weights = w_in[t, :, : 3 * inner] if aligned else w_in[t][:, : 3 * inner]
+        grad_triple = dot_t(low_one[...], qkv[t]).astype(bf16)
+        if aligned:
+            grad_in[t, :, : 3 * inner] = grad_triple
+        else:
+            grad_in[t] = jnp.concatenate([grad_triple, grad_in[t][:, 3 * inner :]], axis=1)
+
+        def body(rows):
+            spare[rows] = spare[rows] + dot_nt(qkv[t, rows], weights)
+
+        body(slice(None))
+
+    norm_back_rows(spare, unit_one, inv_one, vectors[1:2, :], given, given, sums, 1, dims["step"])
+
+
+def saved_shapes(dims):
+    count = dims["images"] * dims["block"]
+    width, inner = dims["width"], dims["heads"] * dims["head"]
+    span = count // dims["spans"]
+    return [
+        ((count, width), f32),
+        ((count, 1), f32),
+        ((count, width), bf16),
+        ((GROUPS, count, 3 * inner), bf16),
+        ((GROUPS * dims["spans"] * dims["heads"], span, span), f32),
+        ((GROUPS, count, inner), bf16),
+        ((count, width), f32),
+        ((count, 1), f32),
+        ((count, width), bf16),
+        ((GROUPS, count, dims["hidden"]), bf16),
+        ((GROUPS, count, dims["hidden"]), f32),
+    ]
+
+
+def decoder_kernel(*refs):
+    projected, codes, weight_rows, images, table, w_in, w_out, head, vectors = refs[:9]
+    grad_in, grad_out, grad_head, grad_projected, vec_out = refs[9:14]
+    stream, given, unit, inverse, low, flow, sums, loss = refs[14:22]
+    saved = refs[22:]
+    dims = DEC
+    count, width = stream.shape
+    block = dims["block"]
+    sums[...] = jnp.zeros_like(sums)
+    loss[...] = jnp.zeros_like(loss)
+
+    def placer(b):
+        return (
+            lax.broadcasted_iota(jnp.int32, (64, block), 0) == codes[b][:, :block]
+        ).astype(f32)
+
+    def block_rows(b):
+        return pl.ds(pl.multiple_of(b * block, block), block)
+
+    @pl.loop(0, dims["images"])
+    def _(b):
+        at = lax.broadcasted_iota(jnp.int32, (64, width), 0)
+        source = jnp.where(at == MASK_ROW, vectors[0:1, :], projected[b])
+        source = jnp.where(at > MASK_ROW, 0.0, source)
+        stream[block_rows(b)] = exact_dot(placer(b), source, ((0,), (0,))) + table[...]
+
+    layer_forward_rows(dims, stream, w_in, w_out, vectors, saved)
+    norm_rows(stream, vectors[5:6, :], vectors[6:7, :], unit, inverse, low, dims["step"])
+    grad_head[...] = jnp.zeros_like(grad_head)
+    pixels_wide = images.shape[-1]
+
+    @pl.loop(0, dims["images"])
+    def _(b):
+        rows = block_rows(b)
+        predicted = dot(low[rows], head[...])
+        pixels = images[b].astype(f32)
+        centred = pixels - jnp.mean(pixels, axis=-1, keepdims=True)
+        variance = jnp.sum(centred * centred, axis=-1, keepdims=True) / (pixels_wide - 1)
+        errors = predicted - centred * lax.rsqrt(variance + eps_norm)
+        at = lax.broadcasted_iota(jnp.int32, (64, 128), 0)
+        spread = jnp.where(at == MASK_ROW, weight_rows[b], 0.0)
+        weight = exact_dot(placer(b), spread, ((0,), (0,)))[:, :1]
+        loss[...] = loss[...] + fold(errors * errors * weight)
+        grad_low = (errors * (2.0 / pixels_wide) * weight).astype(bf16)
+        grad_head[...] = grad_head[...] + dot_t(low[rows], grad_low)
+        given[rows] = dot_nt(grad_low, head[...])
+
+    norm_back_rows(given, unit, inverse, vectors[5:6, :], given, None, sums, 5, dims["step"])
+    layer_backward_rows(
+        dims, given, stream, w_in, w_out, vectors, saved, low, flow, grad_in, grad_out, sums
     )
-    width = incoming.shape[-1]
-    gain_grad = jnp.sum((incoming * unit_values).reshape(-1, width), axis=0)
-    shift_grad = jnp.sum(incoming.reshape(-1, width), axis=0)
-    return (inverse * inner_part, gain_grad, shift_grad)
-
-
-def layer_forward(stream, w_input, w_output, vectors, group_heads, head_dim):
-    image_count, token_count, model_width = stream.shape
-    groups = w_input.shape[0]
-    inner = group_heads * head_dim
-    normed_one, unit_one, inverse_one = norm_forward(stream, vectors[0], vectors[1])
-    input_one = normed_one.astype(bf16)
-    raw_heads = mm("bsd,tdc->btsc", input_one, w_input[:, :, : 3 * inner]).astype(bf16)
-    triple = raw_heads.reshape(image_count, groups, token_count, 3, group_heads, head_dim)
-    scores = mm("btqhd,btkhd->bthqk", triple[:, :, :, 0], triple[:, :, :, 1]) * head_dim ** (-0.5)
-    shifted = jnp.exp(scores - jnp.max(scores, axis=-1, keepdims=True))
-    attention = shifted / jnp.sum(shifted, axis=-1, keepdims=True)
-    mixed = mm("bthqk,btkhd->btqhd", attention.astype(bf16), triple[:, :, :, 2])
-    mixed_low = mixed.reshape(image_count, groups, token_count, inner).astype(bf16)
-    after_attn = stream + mm("btsc,tcd->bsd", mixed_low, w_output[:, :inner])
-    normed_two, unit_two, inverse_two = norm_forward(after_attn, vectors[2], vectors[3])
-    input_two = normed_two.astype(bf16)
-    hidden = mm("bsd,tdc->btsc", input_two, w_input[:, :, 3 * inner :])
-    active = jax.nn.gelu(hidden, approximate=False).astype(bf16)
-    result = after_attn + mm("btsc,tcd->bsd", active, w_output[:, inner:])
-    saved_state = (
-        unit_one,
-        inverse_one,
-        input_one,
-        triple,
-        attention,
-        mixed_low,
-        unit_two,
-        inverse_two,
-        input_two,
-        hidden,
-        active,
+
+    @pl.loop(0, dims["images"])
+    def _(b):
+        back = exact_dot(placer(b), given[block_rows(b)], ((1,), (0,)))
+        at = lax.broadcasted_iota(jnp.int32, (64, width), 0)
+        grad_projected[b] = jnp.where(at < MASK_ROW, back, 0.0).astype(bf16)
+        sums[0] = sums[0] + fold(jnp.where(at == MASK_ROW, back, 0.0))
+
+    for row in range(7):
+        vec_out[row : row + 1, :] = jnp.sum(sums[row], axis=0, keepdims=True)
+    total = jnp.sum(jnp.sum(loss[...], axis=0, keepdims=True), axis=1, keepdims=True)
+    vec_out[7:8, :] = jnp.broadcast_to(total / pixels_wide, (1, width))
+
+
+def decoder_step(projected, codes, weight_rows, images, table, w_in, w_out, head, vectors):
+    dims = DEC
+    count, width = dims["images"] * dims["block"], dims["width"]
+    outs = [
+        jax.ShapeDtypeStruct(w_in.shape, bf16),
+        jax.ShapeDtypeStruct(w_out.shape, bf16),
+        jax.ShapeDtypeStruct(head.shape, f32),
+        jax.ShapeDtypeStruct(projected.shape, bf16),
+        jax.ShapeDtypeStruct((8, width), f32),
+    ]
+    scratch = [
+        ((count, width), f32),
+        ((count, width), f32),
+        ((count, width), f32),
+        ((count, 1), f32),
+        ((count, width), bf16),
+        ((count, dims["hidden"]), bf16),
+        ((7, 8, width), f32),
+        ((8, images.shape[-1]), f32),
+    ] + saved_shapes(dims)
+    return pl.pallas_call(
+        decoder_kernel,
+        out_shape=outs,
+        scratch_shapes=[pltpu.VMEM(shape, dtype) for shape, dtype in scratch],
+        compiler_params=pltpu.CompilerParams(vmem_limit_bytes=62 * 1024 * 1024),
+        name="decoder_step",
+    )(projected, codes, weight_rows, images, table, w_in, w_out, head, vectors)
+
+
+def encoder_forward_kernel(*refs):
+    kept, images, table, w_in, w_out, embed, bridge, vectors = refs[:8]
+    projected, retained, unit, inverse, low = refs[8:13]
+    saved = refs[13:24]
+    (stream,) = refs[24:]
+    dims = ENC
+    count, width = stream.shape
+    block = dims["block"]
+
+    @pl.loop(0, dims["images"])
+    def _(b):
+        rows = pl.ds(pl.multiple_of(b * block, block), block)
+        choice = (
+            lax.broadcasted_iota(jnp.int32, (table.shape[0], block), 0) == kept[b][:, :block]
+        )
+        retained[rows] = dot_t(choice.astype(bf16), images[b]).astype(bf16)
+        places = exact_dot(choice.astype(f32), table[...], ((0,), (0,)))
+        at = lax.broadcasted_iota(jnp.int32, (block, width), 0)
+        start = dot(retained[rows], embed[...]) + places
+        stream[rows] = jnp.where(at == CLASS_ROW, vectors[0:1, :], start)
+
+    layer_forward_rows(dims, stream, w_in, w_out, vectors, saved)
+    norm_rows(stream, vectors[5:6, :], vectors[6:7, :], unit, inverse, low, dims["step"])
+
+    @pl.loop(0, dims["images"])
+    def _(b):
+        rows = pl.ds(pl.multiple_of(b * block, block), block)
+        projected[b] = dot(low[rows], bridge[...])
+
+
+def encoder_forward(kept, images, table, w_in, w_out, embed, bridge, vectors):
+    dims = ENC
+    count, width = dims["images"] * dims["block"], dims["width"]
+    outs = [
+        ((dims["images"], dims["block"], bridge.shape[1]), f32),
+        ((count, images.shape[-1]), bf16),
+        ((count, width), f32),
+        ((count, 1), f32),
+        ((count, width), bf16),
+    ] + saved_shapes(dims)
+    return pl.pallas_call(
+        encoder_forward_kernel,
+        out_shape=[jax.ShapeDtypeStruct(shape, dtype) for shape, dtype in outs],
+        scratch_shapes=[pltpu.VMEM((count, width), f32)],
+        compiler_params=pltpu.CompilerParams(vmem_limit_bytes=62 * 1024 * 1024),
+        name="encoder_forward",
+    )(kept, images, table, w_in, w_out, embed, bridge, vectors)
+
+
+def encoder_backward_kernel(*refs):
+    grad_projected, retained, unit, inverse, low_end = refs[:5]
+    saved = list(refs[5:16])
+    w_in, w_out, bridge, vectors = refs[16:20]
+    grad_in, grad_out, grad_bridge, grad_embed, vec_out = refs[20:25]
+    given, spare, low, flow, sums, qkv, mixed = refs[25:]
+    dims = ENC
+    count, width = given.shape
+    block = dims["block"]
+    sums[...] = jnp.zeros_like(sums)
+    qkv[...] = saved[3][...]
+    mixed[...] = saved[5][...]
+    saved[3], saved[5] = qkv, mixed
+
+    flat = grad_projected[...].reshape(count, grad_projected.shape[-1])
+    grad_bridge[...] = dot_t(low_end[...], flat).astype(bf16)
+    given[...] = dot_nt(flat, bridge[...])
+    norm_back_rows(given, unit, inverse, vectors[5:6, :], given, None, sums, 5, dims["step"])
+    layer_backward_rows(
+        dims, given, spare, w_in, w_out, vectors, saved, low, flow, grad_in, grad_out, sums
     )
-    return (result, saved_state)
-
-
-def layer_backward(stream_grad, saved_state, w_input, w_output, vectors, group_heads, head_dim):
-    (
-        unit_one,
-        inverse_one,
-        input_one,
-        triple,
-        attention,
-        mixed_low,
-        unit_two,
-        inverse_two,
-        input_two,
-        hidden,
-        active,
-    ) = saved_state
-    image_count, token_count, model_width = stream_grad.shape
-    groups = w_input.shape[0]
-    inner = group_heads * head_dim
-    score_scale = head_dim ** (-0.5)
-    grad_low = stream_grad.astype(bf16)
-    grad_down = mm("btsc,bsd->tcd", active, grad_low)
-    grad_active = mm("bsd,tcd->btsc", grad_low, w_output[:, inner:])
-    gelu_back = jax.vjp(lambda values: jax.nn.gelu(values, approximate=False), hidden)[1]
-    grad_hidden = gelu_back(grad_active)[0].astype(bf16)
-    grad_up = mm("bsd,btsc->tdc", input_two, grad_hidden)
-    grad_two = mm("btsc,tdc->bsd", grad_hidden, w_input[:, :, 3 * inner :])
-    grad_mid, gain_two, shift_two = norm_backward(grad_two, unit_two, inverse_two, vectors[2])
-    grad_mid = grad_mid + stream_grad
-    mid_low = grad_mid.astype(bf16)
-    grad_attn_rows = mm("btsc,bsd->tcd", mixed_low, mid_low)
-    grad_mixed = mm("bsd,tcd->btsc", mid_low, w_output[:, :inner]).astype(bf16)
-    grad_mixed = grad_mixed.reshape(image_count, groups, token_count, group_heads, head_dim)
-    grad_values = mm("bthqk,btqhd->btkhd", attention.astype(bf16), grad_mixed)
-    grad_attention = mm("btqhd,btkhd->bthqk", grad_mixed, triple[:, :, :, 2])
-    grad_scores = attention * (
-        grad_attention - jnp.sum(attention * grad_attention, axis=-1, keepdims=True)
-    )
-    scores_low = grad_scores.astype(bf16)
-    grad_queries = mm("bthqk,btkhd->btqhd", scores_low, triple[:, :, :, 1]) * score_scale
-    grad_keys = mm("bthqk,btqhd->btkhd", scores_low, triple[:, :, :, 0]) * score_scale
-    grad_raw = (
-        jnp.stack([grad_queries, grad_keys, grad_values], axis=3)
-        .reshape(image_count, groups, token_count, 3 * inner)
-        .astype(bf16)
-    )
-    grad_triple = mm("bsd,btsc->tdc", input_one, grad_raw)
-    grad_one = mm("btsc,tdc->bsd", grad_raw, w_input[:, :, : 3 * inner])
-    grad_stream, gain_one, shift_one = norm_backward(grad_one, unit_one, inverse_one, vectors[0])
-    grad_in_cols = jnp.concatenate([grad_triple, grad_up], axis=2)
-    grad_out_rows = jnp.concatenate([grad_attn_rows, grad_down], axis=1)
-    return (
-        grad_stream + grad_mid,
-        grad_in_cols,
-        grad_out_rows,
-        jnp.stack([gain_one, shift_one, gain_two, shift_two]),
-    )
+    grad_embed[...] = dot_t(retained[...], given[...].astype(bf16)).astype(bf16)
+
+    def tokens(rows):
+        at = lax.broadcasted_iota(jnp.int32, (block, width), 0)
+        sums[0] = sums[0] + fold(jnp.where(at == CLASS_ROW, given[rows], 0.0))
+
+    row_loop(count, block, tokens)
+    for row in range(7):
+        vec_out[row : row + 1, :] = jnp.sum(sums[row], axis=0, keepdims=True)
+    vec_out[7:8, :] = jnp.zeros((1, width), f32)
+
+
+def encoder_backward(grad_projected, kept_state, w_in, w_out, bridge, vectors):
+    dims = ENC
+    count, width = dims["images"] * dims["block"], dims["width"]
+    shapes = saved_shapes(dims)
+    pixels_wide = kept_state[0].shape[1]
+    outs = [
+        jax.ShapeDtypeStruct(w_in.shape, bf16),
+        jax.ShapeDtypeStruct(w_out.shape, bf16),
+        jax.ShapeDtypeStruct(bridge.shape, bf16),
+        jax.ShapeDtypeStruct((pixels_wide, width), bf16),
+        jax.ShapeDtypeStruct((8, width), f32),
+    ]
+    scratch = [
+        ((count, width), f32),
+        ((count, width), f32),
+        ((count, width), bf16),
+        ((count, dims["hidden"]), bf16),
+        ((7, 8, width), f32),
+        shapes[3],
+        shapes[5],
+    ]
+    return pl.pallas_call(
+        encoder_backward_kernel,
+        out_shape=outs,
+        scratch_shapes=[pltpu.VMEM(shape, dtype) for shape, dtype in scratch],
+        compiler_params=pltpu.CompilerParams(vmem_limit_bytes=62 * 1024 * 1024),
+        name="encoder_backward",
+    )(grad_projected, *kept_state, w_in, w_out, bridge, vectors)
 
 
 def gather_grouped(part, groups):
@@ -568,7 +917,7 @@
 
 
 def scatter_grouped(gradient):
-    flat = gradient.reshape(-1, gradient.shape[-1])
+    flat = gradient.astype(f32).reshape(-1, gradient.shape[-1])
     return lax.psum_scatter(flat, GROUPED, scatter_dimension=0, tiled=True)
 
 
@@ -616,14 +965,11 @@
     return grouped, pixel_w, bridge_w, vectors_all, lax.psum(counted, "dp")
 
 
-def reduce_all(gradients, loss_part, masters):
+def reduce_all(gradients, masters):
     tensor_count = lax.axis_size("tensor")
     columns = masters[6].shape[1]
     dp_at = lax.axis_index("dp")
-    grouped, grad_pixel, grad_bridge, grad_vectors = gradients
-    packed = jnp.concatenate(
-        [grad_vectors, jnp.broadcast_to(loss_part, (1, grad_vectors.shape[1]))], axis=0
-    )
+    grouped, grad_pixel, grad_bridge, packed = gradients
     if ringed(tensor_count):
         shapes = {
             EIN: masters[0].reshape(-1, masters[0].shape[-1]).shape,
@@ -635,7 +981,7 @@
         }
         sources = {PIX: grad_pixel, EIN: grouped[0], EOUT: grouped[1], BRI: grad_bridge, DIN: grouped[2], DOUT: grouped[3]}
         operands = [
-            sources[array].astype(bf16).reshape(whole_shape(array, shapes[array]))
+            sources[array].reshape(whole_shape(array, shapes[array]))
             for array in range(6)
         ]
         sums = scatter_gradients(operands + [packed])
@@ -644,7 +990,7 @@
     else:
 
         def scatter_shared(gradient):
-            part = lax.psum_scatter(gradient, EVERY, scatter_dimension=0, tiled=True)
+            part = lax.psum_scatter(gradient.astype(f32), EVERY, scatter_dimension=0, tiled=True)
             return lax.all_gather(part, "tensor", axis=0, tiled=True)
 
         reduced = [scatter_grouped(gradient) for gradient in grouped]
@@ -652,7 +998,7 @@
         vector_sum = lax.psum(packed, EVERY)
     own = lax.dynamic_slice_in_dim(vector_sum[:7], dp_at * columns, columns, axis=1)
     reduced = [gradient.reshape(master.shape) for gradient, master in zip(reduced + [own], masters)]
-    return reduced, vector_sum[7, 0]
+    return reduced, vector_sum[7, -1]
 
 
 def shards(
@@ -670,12 +1016,8 @@
     counted = jnp.sum(masked.astype(f32) * image_valid.astype(f32)[:, None])
     grouped_w, pixel_w, bridge_w, vectors_all, patch_total = gather_all(masters, counted)
     enc_in_w, enc_out_w, dec_in_w, dec_out_w = grouped_w
-    embedding_weight = pixel_w[:PATCH_DIM]
-    head_w = pixel_w[PATCH_DIM:]
     enc_vectors = vectors_all[:, :ENCODER_WIDTH]
     dec_vectors = vectors_all[:, ENCODER_WIDTH:]
-    enc_heads = H_E // tensor_count
-    dec_heads = H_D // tensor_count
     image_count = images.shape[0] // tensor_count
 
     def own(member):
@@ -684,88 +1026,47 @@
     images, keep_index, unshuffle, masked, image_valid = map(
         own, (images, keep_index, unshuffle, masked, image_valid)
     )
-    patch_flags = masked.astype(f32) * image_valid.astype(f32)[:, None]
-    patch_ids = jnp.arange(IMAGE_PATCHES, dtype=jnp.int32)
-    selection_matrix = (keep_index[:, :, None] == patch_ids[None, None, :]).astype(f32)
-    retained_pixels = mm("bkp,bpc->bkc", selection_matrix.astype(bf16), images).astype(bf16)
-    kept_pos = jnp.einsum(
-        "nau,uc->nac",
-        selection_matrix,
-        sinusoid_table(ENCODER_WIDTH, GRID_PATCHES, IMAGE_PATCHES),
-        precision=highest_precision,
+    block = DEC["block"]
+    images = jnp.pad(images, ((0, 0), (0, block - IMAGE_PATCHES), (0, 0)))
+    lanes = 256
+    codes = jnp.pad(
+        jnp.where(masked == 1, MASK_ROW, unshuffle),
+        ((0, 0), (0, lanes - IMAGE_PATCHES)),
+        constant_values=-1,
     )
-    embedded = mm("fzh,hg->fzg", retained_pixels, embedding_weight) + kept_pos
-    enc_start = jnp.concatenate(
-        [jnp.broadcast_to(enc_vectors[0], (image_count, 1, ENCODER_WIDTH)), embedded], axis=1
+    codes = jnp.where(jnp.arange(lanes) == IMAGE_PATCHES, CLASS_ROW, codes)[:, None, :]
+    kept = jnp.pad(keep_index, ((0, 0), (0, 128 - KEEP)), constant_values=-1)[:, None, :]
+    weight_rows = jnp.broadcast_to(
+        (image_valid.astype(f32) / patch_total)[:, None, None], (image_count, 1, 128)
     )
-    enc_end, enc_saved = layer_forward(
-        enc_start, enc_in_w, enc_out_w, enc_vectors[1:5], enc_heads, HD_E
+    enc_state = encoder_forward(
+        kept,
+        images,
+        sinusoid_table(ENCODER_WIDTH, GRID_PATCHES, IMAGE_PATCHES, block),
+        enc_in_w,
+        enc_out_w,
+        pixel_w[:PATCH_DIM],
+        bridge_w,
+        enc_vectors,
     )
-    enc_normed, enc_unit, enc_inverse = norm_forward(enc_end, enc_vectors[5], enc_vectors[6])
-    enc_low = enc_normed.astype(bf16)
-    projected = mm("bsd,de->bse", enc_low, bridge_w)
-    placer = (unshuffle[:, :, None] == jnp.arange(KEEP, dtype=jnp.int32)[None, None, :]).astype(f32)
-    mask_column = masked.astype(f32)[:, :, None]
-    filled = (
-        jnp.einsum("bpk,bke->bpe", placer, projected[:, 1:], precision=highest_precision)
-        + mask_column * dec_vectors[0]
-        + sinusoid_table(D_D, GRID_PATCHES, IMAGE_PATCHES)
+    grad_dec_in, grad_dec_out, grad_head, grad_projected, dec_sums = decoder_step(
+        enc_state[0],
+        codes,
+        weight_rows,
+        images,
+        sinusoid_table(D_D, GRID_PATCHES, IMAGE_PATCHES, block),
+        dec_in_w,
+        dec_out_w,
+        pixel_w[PATCH_DIM:],
+        dec_vectors,
     )
-    dec_start = jnp.concatenate([projected[:, :1], filled], axis=1)
-    dec_end, dec_saved = layer_forward(
-        dec_start, dec_in_w, dec_out_w, dec_vectors[1:5], dec_heads, HD_D
+    grad_enc_in, grad_enc_out, grad_bridge, grad_embed, enc_sums = encoder_backward(
+        grad_projected, enc_state[1:], enc_in_w, enc_out_w, bridge_w, enc_vectors
     )
-    dec_normed, dec_unit, dec_inverse = norm_forward(dec_end, dec_vectors[5], dec_vectors[6])
-    dec_low = dec_normed.astype(bf16)
-    predicted = mm("bpe,ec->bpc", dec_low[:, 1:], head_w)
-    pixels = images.astype(f32)
-    pix_centred = pixels - jnp.mean(pixels, axis=-1, keepdims=True)
-    variance = jnp.sum(pix_centred * pix_centred, axis=-1, keepdims=True) / (PATCH_DIM - 1)
-    target = pix_centred * lax.rsqrt(variance + eps_norm)
-    errors = predicted - target
-    patch_weight = patch_flags / patch_total
-    loss_part = jnp.sum(jnp.mean(errors * errors, axis=-1) * patch_weight)
-    grad_pred = (errors * (2.0 / PATCH_DIM) * patch_weight[:, :, None]).astype(bf16)
-    grad_head = mm("bpe,bpc->ec", dec_low[:, 1:], grad_pred)
-    grad_dec_rows = mm("bpc,ec->bpe", grad_pred, head_w)
-    grad_dec_norm = jnp.concatenate([jnp.zeros((image_count, 1, D_D), f32), grad_dec_rows], axis=1)
-    grad_dec_end, dec_gain, dec_shift = norm_backward(
-        grad_dec_norm, dec_unit, dec_inverse, dec_vectors[5]
-    )
-    grad_dec_start, grad_dec_in, grad_dec_out, grad_dec_vectors = layer_backward(
-        grad_dec_end, dec_saved, dec_in_w, dec_out_w, dec_vectors[1:5], dec_heads, HD_D
-    )
-    grad_mask = jnp.sum(grad_dec_start[:, 1:] * mask_column, axis=(0, 1))
-    grad_rest = jnp.einsum(
-        "bpk,bpe->bke", placer, grad_dec_start[:, 1:], precision=highest_precision
-    )
-    grad_projected = jnp.concatenate([grad_dec_start[:, :1], grad_rest], axis=1).astype(bf16)
-    grad_bridge = mm("bsd,bse->de", enc_low, grad_projected)
-    grad_enc_norm = mm("bse,de->bsd", grad_projected, bridge_w)
-    grad_enc_end, enc_gain, enc_shift = norm_backward(
-        grad_enc_norm, enc_unit, enc_inverse, enc_vectors[5]
-    )
-    grad_enc_start, grad_enc_in, grad_enc_out, grad_enc_vectors = layer_backward(
-        grad_enc_end, enc_saved, enc_in_w, enc_out_w, enc_vectors[1:5], enc_heads, HD_E
-    )
-    grad_class = jnp.sum(grad_enc_start[:, 0], axis=0)
-    grad_embed = mm("wmx,wmg->xg", retained_pixels, grad_enc_start[:, 1:].astype(bf16))
-    grad_vectors = jnp.concatenate(
-        [
-            jnp.concatenate(
-                [grad_class[None], grad_enc_vectors, enc_gain[None], enc_shift[None]], axis=0
-            ),
-            jnp.concatenate(
-                [grad_mask[None], grad_dec_vectors, dec_gain[None], dec_shift[None]], axis=0
-            ),
-        ],
-        axis=1,
-    )
-    grad_pixel = jnp.concatenate([grad_embed, grad_head], axis=0)
-
+    grad_pixel = jnp.concatenate([grad_embed, grad_head.astype(bf16)], axis=0)
+    packed = jnp.concatenate([enc_sums, dec_sums], axis=1)
     reduced, loss_value = reduce_all(
-        ([grad_enc_in, grad_enc_out, grad_dec_in, grad_dec_out], grad_pixel, grad_bridge, grad_vectors),
-        loss_part,
+        ([grad_enc_in, grad_enc_out, grad_dec_in, grad_dec_out], grad_pixel, grad_bridge, packed),
         masters,
     )
     decays = (decay_matrix,) * 6 + (0.0,)

time: 628 us -> 552 us (0.88); the launches traced: 618 us -> 551 us
  Pallas kernels: 272 us -> 436 us
  matrix products: 148 us -> 0 us
  other arithmetic: 84.8 us -> 36.2 us
  local copies, waits for them, and re-layouts: 66.5 us -> 34.6 us
    pallas_call x0 -> x3, Pallas kernels: none -> 164 us  [the longest x1 98.5 us: decoder_step(): pl.pallas_call(decoder_kernel, out_shape=outs, scratch_shapes=[pltpu.VMEM...]
    dot_general x46 -> x0, matrix products: 135 us -> none  [the longest x43 131 us: mm(): return jnp.einsum(spec, left, right, preferred_element_type=f32)]
    concatenate x7 -> x2, other arithmetic: 23.1 us -> 3.33 us  [the longest x1 2.71 us: shards(): grad_pixel = jnp.concatenate([grad_embed, grad_head.astype(bf16)], axis=0)]
    sub x2 -> x0, matrix products: 13.6 us -> none  [layer_forward(): shifted = jnp.exp(scores - jnp.max(scores, axis=-1, keepdims=True))]
    convert_element_type x5 -> x0, local copies, waits for them, and re-layouts: 10.9 us -> none  [the longest x1 4.52 us: layer_forward(): mm('bsd,tdc->btsc', input_one, w_input[:, :, :3 * inner]).astype(bf16)]
    transpose x2 -> x0, local copies, waits for them, and re-layouts: 8.71 us -> none  [mm(): return jnp.einsum(spec, left, right, preferred_element_type=f32)]
    unnamed x271 -> x90, local copies, waits for them, and re-layouts: 19.4 us -> 11.3 us
where the time goes in v2:
time: 552 us; the launch traced here: 551 us
  Pallas kernels  436 us (79%)
  blocking collectives  39.4 us (7%)
  other arithmetic  36.2 us (7%)
  local copies, waits for them, and re-layouts  34.6 us (6%)
    pallas_call x1, Pallas kernels, scatter_gradients(): pl.pallas_call(functools.partial(scatter_kernel, shapes, units), out_shap...  142 us
    pallas_call x1, Pallas kernels, gather_weights(): pl.pallas_call(gather_kernel, out_shape=outs, in_specs=[pl.BlockSpec(memo...  130 us
    pallas_call x1, Pallas kernels, decoder_step(): pl.pallas_call(decoder_kernel, out_shape=outs, scratch_shapes=[pltpu.VMEM...  98.5 us
    psum x1, blocking collectives, shards(): totals = lax.psum((squares(masters), squares(updates)), EVERY)  39.4 us
    pallas_call x1, Pallas kernels, encoder_backward(): pl.pallas_call(encoder_backward_kernel, out_shape=outs, scratch_shapes=[p...  34.7 us
    pallas_call x1, Pallas kernels, encoder_forward(): pl.pallas_call(encoder_forward_kernel, out_shape=[jax.ShapeDtypeStruct(sh...  30.7 us
    reduce_sum x9, other arithmetic, squares(): jnp.sum(member * member) / count  17.2 us
    unnamed x90, local copies, waits for them, and re-layouts  11.3 us

profile of v2, /device:TPU:0, one launch (start us, length us, event | category | flops | bytes accessed | tf_op | source)
XLA Modules:
  0.0 551.0 jit_solution(11581289230724723582)
XLA Ops:
  2.0 2.3 constant_dynamic-slice_fusion
  5.6 1.5 dynamic-slice_convert_fusion.refs_0_
  13.3 129.8 %gather_weights.1 = (bf16[4,2,2,2,40,768]{5,4,3,2,1,0:T(8,128)(2,1)}, bf16[2,2,4,2,96,1344]{5,4,3,2,1,0:T(8,128)(2,1)}, bf16[2,2,4,2,120,768]{5,4,3,2,1,0:T(8,12...) custom-call(bf16[40,768]{1,0:T(8,128)(2,1)} %dynamic-slice_convert_f, ...), custom_call_target="tpu_custom_call" | custom-call | bytes 46923776 | tf_op jit(solution)/shard_map/gather_weights/pallas_call | solution.py:194
  143.1 2.4 slice.64.refs_5_
  147.0 30.7 %encoder_forward.1 = (f32[4,64,512]{2,1,0:T(8,128)}, bf16[256,768]{1,0:T(8,128)(2,1)}, f32[256,768]{1,0:T(8,128)}, f32[256,1]{1,0:T(8,128)}, bf16[256,768]{1,0:T...) custom-call(s32[4,1,128]{2,1,0:T(1,128)} %bitcast.122, ...), custom_call_target="tpu_custom_call" | custom-call | tf_op jit(solution)/shard_map/encoder_forward/pallas_call | solution.py:842
  181.1 2.0 slice.68.refs_7_
  183.7 98.5 %decoder_step.1 = (bf16[4,512,896]{2,1,0:T(8,128)(2,1)}, bf16[4,640,512]{2,1,0:T(8,128)(2,1)}, f32[512,768]{1,0:T(8,128)}, bf16[4,64,512]{2,1,0:T(8,128)(2,1)}, f32[8,512]{1,0:T(8,128)}) custom-call(f32[4,64,512]{2,1,0:T(8,128)} %get-tuple-element.68.refs_0_, s32[4,1,256]{2,1,0:T(1,128)} %broadcast_in_dim.30.refs_1_, f32[4,1,128]{2,1,0:T(1,128)} %broadcast_in_dim.31.refs_2_, ...), custom_call_target="tpu_custom_call" | custom-call | tf_op jit(solution)/shard_map/decoder_step/pallas_call | solution.py:793
  283.7 34.7 %encoder_backward.1 = (bf16[4,768,1344]{2,1,0:T(8,128)(2,1)}, bf16[4,960,768]{2,1,0:T(8,128)(2,1)}, bf16[768,512]{1,0:T(8,128)(2,1)}, bf16[768,768]{1,0:T(8,128)(2,1)}, f32[8,768]{1,0:T(8,128)}) custom-call(bf16[4,64,512]{2,1,0:T(8,128)(2,1)} %get-tuple-element.71.refs_0_, bf16[256,768]{1,0:T(8,128)(2,1)} %get-tuple-element.72.refs_1_, ...), custom_call_target="tpu_custom_call" | custom-call | tf_op jit(solution)/shard_map/encoder_backward/pallas_call | solution.py:905
  318.4 2.7 pad_maximum_fusion
  321.8 142.1 %scatter_gradients.1 = (f32[4,40,768]{2,1,0:T(8,128)}, f32[96,1344]{1,0:T(8,128)}, f32[120,768]{1,0:T(8,128)}, f32[4,24,512]{2,1,0:T(8,128)}, f32[64,896]{1,0:T(...) custom-call(bf16[4,2,2,2,40,768]{5,4,3,2,1,0:T(8,128)(2,1)} %bitcast.106, bf16[2,2,4,2,96,1344]{5,4,3,2,1,0:T(8,128)(2,1)} %bitcast.105, ...), custom_call_target="tpu_custom_call" | custom-call | bytes 46481408 | tf_op jit(solution)/shard_map/scatter_gradients/pallas_call | solution.py:421
  465.3 3.1 multiply_reduce_fusion
  468.5 1.8 multiply_reduce_fusion.5
  470.2 1.5 multiply_reduce_fusion.6
  473.2 1.8 multiply_reduce_fusion.3
  475.7 2.8 multiply_reduce_fusion.9
  479.1 2.1 multiply_reduce_fusion.14
  481.9 2.7 stack.73
  484.5 1.7 multiply_reduce_fusion.1
  489.2 2.7 stack.64
  491.9 39.4 %all-reduce.5 = (f32[7]{0:T(128)}, f32[7]{0:T(128)}) all-reduce(f32[7]{0:T(128)S(1)} %stack.73, f32[7]{0:T(128)S(1)} %stack.64), channel_id=1, replica_groups=mesh['dp'=8,'tensor'=4] {'dp','tensor'}, use_global_device_ids=true, to_apply=%region_17.18 | all-reduce | flops 14 | bytes 112 | tf_op jit(solution)/shard_map/psum | solution.py:1094
  532.6 2.4 copy.63
  535.0 1.9 copy.64
  542.0 1.6 multiply_subtract_fusion.2
  546.6 1.7 multiply_subtract_fusion.1
  (123 shorter events, 32.2 us)
Async XLA Ops:
  4.4 5.6 %copy-start.3 = (f32[64,1,896]{2,1,0:T(1,128)S(1)}, f32[64,1,896]{2,1,0:T(1,128)}, u32[]{:S(2)}) copy-start(f32[64,1,896]{2,1,0:T(1,128)} %param.35) | copy-start | bytes 688132
  4.4 6.2 %copy-start.10 = (f32[1,80,512]{2,1,0:T(8,128)S(1)}, f32[1,80,512]{2,1,0:T(8,128)}, u32[]{:S(2)}) copy-start(f32[1,80,512]{2,1,0:T(8,128)} %param.36) | copy-start | bytes 491524
  4.4 6.9 %copy-start.32 = (f32[7,160]{1,0:T(8,128)S(1)}, f32[7,160]{1,0:T(8,128)}, u32[]{:S(2)}) copy-start(f32[7,160]{1,0:T(8,128)} %param.39) | copy-start | bytes 13444
  4.5 6.9 %copy-start.39 = (s32[16]{0:T(128)S(1)}, s32[16]{0:T(128)}, u32[]{:S(2)}) copy-start(s32[16]{0:T(128)} %param.32) | copy-start | bytes 196
  4.5 6.9 %copy-start.35 = (s32[16,196]{1,0:T(8,128)S(1)}, s32[16,196]{1,0:T(8,128)}, u32[]{:S(2)}) copy-start(s32[16,196]{1,0:T(8,128)} %param.31) | copy-start | bytes 37636
  321.8 143.5 %copy-start.19 = (f32[96,1,1344]{2,1,0:T(1,128)S(1)}, f32[96,1,1344]{2,1,0:T(1,128)}, u32[]{:S(2)}) copy-start(f32[96,1,1344]{2,1,0:T(1,128)} %param.40) | copy-start | bytes 1548292
  465.3 4.9 copy-start.26
  465.3 4.9 copy-start.27
  465.3 4.9 copy-start.28
  471.8 7.3 %copy-start.38 = (f32[7,160]{1,0:T(8,128)S(1)}, f32[7,160]{1,0:T(8,128)}, u32[]{:S(2)}) copy-start(f32[7,160]{1,0:T(8,128)} %param.46) | copy-start | bytes 13444
  473.2 72.0 %copy-start.17 = (f32[1,80,512]{2,1,0:T(8,128)}, f32[1,80,512]{2,1,0:T(8,128)S(1)}, u32[]{:S(2)}) copy-start(f32[1,80,512]{2,1,0:T(8,128)S(1)} %get-tuple-element.144) | copy-start | bytes 491524
  475.0 71.6 %copy-start.6 = (f32[160,768]{1,0:T(8,128)}, f32[160,768]{1,0:T(8,128)S(1)}, u32[]{:S(2)}) copy-start(f32[160,768]{1,0:T(8,128)S(1)} %get-tuple-element.142) | copy-start | bytes 1474564
  481.2 68.6 %copy-start.33 = (f32[7,160]{1,0:T(8,128)}, f32[7,160]{1,0:T(8,128)S(1)}, u32[]{:S(2)}) copy-start(f32[7,160]{1,0:T(8,128)S(1)} %get-tuple-element.138) | copy-start | bytes 13444
  531.3 7.0 %copy-start.12 = (f32[64,1,896]{2,0,1:T(8,128)S(1)}, f32[64,1,896]{2,0,1:T(8,128)}, u32[]{:S(2)}) copy-start(f32[64,1,896]{2,0,1:T(8,128)} %get-tuple-element.149) | copy-start | bytes 688132
  535.0 7.0 %copy-start.8 = (f32[1,120,768]{2,1,0:T(8,128)S(1)}, f32[1,120,768]{2,1,0:T(8,128)}, u32[]{:S(2)}) copy-start(f32[1,120,768]{2,1,0:T(8,128)} %get-tuple-element.150) | copy-start | bytes 1105924
  535.0 7.0 %copy-start.9 = (f32[1,120,768]{2,1,0:T(8,128)S(1)}, f32[1,120,768]{2,1,0:T(8,128)}, u32[]{:S(2)}) copy-start(f32[1,120,768]{2,1,0:T(8,128)} %get-tuple-element.151) | copy-start | bytes 1105924
  536.9 6.7 %copy-start.13 = (f32[64,1,896]{2,0,1:T(8,128)S(1)}, f32[64,1,896]{2,0,1:T(8,128)}, u32[]{:S(2)}) copy-start(f32[64,1,896]{2,0,1:T(8,128)} %get-tuple-element.147) | copy-start | bytes 688132
  539.8 5.4 copy-start.18
  539.8 6.8 %copy-start.7 = (f32[160,768]{1,0:T(8,128)S(1)}, f32[160,768]{1,0:T(8,128)}, u32[]{:S(2)}) copy-start(f32[160,768]{1,0:T(8,128)} %get-tuple-element.143) | copy-start | bytes 1474564
  542.0 6.3 %copy-start.14 = (f32[96,512]{1,0:T(8,128)S(1)}, f32[96,512]{1,0:T(8,128)}, u32[]{:S(2)}) copy-start(f32[96,512]{1,0:T(8,128)} %param.38) | copy-start | bytes 589828
  542.0 6.3 %copy-start.15 = (f32[96,512]{1,0:T(8,128)S(1)}, f32[96,512]{1,0:T(8,128)}, u32[]{:S(2)}) copy-start(f32[96,512]{1,0:T(8,128)} %get-tuple-element.140) | copy-start | bytes 589828
  542.0 6.3 %copy-start.16 = (f32[96,512]{1,0:T(8,128)S(1)}, f32[96,512]{1,0:T(8,128)}, u32[]{:S(2)}) copy-start(f32[96,512]{1,0:T(8,128)} %get-tuple-element.141) | copy-start | bytes 589828
  542.0 9.0 %copy-start.1 = (s32[16,49]{1,0:T(8,128)S(1)}, s32[16,49]{1,0:T(8,128)}, u32[]{:S(2)}) copy-start(s32[16,49]{1,0:T(8,128)} %param.29) | copy-start | bytes 9412
  543.6 6.2 %copy-start.34 = (f32[7,160]{1,0:T(8,128)S(1)}, f32[7,160]{1,0:T(8,128)}, u32[]{:S(2)}) copy-start(f32[7,160]{1,0:T(8,128)} %get-tuple-element.139) | copy-start | bytes 13444
  (16 other events, 58.9 us)

commit v3 on v2

--- a/solution.py
+++ b/solution.py
@@ -216,17 +216,93 @@
     ((EIN, 0, 32, 0), (EIN, 32, 16, 1)),
     ((EIN, 48, 16, 0), (EIN, 64, 32, 1)),
 )
+STAT_LANES = {EIN: 0, EOUT: 1, DIN: 2, DOUT: 3, PIX: 4, BRI: 5, VEC: 6}
+
+
+def state_rows(ref, rows):
+    if len(ref.shape) == 2:
+        return ref[rows]
+    return ref[rows, 0, :] if ref.shape[1] == 1 else ref[0, rows, :]
+
+
+def put_rows(ref, rows, values):
+    if len(ref.shape) == 2:
+        ref[rows] = values
+    elif ref.shape[1] == 1:
+        ref[rows, 0, :] = values
+    else:
+        ref[0, rows, :] = values
+
+
+def moments(gradient, moment_one, moment_two, master, decay):
+    next_one = beta_one * moment_one + (1.0 - beta_one) * gradient
+    next_two = beta_two * moment_two + (1.0 - beta_two) * gradient * gradient
+    bias_one = 1.0 - beta_one**step_count
+    bias_two = 1.0 - beta_two**step_count
+    update = next_one / bias_one / (jnp.sqrt(next_two / bias_two) + eps_moment) + decay * master
+    return next_one, next_two, update
+
+
+def state_step(rows):
+    return next(step for step in (32, 40, rows) if rows % step == 0)
+
+
 def scatter_kernel(shapes, units, *refs):
     grads = refs[:7]
-    outs = refs[7:14]
-    refs = refs[14:]
+    masters, firsts, seconds = refs[7:14], refs[14:21], refs[21:28]
+    outs = refs[28:36]
+    refs = refs[36:]
     n = len(units)
     own, one, two, three, four = (refs[k * n : (k + 1) * n] for k in range(5))
     vec_one, vec_two, vec_three, vec_four, vec_sum = refs[5 * n : 5 * n + 5]
-    send, recv, local, vsend, vrecv, tsend, trecv = refs[5 * n + 5 :]
+    stats, stat_one, stat_two, stat_three, stat_four = refs[5 * n + 5 : 5 * n + 10]
+    send, recv, local, vsend, vrecv, tsend, trecv, ssend, srecv = refs[5 * n + 10 :]
     z, x, y, c = place()
     every = slice(None)
     copies = {}
+    stat_row = lax.broadcasted_iota(jnp.int32, (8, 128), 0)
+    stat_lane = lax.broadcasted_iota(jnp.int32, (8, 128), 1)
+
+    def tally(array):
+        if array == VEC:
+            gradient = outs[VEC][:7, : masters[VEC].shape[1]]
+            update = moments(
+                gradient, firsts[VEC][...], seconds[VEC][...], masters[VEC][...], 0.0
+            )[2]
+            squares = [jnp.sum(v * v, axis=0, keepdims=True) for v in (masters[VEC][...], update)]
+        else:
+            flat = (array in SHARED) and outs[array].shape[0] == 4
+            count = outs[array].shape[0] * outs[array].shape[1] if flat else outs[array].shape[0]
+            columns = outs[array].shape[-1]
+            step = outs[array].shape[1] if flat else state_step(count)
+
+            def body(k, carry):
+                rows = pl.ds(pl.multiple_of(k * step, 8), step)
+                gradient = outs[array][k] if flat else outs[array][rows]
+                master = state_rows(masters[array], rows)
+                update = moments(
+                    gradient,
+                    state_rows(firsts[array], rows),
+                    state_rows(seconds[array], rows),
+                    master,
+                    decay_matrix,
+                )[2]
+                return tuple(
+                    total + jnp.sum((v * v).reshape(step // 8, 8, columns), axis=0)
+                    for total, v in zip(carry, (master, update))
+                )
+
+            start = (jnp.zeros((8, columns), f32),) * 2
+            squares = [
+                jnp.sum(v, axis=0, keepdims=True)
+                for v in lax.fori_loop(0, count // step, body, start)
+            ]
+        share = 0.25 if array in SHARED + (VEC,) else 1.0
+        total = stats[...]
+        for row, square in enumerate(squares):
+            value = jnp.sum(square, axis=1, keepdims=True) * share
+            total = total + jnp.where((stat_row == row) & (stat_lane == STAT_LANES[array]), value, 0.0)
+        stats[...] = total
 
     def remote(src, dst, key, send_sem, recv_sem, peer):
         copies[key] = pltpu.make_async_remote_copy(
@@ -320,6 +396,7 @@
                 local.at[number],
             )
         )
+    stats[...] = jnp.zeros_like(stats)
     greet(z, x, y, c)
     steps = units[-1][0] + 1
 
@@ -360,29 +437,59 @@
                 vec_four[z] = vec_sum[...]
                 for m in (1, 2, 3):
                     remote(vec_sum.at[...], vec_four.at[z], ("v", 2 + m), vsend.at[2 + m], vrecv.at[2 + m], device(flip(z, m), x, y, c))
-        if 1 <= tick <= 3:
-            pass
         if tick < 3:
             copies["v", tick].wait()
             vec_sum[...] = vec_sum[...] + vec_dst[tick][...]
         if tick == 4:
             for m in (1, 2, 3):
                 copies["v", 2 + m].wait()
-            outs[6][...] = ((vec_four[0] + vec_four[1]) + (vec_four[2] + vec_four[3]))
-        for array in SHARED:
+            vec_sum[...] = (vec_four[0] + vec_four[1]) + (vec_four[2] + vec_four[3])
+            outs[VEC][...] = vec_sum[z * 2 + x]
+            tally(VEC)
+        for array in range(6):
             last = max(units[number][0] for number in range(n) if units[number][1] == array)
-            if tick == last + 4:
+            if array in SHARED and tick == last + 4:
                 here = y * 2 + c
-                for k, peer in enumerate((device(z, x, y, 1 - c), device(z, x, 1 - y, c), device(z, x, 1 - y, 1 - c))):
+                peers = (
+                    device(z, x, y, 1 - c),
+                    device(z, x, 1 - y, c),
+                    device(z, x, 1 - y, 1 - c),
+                )
+                for k, peer in enumerate(peers):
                     slot = SHARED.index(array) * 3 + k
-                    remote(outs[array].at[here], outs[array].at[here], ("t", slot), tsend.at[slot], trecv.at[slot], peer)
-    for slot in range(6):
-        copies["t", slot].wait()
+                    piece = outs[array].at[here]
+                    remote(piece, piece, ("t", slot), tsend.at[slot], trecv.at[slot], peer)
+            elif array in SHARED and tick == last + 5:
+                for k in range(3):
+                    copies["t", SHARED.index(array) * 3 + k].wait()
+                tally(array)
+            elif array not in SHARED and tick == last + 4:
+                tally(array)
+    stat_peers = (device(z, x, y, 1 - c), device(z, 1 - x, y, c), device(z, x, 1 - y, c))
+    for stage, (held, peer) in enumerate(zip((stat_one, stat_two, stat_three), stat_peers)):
+        remote(stats, held, ("s", stage), ssend.at[stage], srecv.at[stage], peer)
+        copies["s", stage].wait()
+        stats[...] = stats[...] + held[...]
+    stat_four[z] = stats[...]
+    for m in (1, 2, 3):
+        remote(
+            stats,
+            stat_four.at[z],
+            ("s", 2 + m),
+            ssend.at[2 + m],
+            srecv.at[2 + m],
+            device(flip(z, m), x, y, c),
+        )
+    for m in (1, 2, 3):
+        copies["s", 2 + m].wait()
+    norms = jnp.sqrt((stat_four[0] + stat_four[1]) + (stat_four[2] + stat_four[3]))
+    loss = vec_sum[7, 7:8, 128:256][:, 31:32]
+    outs[7][...] = jnp.where(stat_row == 2, loss, norms)
     for number in range(n):
         copies[number, 0].wait_send()
 
 
-def scatter_gradients(grads):
+def scatter_gradients(grads, masters, firsts, seconds):
     units = [(at,) + unit for at, step in enumerate(SCATTER_STEPS) for unit in step]
     n = len(units)
     shapes = [grad.shape for grad in grads]
@@ -393,7 +500,8 @@
             outs.append(jax.ShapeDtypeStruct((4, rows, columns), f32))
         else:
             outs.append(jax.ShapeDtypeStruct((rows, columns), f32))
-    outs.append(jax.ShapeDtypeStruct(grads[6].shape, f32))
+    outs.append(jax.ShapeDtypeStruct(grads[6].shape[1:], f32))
+    outs.append(jax.ShapeDtypeStruct((8, 128), f32))
     scratch = []
     for stage in range(5):
         for at, array, first, size, turn in units:
@@ -408,10 +516,13 @@
             scratch.append(pltpu.VMEM(lead + (size, shapes[array][5]), bf16))
     vec = grads[6].shape
     scratch += [pltpu.VMEM(vec, f32)] * 3 + [pltpu.VMEM((4,) + vec, f32), pltpu.VMEM(vec, f32)]
+    scratch += [pltpu.VMEM((8, 128), f32)] * 4 + [pltpu.VMEM((4, 8, 128), f32)]
     scratch += [
         pltpu.SemaphoreType.DMA((n, 6)),
         pltpu.SemaphoreType.DMA((n, 6)),
         pltpu.SemaphoreType.DMA((n,)),
+        pltpu.SemaphoreType.DMA((6,)),
+        pltpu.SemaphoreType.DMA((6,)),
         pltpu.SemaphoreType.DMA((6,)),
         pltpu.SemaphoreType.DMA((6,)),
         pltpu.SemaphoreType.DMA((6,)),
@@ -421,15 +532,67 @@
     return pl.pallas_call(
         functools.partial(scatter_kernel, shapes, units),
         out_shape=outs,
-        in_specs=[pl.BlockSpec(memory_space=pl.ANY)] * 6 + [pl.BlockSpec(memory_space=pltpu.VMEM)],
-        out_specs=[pl.BlockSpec(memory_space=pltpu.VMEM)] * 7,
+        in_specs=[pl.BlockSpec(memory_space=pl.ANY)] * 6
+        + [pl.BlockSpec(memory_space=pltpu.VMEM)] * 22,
+        out_specs=[pl.BlockSpec(memory_space=pltpu.VMEM)] * 8,
         scratch_shapes=scratch,
         compiler_params=pltpu.CompilerParams(
             collective_id=1, has_side_effects=True, vmem_limit_bytes=60 * 1024 * 1024
         ),
         cost_estimate=pl.CostEstimate(flops=0, bytes_accessed=2 * total, transcendentals=0),
         name="scatter_gradients",
-    )(*grads)
+    )(*grads, *masters, *firsts, *seconds)
+
+
+def apply_kernel(*refs):
+    grads, masters, firsts, seconds = (refs[7 * k : 7 * k + 7] for k in range(4))
+    stats = refs[28]
+    next_firsts, next_seconds, news = (refs[29 + 7 * k : 36 + 7 * k] for k in range(3))
+    loss, pairs = refs[50:]
+    for array in range(7):
+        lane = STAT_LANES[array]
+        norms = [stats[row : row + 1, :][:, lane : lane + 1] for row in range(2)]
+        ratio = learn_rate * norms[0] / norms[1]
+        count = masters[array].shape[0]
+        if len(masters[array].shape) == 3:
+            count = count * masters[array].shape[1]
+        decay = 0.0 if array == VEC else decay_matrix
+
+        def body(rows, array=array, ratio=ratio, decay=decay):
+            if array == VEC:
+                gradient = grads[VEC][:7, : masters[VEC].shape[1]]
+            else:
+                gradient = grads[array][rows]
+            master = state_rows(masters[array], rows)
+            next_one, next_two, update = moments(
+                gradient,
+                state_rows(firsts[array], rows),
+                state_rows(seconds[array], rows),
+                master,
+                decay,
+            )
+            put_rows(next_firsts[array], rows, next_one)
+            put_rows(next_seconds[array], rows, next_two)
+            put_rows(news[array], rows, master - ratio * update)
+
+        if array == VEC:
+            body(slice(None))
+        else:
+            row_loop(count, state_step(count), body)
+    pairs[...] = stats[:2, :][:, :7]
+    loss[...] = stats[2:3, :][:, :1]
+
+
+def apply_update(reduced, masters, firsts, seconds, stats):
+    shapes = [jax.ShapeDtypeStruct(master.shape, f32) for master in masters]
+    results = pl.pallas_call(
+        apply_kernel,
+        out_shape=shapes * 3
+        + [jax.ShapeDtypeStruct((1, 1), f32), jax.ShapeDtypeStruct((2, 7), f32)],
+        compiler_params=pltpu.CompilerParams(vmem_limit_bytes=48 * 1024 * 1024),
+        name="apply_update",
+    )(*reduced, *masters, *firsts, *seconds, stats)
+    return results[:7], results[7:14], results[14:21], results[21].reshape(()), results[22]
 
 
 def sinusoid_table(feature_width, grid_side, patch_count, padded):
@@ -965,40 +1128,66 @@
     return grouped, pixel_w, bridge_w, vectors_all, lax.psum(counted, "dp")
 
 
-def reduce_all(gradients, masters):
+def ring_finish(gradients, masters, firsts, seconds):
+    grouped, grad_pixel, grad_bridge, packed = gradients
     tensor_count = lax.axis_size("tensor")
     columns = masters[6].shape[1]
-    dp_at = lax.axis_index("dp")
+    order = (4, 0, 1, 5, 2, 3, 6)
+    sources = (grad_pixel, grouped[0], grouped[1], grad_bridge, grouped[2], grouped[3])
+    operands = []
+    for array, source in enumerate(sources):
+        master = masters[order[array]]
+        rows, wide = master.size // master.shape[-1], master.shape[-1]
+        if array in SHARED:
+            rows = rows // tensor_count
+        operands.append(source.reshape(whole_shape(array, (rows, wide))))
+    packed = packed.reshape(8, -1, columns).transpose(1, 0, 2)
+    operands.append(jnp.pad(packed, ((0, 0), (0, 0), (0, 256 - columns))))
+    states = [[members[k] for k in order] for members in (masters, firsts, seconds)]
+    *sums, stats = scatter_gradients(operands, *states)
+    for array in SHARED:
+        sums[array] = sums[array].reshape(-1, sums[array].shape[-1])
+    *results, loss_value, pairs = apply_update(sums, *states, stats)
+    place_of = {k: at for at, k in enumerate(order)}
+    results = [[members[place_of[k]] for k in range(7)] for members in results]
+    return (loss_value, pairs, *results[0], *results[1], *results[2])
+
+
+def plain_finish(gradients, masters, firsts, seconds):
     grouped, grad_pixel, grad_bridge, packed = gradients
-    if ringed(tensor_count):
-        shapes = {
-            EIN: masters[0].reshape(-1, masters[0].shape[-1]).shape,
-            EOUT: masters[1].reshape(-1, masters[1].shape[-1]).shape,
-            DIN: masters[2].reshape(-1, masters[2].shape[-1]).shape,
-            DOUT: masters[3].reshape(-1, masters[3].shape[-1]).shape,
-            PIX: (masters[4].shape[0] // tensor_count, masters[4].shape[1]),
-            BRI: (masters[5].shape[0] // tensor_count, masters[5].shape[1]),
-        }
-        sources = {PIX: grad_pixel, EIN: grouped[0], EOUT: grouped[1], BRI: grad_bridge, DIN: grouped[2], DOUT: grouped[3]}
-        operands = [
-            sources[array].reshape(whole_shape(array, shapes[array]))
-            for array in range(6)
-        ]
-        sums = scatter_gradients(operands + [packed])
-        reduced = [sums[EIN], sums[EOUT], sums[DIN], sums[DOUT], sums[PIX], sums[BRI]]
-        vector_sum = sums[VEC]
-    else:
-
-        def scatter_shared(gradient):
-            part = lax.psum_scatter(gradient.astype(f32), EVERY, scatter_dimension=0, tiled=True)
-            return lax.all_gather(part, "tensor", axis=0, tiled=True)
-
-        reduced = [scatter_grouped(gradient) for gradient in grouped]
-        reduced += [scatter_shared(grad_pixel), scatter_shared(grad_bridge)]
-        vector_sum = lax.psum(packed, EVERY)
-    own = lax.dynamic_slice_in_dim(vector_sum[:7], dp_at * columns, columns, axis=1)
+    tensor_count = lax.axis_size("tensor")
+    columns = masters[6].shape[1]
+
+    def scatter_shared(gradient):
+        part = lax.psum_scatter(gradient.astype(f32), EVERY, scatter_dimension=0, tiled=True)
+        return lax.all_gather(part, "tensor", axis=0, tiled=True)
+
+    reduced = [scatter_grouped(gradient) for gradient in grouped]
+    reduced += [scatter_shared(grad_pixel), scatter_shared(grad_bridge)]
+    vector_sum = lax.psum(packed, EVERY)
+    own = lax.dynamic_slice_in_dim(
+        vector_sum[:7], lax.axis_index("dp") * columns, columns, axis=1
+    )
     reduced = [gradient.reshape(master.shape) for gradient, master in zip(reduced + [own], masters)]
-    return reduced, vector_sum[7, -1]
+    decays = (decay_matrix,) * 6 + (0.0,)
+    share_counts = (1.0,) * 4 + (float(tensor_count),) * 3
+    steps = [moments(*member) for member in zip(reduced, firsts, seconds, masters, decays)]
+    new_firsts, new_seconds, updates = zip(*steps)
+
+    def squares(members):
+        return jnp.stack(
+            [jnp.sum(member * member) / count for member, count in zip(members, share_counts)]
+        )
+
+    weight_norm, update_norm = map(
+        jnp.sqrt, lax.psum((squares(masters), squares(updates)), EVERY)
+    )
+    ratio = learn_rate * weight_norm / update_norm
+    news = [
+        master - ratio[position] * update
+        for position, (master, update) in enumerate(zip(masters, updates))
+    ]
+    return (vector_sum[7, -1], jnp.stack([weight_norm, update_norm]), *new_firsts, *new_seconds, *news)
 
 
 def shards(
@@ -1065,42 +1254,12 @@
     )
     grad_pixel = jnp.concatenate([grad_embed, grad_head.astype(bf16)], axis=0)
     packed = jnp.concatenate([enc_sums, dec_sums], axis=1)
-    reduced, loss_value = reduce_all(
+    finish = ring_finish if ringed(tensor_count) else plain_finish
+    return finish(
         ([grad_enc_in, grad_enc_out, grad_dec_in, grad_dec_out], grad_pixel, grad_bridge, packed),
         masters,
-    )
-    decays = (decay_matrix,) * 6 + (0.0,)
-    share_counts = (1.0,) * 4 + (float(tensor_count),) * 3
-    bias_one = 1.0 - beta_one**step_count
-    bias_two = 1.0 - beta_two**step_count
-    new_firsts, new_seconds, updates = ([], [], [])
-    for gradient, master, moment_one, moment_two, decay_value in zip(
-        reduced, masters, firsts, seconds, decays
-    ):
-        next_one = beta_one * moment_one + (1.0 - beta_one) * gradient
-        next_two = beta_two * moment_two + (1.0 - beta_two) * gradient * gradient
-        new_firsts.append(next_one)
-        new_seconds.append(next_two)
-        updates.append(
-            next_one / bias_one / (jnp.sqrt(next_two / bias_two) + eps_moment)
-            + decay_value * master
-        )
-
-    def squares(members):
-        return jnp.stack(
-            [jnp.sum(member * member) / count for member, count in zip(members, share_counts)]
-        )
-
-    totals = lax.psum((squares(masters), squares(updates)), EVERY)
-    weight_norm = jnp.sqrt(totals[0])
-    update_norm = jnp.sqrt(totals[1])
-    step_ratio = learn_rate * weight_norm / update_norm
-    news = [
-        master - step_ratio[position] * update
-        for position, (master, update) in enumerate(zip(masters, updates))
-    ]
-    return tuple(
-        [loss_value, jnp.stack([weight_norm, update_norm])] + new_firsts + new_seconds + news
+        firsts,
+        seconds,
     )
 
 

time: 552 us -> 495 us (0.90)
  blocking collectives: 39.4 us -> 0 us
  other arithmetic: 36.2 us -> 8.28 us
  Pallas kernels: 436 us -> 458 us
  local copies, waits for them, and re-layouts: 34.6 us -> 27.3 us
    psum x1 -> x0, blocking collectives: 39.4 us -> none  [shards(): totals = lax.psum((squares(masters), squares(updates)), EVERY)]
    reduce_sum x9 -> x0, other arithmetic: 17.2 us -> none  [squares(): jnp.sum(member * member) / count]
    pallas_call x1, Pallas kernels: 142 us -> 156 us  [scatter_gradients(): pl.pallas_call(functools.partial(scatter_kernel, shapes, units), out_shap...]
    sub x7 -> x0, other arithmetic: 8.83 us -> none  [shards(): master - step_ratio[position] * update]
    pallas_call x0 -> x1, Pallas kernels: none -> 7.84 us  [apply_update(): pl.pallas_call(apply_kernel, out_shape=shapes * 3 + [jax.ShapeDtypeStruct...]
    unnamed x90 -> x76, local copies, waits for them, and re-layouts: 11.3 us -> 10.4 us
where the time goes in v3:
time: 495 us; the launch traced here: 494 us
  Pallas kernels  458 us (93%)
  local copies, waits for them, and re-layouts  27.3 us (6%)
  other arithmetic  8.28 us (2%)
    pallas_call x1, Pallas kernels, scatter_gradients(): pl.pallas_call(functools.partial(scatter_kernel, shapes, units), out_shap...  156 us
    pallas_call x1, Pallas kernels, gather_weights(): pl.pallas_call(gather_kernel, out_shape=outs, in_specs=[pl.BlockSpec(memo...  130 us
    pallas_call x1, Pallas kernels, decoder_step(): pl.pallas_call(decoder_kernel, out_shape=outs, scratch_shapes=[pltpu.VMEM...  98.5 us
    pallas_call x1, Pallas kernels, encoder_backward(): pl.pallas_call(encoder_backward_kernel, out_shape=outs, scratch_shapes=[p...  34.8 us
    pallas_call x1, Pallas kernels, encoder_forward(): pl.pallas_call(encoder_forward_kernel, out_shape=[jax.ShapeDtypeStruct(sh...  30.7 us
    unnamed x76, local copies, waits for them, and re-layouts  10.4 us

profile of v3, /device:TPU:0, one launch (start us, length us, event | category | flops | bytes accessed | tf_op | source)
XLA Modules:
  0.0 494.4 jit_solution(8176598751569433769)
XLA Ops:
  2.0 2.3 constant_dynamic-slice_fusion
  4.5 1.2 pad.25.refs_1_.refs_3_
  5.7 1.5 dynamic-slice_convert_fusion.refs_0_
  7.2 0.7 copy.70
  8.6 1.4 dynamic-slice_convert_fusion.1.refs_3_
  12.1 1.2 concatenate.9.refs_6_
  13.3 129.8 %gather_weights.1 = (bf16[4,2,2,2,40,768]{5,4,3,2,1,0:T(8,128)(2,1)}, bf16[2,2,4,2,96,1344]{5,4,3,2,1,0:T(8,128)(2,1)}, bf16[2,2,4,2,120,768]{5,4,3,2,1,0:T(8,12...) custom-call(bf16[40,768]{1,0:T(8,128)(2,1)} %dynamic-slice_convert_f, ...), custom_call_target="tpu_custom_call" | custom-call | bytes 46923776 | tf_op jit(solution)/shard_map/gather_weights/pallas_call | solution.py:194
  143.1 2.4 slice.28.refs_5_
  145.5 0.8 slice.22
  147.1 30.7 %encoder_forward.1 = (f32[4,64,512]{2,1,0:T(8,128)}, bf16[256,768]{1,0:T(8,128)(2,1)}, f32[256,768]{1,0:T(8,128)}, f32[256,1]{1,0:T(8,128)}, bf16[256,768]{1,0:T...) custom-call(s32[4,1,128]{2,1,0:T(1,128)} %bitcast.58, ...), custom_call_target="tpu_custom_call" | custom-call | tf_op jit(solution)/shard_map/encoder_forward/pallas_call | solution.py:1005
  181.1 2.1 slice.32.refs_7_
  183.7 98.5 %decoder_step.1 = (bf16[4,512,896]{2,1,0:T(8,128)(2,1)}, bf16[4,640,512]{2,1,0:T(8,128)(2,1)}, f32[512,768]{1,0:T(8,128)}, bf16[4,64,512]{2,1,0:T(8,128)(2,1)}, f32[8,512]{1,0:T(8,128)}) custom-call(f32[4,64,512]{2,1,0:T(8,128)} %get-tuple-element.92.refs_0_, s32[4,1,256]{2,1,0:T(1,128)} %broadcast_in_dim.30.refs_1_, f32[4,1,128]{2,1,0:T(1,128)} %broadcast_in_dim.31.refs_2_, ...), custom_call_target="tpu_custom_call" | custom-call | tf_op jit(solution)/shard_map/decoder_step/pallas_call | solution.py:956
  282.3 1.5 convert_element_type.62
  283.7 34.8 %encoder_backward.1 = (bf16[4,768,1344]{2,1,0:T(8,128)(2,1)}, bf16[4,960,768]{2,1,0:T(8,128)(2,1)}, bf16[768,512]{1,0:T(8,128)(2,1)}, bf16[768,768]{1,0:T(8,128)(2,1)}, f32[8,768]{1,0:T(8,128)}) custom-call(bf16[4,64,512]{2,1,0:T(8,128)(2,1)} %get-tuple-element.95.refs_0_, bf16[256,768]{1,0:T(8,128)(2,1)} %get-tuple-element.96.refs_1_, ...), custom_call_target="tpu_custom_call" | custom-call | tf_op jit(solution)/shard_map/encoder_backward/pallas_call | solution.py:1068
  318.6 2.7 pad_maximum_fusion
  322.2 155.9 %scatter_gradients.1 = (f32[4,40,768]{2,1,0:T(8,128)}, f32[96,1344]{1,0:T(8,128)}, f32[120,768]{1,0:T(8,128)}, f32[4,24,512]{2,1,0:T(8,128)}, f32[64,896]{1,0:T(...) custom-call(bf16[4,2,2,2,40,768]{5,4,3,2,1,0:T(8,128)(2,1)} %bitcast.41, ...), custom_call_target="tpu_custom_call" | custom-call | bytes 46530560 | tf_op jit(solution)/shard_map/scatter_gradients/pallas_call | solution.py:532
  478.4 0.9 copy-done.18
  479.3 0.9 copy-done.19
  480.2 1.0 copy-done.20
  481.2 1.0 copy-done.21
  482.2 0.9 copy-done.22
  483.2 0.9 copy-done.23
  484.1 0.9 copy-done.24
  486.4 7.8 %apply_update.1 = (f32[160,768]{1,0:T(8,128)}, f32[96,1,1344]{2,1,0:T(1,128)}, f32[1,120,768]{2,1,0:T(8,128)}, f32[96,512]{1,0:T(8,128)}, f32[64,1,896]{2,1,0:T(...) custom-call(f32[160,768]{1,0:T(8,128)S(1)} %bitcast.34, ...), custom_call_target="tpu_custom_call" | custom-call | tf_op jit(solution)/shard_map/apply_update/pallas_call | solution.py:588
  (90 shorter events, 11.0 us)
Async XLA Ops:
  4.3 2.9 copy-start.31
  4.3 3.7 copy-start.2
  4.4 5.6 %copy-start.5 = (f32[64,1,896]{2,1,0:T(1,128)S(1)}, f32[64,1,896]{2,1,0:T(1,128)}, u32[]{:S(2)}) copy-start(f32[64,1,896]{2,1,0:T(1,128)} %refs_11_.3) | copy-start | bytes 688132
  4.4 6.3 %copy-start.11 = (f32[1,80,512]{2,1,0:T(8,128)S(1)}, f32[1,80,512]{2,1,0:T(8,128)}, u32[]{:S(2)}) copy-start(f32[1,80,512]{2,1,0:T(8,128)} %refs_12_.3) | copy-start | bytes 491524
  4.4 6.9 %copy-start.25 = (f32[7,160]{1,0:T(8,128)S(1)}, f32[7,160]{1,0:T(8,128)}, u32[]{:S(2)}) copy-start(f32[7,160]{1,0:T(8,128)} %refs_13_.3) | copy-start | bytes 13444
  4.5 6.9 %copy-start.35 = (s32[16]{0:T(128)S(1)}, s32[16]{0:T(128)}, u32[]{:S(2)}) copy-start(s32[16]{0:T(128)} %param.32) | copy-start | bytes 196
  4.5 6.9 %copy-start.32 = (s32[16,196]{1,0:T(8,128)S(1)}, s32[16,196]{1,0:T(8,128)}, u32[]{:S(2)}) copy-start(s32[16,196]{1,0:T(8,128)} %param.31) | copy-start | bytes 37636
  322.1 156.1 %copy-start.3 = (f32[1,120,768]{2,1,0:T(8,128)S(1)}, f32[1,120,768]{2,1,0:T(8,128)}, u32[]{:S(2)}) copy-start(f32[1,120,768]{2,1,0:T(8,128)} %refs_9_.3) | copy-start | bytes 1105924
  322.1 156.1 %copy-start.4 = (f32[160,768]{1,0:T(8,128)S(1)}, f32[160,768]{1,0:T(8,128)}, u32[]{:S(2)}) copy-start(f32[160,768]{1,0:T(8,128)} %refs_7_.3) | copy-start | bytes 1474564
  322.1 156.1 %copy-start.6 = (f32[64,1,896]{2,1,0:T(1,128)S(1)}, f32[64,1,896]{2,1,0:T(1,128)}, u32[]{:S(2)}) copy-start(f32[64,1,896]{2,1,0:T(1,128)} %refs_11_.3) | copy-start | bytes 688132
  322.1 156.1 %copy-start.7 = (f32[160,768]{1,0:T(8,128)S(1)}, f32[160,768]{1,0:T(8,128)}, u32[]{:S(2)}) copy-start(f32[160,768]{1,0:T(8,128)} %refs_14_.3) | copy-start | bytes 1474564
  322.1 156.1 %copy-start.8 = (f32[160,768]{1,0:T(8,128)S(1)}, f32[160,768]{1,0:T(8,128)}, u32[]{:S(2)}) copy-start(f32[160,768]{1,0:T(8,128)} %refs_21_.3) | copy-start | bytes 1474564
  322.1 156.1 %copy-start.9 = (f32[1,120,768]{2,1,0:T(8,128)S(1)}, f32[1,120,768]{2,1,0:T(8,128)}, u32[]{:S(2)}) copy-start(f32[1,120,768]{2,1,0:T(8,128)} %refs_16_.3) | copy-start | bytes 1105924
  322.1 156.1 %copy-start.10 = (f32[1,120,768]{2,1,0:T(8,128)S(1)}, f32[1,120,768]{2,1,0:T(8,128)}, u32[]{:S(2)}) copy-start(f32[1,120,768]{2,1,0:T(8,128)} %refs_23_.3) | copy-start | bytes 1105924
  322.1 156.1 %copy-start.12 = (f32[1,80,512]{2,1,0:T(8,128)S(1)}, f32[1,80,512]{2,1,0:T(8,128)}, u32[]{:S(2)}) copy-start(f32[1,80,512]{2,1,0:T(8,128)} %refs_12_.3) | copy-start | bytes 491524
  322.1 156.1 %copy-start.13 = (f32[64,1,896]{2,1,0:T(1,128)S(1)}, f32[64,1,896]{2,1,0:T(1,128)}, u32[]{:S(2)}) copy-start(f32[64,1,896]{2,1,0:T(1,128)} %refs_18_.3) | copy-start | bytes 688132
  322.2 156.1 %copy-start.14 = (f32[64,1,896]{2,1,0:T(1,128)S(1)}, f32[64,1,896]{2,1,0:T(1,128)}, u32[]{:S(2)}) copy-start(f32[64,1,896]{2,1,0:T(1,128)} %refs_25_.3) | copy-start | bytes 688132
  322.2 156.1 %copy-start.15 = (f32[96,512]{1,0:T(8,128)S(1)}, f32[96,512]{1,0:T(8,128)}, u32[]{:S(2)}) copy-start(f32[96,512]{1,0:T(8,128)} %refs_10_.3) | copy-start | bytes 589828
  322.2 156.1 %copy-start.16 = (f32[96,512]{1,0:T(8,128)S(1)}, f32[96,512]{1,0:T(8,128)}, u32[]{:S(2)}) copy-start(f32[96,512]{1,0:T(8,128)} %refs_17_.3) | copy-start | bytes 589828
  322.2 156.1 %copy-start.17 = (f32[96,512]{1,0:T(8,128)S(1)}, f32[96,512]{1,0:T(8,128)}, u32[]{:S(2)}) copy-start(f32[96,512]{1,0:T(8,128)} %refs_24_.3) | copy-start | bytes 589828
  322.2 156.1 %copy-start.26 = (f32[7,160]{1,0:T(8,128)S(1)}, f32[7,160]{1,0:T(8,128)}, u32[]{:S(2)}) copy-start(f32[7,160]{1,0:T(8,128)} %refs_13_.3) | copy-start | bytes 13444
  322.2 156.1 %copy-start.27 = (f32[7,160]{1,0:T(8,128)S(1)}, f32[7,160]{1,0:T(8,128)}, u32[]{:S(2)}) copy-start(f32[7,160]{1,0:T(8,128)} %refs_20_.3) | copy-start | bytes 13444
  322.2 156.1 %copy-start.28 = (f32[7,160]{1,0:T(8,128)S(1)}, f32[7,160]{1,0:T(8,128)}, u32[]{:S(2)}) copy-start(f32[7,160]{1,0:T(8,128)} %refs_27_.3) | copy-start | bytes 13444
  478.2 16.0 %copy-start.1 = (s32[16,49]{1,0:T(8,128)S(1)}, s32[16,49]{1,0:T(8,128)}, u32[]{:S(2)}) copy-start(s32[16,49]{1,0:T(8,128)} %param.29) | copy-start | bytes 9412
  (12 other events, 14.2 us)

commit v4 on v3

--- a/solution.py
+++ b/solution.py
@@ -93,17 +93,14 @@
     ((EIN, 0, 32, 0), (EIN, 32, 16, 1)),
     ((EIN, 48, 16, 0), (EIN, 64, 32, 1)),
     ((EOUT, 0, 32, 0), (EOUT, 32, 32, 1)),
-    ((EOUT, 64, 32, 0), (EOUT, 96, 24, 1)),
-    ((BRI, 0, 8, 0), (BRI, 8, 16, 1), (DIN, 0, 32, 0), (DIN, 32, 32, 1)),
+    ((EOUT, 64, 32, 0), (EOUT, 96, 24, 1), (BRI, 0, 16, 1), (BRI, 16, 8, 0)),
+    ((DIN, 0, 32, 0), (DIN, 32, 32, 1)),
     ((DOUT, 0, 48, 0), (DOUT, 48, 32, 1)),
 )
 
 
-def gather_kernel(*refs):
+def gather_ticks(parts, outs, send, recv, local):
     count = 7
-    parts = refs[:count]
-    outs = refs[count : 2 * count]
-    send, recv, local = refs[2 * count :]
     z, x, y, c = place()
     units = []
     for at, step in enumerate(GATHER_STEPS):
@@ -179,32 +176,12 @@
         for number, unit in enumerate(units):
             if unit[0] == tick - 4:
                 copies[number, 5].wait_recv()
+        if tick < steps + 3:
+            yield tick
     for key in copies:
         copies[key].wait_send()
-
-
-def gather_weights(parts):
-    count = 7
-    units = sum(len(step) for step in GATHER_STEPS)
-    outs = [
-        jax.ShapeDtypeStruct(whole_shape(array, part.shape), part.dtype)
-        for array, part in enumerate(parts)
-    ]
-    total = sum(int(part.size) * 32 * part.dtype.itemsize for part in parts)
-    return pl.pallas_call(
-        gather_kernel,
-        out_shape=outs,
-        in_specs=[pl.BlockSpec(memory_space=pltpu.VMEM)] * count,
-        out_specs=[pl.BlockSpec(memory_space=pl.ANY)] * count,
-        scratch_shapes=[
-            pltpu.SemaphoreType.DMA((units, 6)),
-            pltpu.SemaphoreType.DMA((units, 6)),
-            pltpu.SemaphoreType.DMA((count,)),
-        ],
-        compiler_params=pltpu.CompilerParams(collective_id=0, has_side_effects=True),
-        cost_estimate=pl.CostEstimate(flops=0, bytes_accessed=2 * total, transcendentals=0),
-        name="gather_weights",
-    )(*parts)
+    yield steps + 3
+    yield None
 
 
 SCATTER_STEPS = (
@@ -608,8 +585,8 @@
 
 
 GROUPS = 4
-ENC = dict(step=128, images=4, block=64, tokens=50, width=768, heads=3, head=64, hidden=768, spans=1)
-DEC = dict(step=208, images=4, block=208, tokens=197, width=512, heads=4, head=32, hidden=512, spans=4)
+ENC = dict(step=128, first=0, images=4, block=64, tokens=50, width=768, heads=3, head=64, hidden=768, spans=1)
+DEC = dict(step=208, first=768, images=4, block=208, tokens=197, width=512, heads=4, head=32, hidden=512, spans=4)
 CLASS_ROW = 49
 MASK_ROW = 50
 
@@ -678,19 +655,26 @@
     row_loop(incoming.shape[0], step, body)
 
 
-def attend_mask(dims):
-    size = dims["block"] * dims["images"] // dims["spans"]
-    key = lax.broadcasted_iota(jnp.int32, (size, size), 1)
+def lane_chunks(size):
+    return [slice(at, min(at + 128, size)) for at in range(0, size, 128)]
+
+
+def attend_mask(dims, scores, start):
     if dims["spans"] == 1:
-        query = lax.broadcasted_iota(jnp.int32, (size, size), 0)
-        return ((key // dims["block"]) == (query // dims["block"])) & (
+        key = lax.broadcasted_iota(jnp.int32, scores.shape, 0)
+        query = lax.broadcasted_iota(jnp.int32, scores.shape, 1) + start
+        allowed = ((key // dims["block"]) == (query // dims["block"])) & (
             (key % dims["block"]) < dims["tokens"]
         )
-    return key < dims["tokens"]
+        return jnp.where(allowed, scores, -1e30)
+    first = dims["tokens"] // 16 * 16
+    tail = scores[first:]
+    key = lax.broadcasted_iota(jnp.int32, tail.shape, 0) + first
+    return jnp.concatenate([scores[:first], jnp.where(key < dims["tokens"], tail, -1e30)], axis=0)
 
 
 def layer_forward_rows(dims, stream, w_in, w_out, vectors, saved):
-    unit_one, inv_one, low_one, qkv, probs, mixed, unit_two, inv_two, low_two, active, slope = saved
+    unit_one, inv_one, low_one, qkv, probs, mixed, unit_two, inv_two, low_two, active, slope, work, low_work, low_more = saved
     count, width = stream.shape
     inner = dims["heads"] * dims["head"]
     span = count // dims["spans"]
@@ -713,19 +697,24 @@
         b = k % dims["spans"]
         rows = pl.ds(pl.multiple_of(b * span, span), span)
         triple = qkv[t, rows]
-        allowed = attend_mask(dims)
-        results = []
-        for head in range(dims["heads"]):
-            q, key, v = (
-                triple[:, part * inner + head * dims["head"] : part * inner + (head + 1) * dims["head"]]
-                for part in range(3)
-            )
-            scores = jnp.where(allowed, dot_nt(q, key) * scale, -1e30)
-            shifted = jnp.exp(scores - jnp.max(scores, axis=-1, keepdims=True))
-            share = shifted / jnp.sum(shifted, axis=-1, keepdims=True)
-            probs[k * dims["heads"] + head] = share
-            results.append(dot(share.astype(bf16), v))
-        mixed[t, rows] = jnp.concatenate(results, axis=1).astype(bf16)
+        query_t = triple[:, :inner].T
+        value_t = triple[:, 2 * inner :].T
+        heads = range(dims["heads"])
+        lanes = [slice(head * dims["head"], (head + 1) * dims["head"]) for head in heads]
+        for head in heads:
+            key = triple[:, inner : 2 * inner][:, lanes[head]]
+            work[head] = dot(key, query_t[lanes[head]])
+        for head in heads:
+            for columns in lane_chunks(span):
+                scores = attend_mask(dims, work[head, :, columns] * scale, columns.start)
+                shifted = jnp.exp(scores - jnp.max(scores, axis=0, keepdims=True))
+                share = shifted * (1.0 / jnp.sum(shifted, axis=0, keepdims=True))
+                probs[k * dims["heads"] + head, :, columns] = share
+                low_work[head, :, columns] = share.astype(bf16)
+        results = [dot(value_t[lanes[head]], low_work[head]) for head in heads]
+        mixed[t, rows] = jnp.concatenate(results, axis=0).T.astype(bf16)
+
+    yield "attended"
 
     @pl.loop(0, GROUPS)
     def _(t):
@@ -738,15 +727,10 @@
 
     norm_rows(stream, vectors[3:4, :], vectors[4:5, :], unit_two, inv_two, low_two, dims["step"])
 
-    @pl.loop(0, GROUPS)
-    def _(t):
+    def feed(t):
         up = w_in[t, :, 3 * inner :] if inner % 128 == 0 else w_in[t][:, 3 * inner :]
         down = w_out[t, inner:]
-
-        def body(rows):
-            slope[t, rows] = dot(low_two[rows], up)
-
-        body(slice(None))
+        slope[t] = dot(low_two[...], up)
 
         def bend(rows):
             hidden = slope[t, rows]
@@ -757,15 +741,17 @@
             )
 
         row_loop(count, 32, bend)
-
-        def body_two(rows):
-            stream[rows] = stream[rows] + dot(active[t, rows], down)
-
-        body_two(slice(None))
+        stream[...] = stream[...] + dot(active[t], down)
+
+    half = GROUPS // 2 if dims["spans"] == 1 else GROUPS
+    pl.loop(0, half)(feed)
+    if half < GROUPS:
+        yield "halfway"
+        pl.loop(half, GROUPS)(feed)
 
 
 def layer_backward_rows(dims, given, spare, w_in, w_out, vectors, saved, low, flow, grad_in, grad_out, sums):
-    unit_one, inv_one, low_one, qkv, probs, mixed, unit_two, inv_two, low_two, active, slope = saved
+    unit_one, inv_one, low_one, qkv, probs, mixed, unit_two, inv_two, low_two, active, slope, work, low_work, low_more = saved
     count, width = given.shape
     inner = dims["heads"] * dims["head"]
     span = count // dims["spans"]
@@ -816,21 +802,26 @@
         rows = pl.ds(pl.multiple_of(b * span, span), span)
         triple = qkv[t, rows]
         back = mixed[t, rows]
+        key_t = triple[:, inner : 2 * inner].T
+        back_t = back.T
+        heads = range(dims["heads"])
+        lanes = [slice(head * dims["head"], (head + 1) * dims["head"]) for head in heads]
+        for head in heads:
+            work[head] = dot(triple[:, 2 * inner :][:, lanes[head]], back_t[lanes[head]])
+        for head in heads:
+            for columns in lane_chunks(span):
+                share = probs[k * dims["heads"] + head, :, columns]
+                grad_p = work[head, :, columns]
+                grad_s = share * (grad_p - jnp.sum(share * grad_p, axis=0, keepdims=True))
+                low_work[head, :, columns] = grad_s.astype(bf16)
+                low_more[head, :, columns] = share.astype(bf16)
         parts = ([], [], [])
-        for head in range(dims["heads"]):
-            q, key, v = (
-                triple[:, part * inner + head * dims["head"] : part * inner + (head + 1) * dims["head"]]
-                for part in range(3)
-            )
-            grad_o = back[:, head * dims["head"] : (head + 1) * dims["head"]]
-            share = probs[k * dims["heads"] + head]
-            grad_p = dot_nt(grad_o, v)
-            grad_s = share * (grad_p - jnp.sum(share * grad_p, axis=-1, keepdims=True))
-            low_s = grad_s.astype(bf16)
-            parts[0].append(dot(low_s, key) * scale)
-            parts[1].append(dot_t(low_s, q) * scale)
-            parts[2].append(dot_t(share.astype(bf16), grad_o))
-        qkv[t, rows] = jnp.concatenate(parts[0] + parts[1] + parts[2], axis=1).astype(bf16)
+        for head in heads:
+            parts[0].append(dot(key_t[lanes[head]], low_work[head]) * scale)
+            parts[1].append(dot(low_work[head], triple[:, :inner][:, lanes[head]]) * scale)
+            parts[2].append(dot(low_more[head], back[:, lanes[head]]))
+        grad_query = jnp.concatenate(parts[0], axis=0).T
+        qkv[t, rows] = jnp.concatenate([grad_query] + parts[1] + parts[2], axis=1).astype(bf16)
 
     @pl.loop(0, GROUPS)
     def _(t):
@@ -868,20 +859,40 @@
     ]
 
 
+def work_shapes(dims):
+    span = dims["images"] * dims["block"] // dims["spans"]
+    shape = (dims["heads"], span, span)
+    return [(shape, f32), (shape, bf16), (shape, bf16)]
+
+
+def token_gain(vectors, dims):
+    return vectors.at[:, pl.ds(dims["first"], dims["width"])]
+
+
 def decoder_kernel(*refs):
-    projected, codes, weight_rows, images, table, w_in, w_out, head, vectors = refs[:9]
-    grad_in, grad_out, grad_head, grad_projected, vec_out = refs[9:14]
-    stream, given, unit, inverse, low, flow, sums, loss = refs[14:22]
-    saved = refs[22:]
+    projected, codes, images, table, w_in, w_out, pixel_w, vectors_all = refs[:8]
+    grad_in, grad_out, grad_head, grad_projected, vec_out = refs[8:13]
+    stream, given, unit, inverse, low, flow, sums, loss, head, pixels_here, head_sum, loaded = refs[13:25]
+    saved = refs[25:]
     dims = DEC
+    vectors = token_gain(vectors_all, dims)
     count, width = stream.shape
     block = dims["block"]
+    copies = [pltpu.make_async_copy(pixel_w.at[pl.ds(PATCH_DIM, width)], head, loaded.at[0])]
+    for b in range(dims["images"]):
+        copies.append(
+            pltpu.make_async_copy(
+                images.at[b], pixels_here.at[b], loaded.at[1 + b]
+            )
+        )
+    for copy in copies:
+        copy.start()
     sums[...] = jnp.zeros_like(sums)
     loss[...] = jnp.zeros_like(loss)
 
     def placer(b):
         return (
-            lax.broadcasted_iota(jnp.int32, (64, block), 0) == codes[b][:, :block]
+            lax.broadcasted_iota(jnp.int32, (64, block), 0) == codes[b][:1, :block]
         ).astype(f32)
 
     def block_rows(b):
@@ -894,27 +905,36 @@
         source = jnp.where(at > MASK_ROW, 0.0, source)
         stream[block_rows(b)] = exact_dot(placer(b), source, ((0,), (0,))) + table[...]
 
-    layer_forward_rows(dims, stream, w_in, w_out, vectors, saved)
+    for _ in layer_forward_rows(dims, stream, w_in, w_out, vectors, saved):
+        pass
     norm_rows(stream, vectors[5:6, :], vectors[6:7, :], unit, inverse, low, dims["step"])
-    grad_head[...] = jnp.zeros_like(grad_head)
-    pixels_wide = images.shape[-1]
+    for copy in copies:
+        copy.wait()
+    head_sum[...] = jnp.zeros_like(head_sum)
+    pixels_wide = pixels_here.shape[-1]
+    counted = vectors_all[7:8, :]
+    patch_total = jnp.sum(counted, axis=1, keepdims=True) / (counted.shape[1] // 8)
 
     @pl.loop(0, dims["images"])
     def _(b):
         rows = block_rows(b)
         predicted = dot(low[rows], head[...])
-        pixels = images[b].astype(f32)
+        pixels = jnp.concatenate(
+            [pixels_here[b], jnp.zeros((block - IMAGE_PATCHES, pixels_wide), bf16)], axis=0
+        ).astype(f32)
         centred = pixels - jnp.mean(pixels, axis=-1, keepdims=True)
         variance = jnp.sum(centred * centred, axis=-1, keepdims=True) / (pixels_wide - 1)
         errors = predicted - centred * lax.rsqrt(variance + eps_norm)
         at = lax.broadcasted_iota(jnp.int32, (64, 128), 0)
-        spread = jnp.where(at == MASK_ROW, weight_rows[b], 0.0)
+        share = codes[b][2:3, :128].astype(f32) / patch_total
+        spread = jnp.where(at == MASK_ROW, share, 0.0)
         weight = exact_dot(placer(b), spread, ((0,), (0,)))[:, :1]
         loss[...] = loss[...] + fold(errors * errors * weight)
         grad_low = (errors * (2.0 / pixels_wide) * weight).astype(bf16)
-        grad_head[...] = grad_head[...] + dot_t(low[rows], grad_low)
+        head_sum[...] = head_sum[...] + dot_t(low[rows], grad_low)
         given[rows] = dot_nt(grad_low, head[...])
 
+    grad_head[...] = head_sum[...].astype(bf16)
     norm_back_rows(given, unit, inverse, vectors[5:6, :], given, None, sums, 5, dims["step"])
     layer_backward_rows(
         dims, given, stream, w_in, w_out, vectors, saved, low, flow, grad_in, grad_out, sums
@@ -933,13 +953,14 @@
     vec_out[7:8, :] = jnp.broadcast_to(total / pixels_wide, (1, width))
 
 
-def decoder_step(projected, codes, weight_rows, images, table, w_in, w_out, head, vectors):
+def decoder_step(projected, codes, images, table, w_in, w_out, pixel_w, vectors):
     dims = DEC
     count, width = dims["images"] * dims["block"], dims["width"]
+    wide = images.shape[-1]
     outs = [
         jax.ShapeDtypeStruct(w_in.shape, bf16),
         jax.ShapeDtypeStruct(w_out.shape, bf16),
-        jax.ShapeDtypeStruct(head.shape, f32),
+        jax.ShapeDtypeStruct((width, wide), bf16),
         jax.ShapeDtypeStruct(projected.shape, bf16),
         jax.ShapeDtypeStruct((8, width), f32),
     ]
@@ -951,79 +972,275 @@
         ((count, width), bf16),
         ((count, dims["hidden"]), bf16),
         ((7, 8, width), f32),
-        ((8, images.shape[-1]), f32),
-    ] + saved_shapes(dims)
+        ((8, wide), f32),
+        ((width, wide), bf16),
+        ((dims["images"],) + images.shape[1:], bf16),
+        ((width, wide), f32),
+        None,
+    ]
+    scratch += saved_shapes(dims) + work_shapes(dims)
+    in_vmem = pl.BlockSpec(memory_space=pltpu.VMEM)
+    anywhere = pl.BlockSpec(memory_space=pl.ANY)
     return pl.pallas_call(
         decoder_kernel,
         out_shape=outs,
-        scratch_shapes=[pltpu.VMEM(shape, dtype) for shape, dtype in scratch],
+        in_specs=[in_vmem, in_vmem, anywhere, in_vmem, in_vmem, in_vmem, anywhere, in_vmem],
+        scratch_shapes=[
+            pltpu.SemaphoreType.DMA((5,)) if shape is None else pltpu.VMEM(*shape)
+            for shape in scratch
+        ],
         compiler_params=pltpu.CompilerParams(vmem_limit_bytes=62 * 1024 * 1024),
         name="decoder_step",
-    )(projected, codes, weight_rows, images, table, w_in, w_out, head, vectors)
-
-
-def encoder_forward_kernel(*refs):
-    kept, images, table, w_in, w_out, embed, bridge, vectors = refs[:8]
-    projected, retained, unit, inverse, low = refs[8:13]
-    saved = refs[13:24]
-    (stream,) = refs[24:]
+    )(projected, codes, images, table, w_in, w_out, pixel_w, vectors)
+
+
+def encode_kernel(ring, *refs):
     dims = ENC
+    images, codes, table = refs[:3]
+    refs = refs[3:]
+    group = lax.axis_index("tensor")
+    if ring:
+        masters, count_row, refs = refs[:7], refs[7], refs[8:]
+        wholes, vectors_all, projected, kept_state = refs[:7], refs[7], refs[8], refs[9:24]
+        refs = refs[24:]
+        parts, send, recv, local, vec_parts = refs[:7], *refs[7:11]
+        raw = dict(zip((PIX, EOUT, BRI), refs[11:14]))
+        refs = refs[14:]
+    else:
+        wholes, vectors_all = refs[:4], refs[4]
+        projected, kept_state = refs[5], refs[6:21]
+        refs = refs[21:]
+        wholes = dict(zip((PIX, EIN, EOUT, BRI), wholes))
+    loaded, flushed = refs[:2]
+    pixels_here, stream, w_in, w_out, embed, bridge = refs[2:8]
+    retained, unit, inverse, low = refs[8:12]
+    saved = refs[12:23]
+    work = refs[23:]
+    held = (retained, unit, inverse, low) + tuple(saved)
+    vectors = token_gain(vectors_all, dims)
     count, width = stream.shape
     block = dims["block"]
+
+    picture_copies = [
+        pltpu.make_async_copy(
+            images.at[b], pixels_here.at[b], loaded.at[4 + b]
+        )
+        for b in range(dims["images"])
+    ]
+    for copy in picture_copies:
+        copy.start()
+
+    def load(slot, array, target):
+        if not ring:
+            source = wholes[array]
+            if array == PIX:
+                source = source.at[pl.ds(0, PATCH_DIM)]
+            pltpu.make_async_copy(source, target, loaded.at[slot]).start()
+            return pltpu.make_async_copy(source, target, loaded.at[slot])
+        if array != EIN:
+            pltpu.make_async_copy(wholes[array], raw[array], loaded.at[slot]).start()
+            return pltpu.make_async_copy(wholes[array], raw[array], loaded.at[slot])
+        rows = wholes[array].shape[4]
+
+        @pl.loop(0, 32)
+        def _(k):
+            pltpu.make_async_copy(
+                wholes[array].at[k // 16, (k // 8) % 2, (k // 2) % 4, k % 2],
+                target.at[k // 8, pl.ds(pl.multiple_of((k % 8) * rows, rows), rows)],
+                loaded.at[slot],
+            ).start()
+
+        return pltpu.make_async_copy(target, target, loaded.at[slot])
+
+    def assemble(array, target):
+        if ring and array in SHARED:
+            count = -(-target.shape[0] // raw[array].shape[4])
+            pieces = [
+                raw[array][k // 8, (k // 4) % 2, (k // 2) % 2, k % 2] for k in range(count)
+            ]
+            target[...] = jnp.concatenate(pieces, axis=0)[: target.shape[0]]
+        elif ring:
+
+            @pl.loop(0, GROUPS)
+            def _(t):
+                pieces = [raw[array][t // 2, t % 2, k // 2, k % 2] for k in range(8)]
+                target[t] = jnp.concatenate(pieces, axis=0)
+
+    flushes = []
+
+    def flush(*members):
+        for member in members:
+            copy = pltpu.make_async_copy(held[member], kept_state[member], flushed.at[member])
+            copy.start()
+            flushes.append(copy)
+
+    if ring:
+        for array in range(6):
+            if array in SHARED:
+                rows = masters[array].shape[0] // 4
+                rows = pl.ds(pl.multiple_of(group * rows, 8), rows)
+                parts[array][...] = masters[array][rows].astype(bf16)
+            else:
+                parts[array][...] = state_rows(masters[array], slice(None)).astype(bf16)
+        columns = masters[VEC].shape[1]
+        parts[VEC][...] = jnp.zeros_like(parts[VEC])
+        parts[VEC][:7, :columns] = masters[VEC][...].astype(bf16).astype(f32)
+        parts[VEC][7:8, :] = count_row[...]
+        ticks = gather_ticks(parts, wholes, send, recv, local)
+
+    def advance(times):
+        if ring:
+            for _ in range(times):
+                next(ticks)
+
+    advance(5)
+    embed_copy = load(0, PIX, embed)
+    if ring:
+        vec_copy = pltpu.make_async_copy(wholes[VEC], vec_parts, loaded.at[1])
+        vec_copy.start()
+        vec_copy.wait()
+        vectors_all[...] = jnp.concatenate(
+            [vec_parts[0, 0, k // 2, k % 2][:, :columns] for k in range(8)], axis=1
+        )
+    for copy in picture_copies:
+        copy.wait()
+    embed_copy.wait()
+    assemble(PIX, embed)
 
     @pl.loop(0, dims["images"])
     def _(b):
         rows = pl.ds(pl.multiple_of(b * block, block), block)
         choice = (
-            lax.broadcasted_iota(jnp.int32, (table.shape[0], block), 0) == kept[b][:, :block]
+            lax.broadcasted_iota(jnp.int32, (IMAGE_PATCHES, block), 0) == codes[b][1:2, :block]
         )
-        retained[rows] = dot_t(choice.astype(bf16), images[b]).astype(bf16)
+        retained[rows] = dot_t(choice.astype(bf16), pixels_here[b]).astype(bf16)
         places = exact_dot(choice.astype(f32), table[...], ((0,), (0,)))
         at = lax.broadcasted_iota(jnp.int32, (block, width), 0)
         start = dot(retained[rows], embed[...]) + places
         stream[rows] = jnp.where(at == CLASS_ROW, vectors[0:1, :], start)
 
-    layer_forward_rows(dims, stream, w_in, w_out, vectors, saved)
+    flush(0)
+    advance(2)
+    load(2, EIN, w_in).wait()
+    layer = layer_forward_rows(dims, stream, w_in, w_out, vectors, saved + work)
+    next(layer)
+    flush(4, 5, 6, 7, 8, 9)
+    advance(2)
+    bridge_copy = load(1, BRI, bridge)
+    load(3, EOUT, w_out).wait()
+    assemble(EOUT, w_out)
+    next(layer)
+    flush(10, 11, 12)
+    advance(1)
+    for _ in layer:
+        pass
+    flush(13, 14)
     norm_rows(stream, vectors[5:6, :], vectors[6:7, :], unit, inverse, low, dims["step"])
+    flush(1, 2, 3)
+    bridge_copy.wait()
+    assemble(BRI, bridge)
 
     @pl.loop(0, dims["images"])
     def _(b):
         rows = pl.ds(pl.multiple_of(b * block, block), block)
         projected[b] = dot(low[rows], bridge[...])
 
-
-def encoder_forward(kept, images, table, w_in, w_out, embed, bridge, vectors):
+    advance(2)
+    for copy in flushes:
+        copy.wait()
+
+
+def encode(images, codes, table, weights, count_row=None, vectors=None):
     dims = ENC
+    ring = vectors is None
     count, width = dims["images"] * dims["block"], dims["width"]
-    outs = [
-        ((dims["images"], dims["block"], bridge.shape[1]), f32),
+    bridge_wide = weights[BRI].shape[-1]
+    in_vmem = pl.BlockSpec(memory_space=pltpu.VMEM)
+    anywhere = pl.BlockSpec(memory_space=pl.ANY)
+    kept_shapes = [
         ((count, images.shape[-1]), bf16),
         ((count, width), f32),
         ((count, 1), f32),
         ((count, width), bf16),
     ] + saved_shapes(dims)
+    outs = [((dims["images"], dims["block"], bridge_wide), f32)] + kept_shapes
+    out_specs = [in_vmem] + [anywhere] * len(kept_shapes)
+    in_specs = [anywhere, in_vmem, in_vmem]
+    scratch = []
+    if ring:
+        shapes = []
+        for array in range(6):
+            rows, wide = weights[array].size // weights[array].shape[-1], weights[array].shape[-1]
+            shapes.append((rows // 4 if array in SHARED else rows, wide))
+        shapes.append((8, 256))
+        types = [bf16] * 6 + [f32]
+        operands = [images, codes, table, *weights, count_row]
+        in_specs += [in_vmem] * 8
+        gathered = [(whole_shape(k, shape), types[k]) for k, shape in enumerate(shapes)]
+        outs = gathered + [((8, shapes_total(weights[VEC])), f32)] + outs
+        out_specs = [anywhere] * 7 + [in_vmem] + out_specs
+        units = sum(len(step) for step in GATHER_STEPS)
+        scratch += [pltpu.VMEM(shape, kind) for shape, kind in zip(shapes, types)]
+        scratch += [
+            pltpu.SemaphoreType.DMA((units, 6)),
+            pltpu.SemaphoreType.DMA((units, 6)),
+            pltpu.SemaphoreType.DMA((7,)),
+            pltpu.VMEM(whole_shape(VEC, shapes[VEC]), f32),
+        ]
+        scratch += [
+            pltpu.VMEM(whole_shape(array, shapes[array]), bf16) for array in (PIX, EOUT, BRI)
+        ]
+        params = dict(collective_id=0, has_side_effects=True)
+        w_shapes = [
+            (GROUPS, 8 * shapes[EIN][0], shapes[EIN][1]),
+            (GROUPS, 8 * shapes[EOUT][0], shapes[EOUT][1]),
+        ]
+    else:
+        operands = [images, codes, table] + [weights[k] for k in (PIX, EIN, EOUT, BRI)] + [vectors]
+        in_specs += [anywhere] * 4 + [in_vmem]
+        params = {}
+        w_shapes = [weights[EIN].shape, weights[EOUT].shape]
+    scratch += [pltpu.SemaphoreType.DMA((8,)), pltpu.SemaphoreType.DMA((15,))]
+    buffers = [
+        ((dims["images"],) + images.shape[1:], bf16),
+        ((count, width), f32),
+        (w_shapes[0], bf16),
+        (w_shapes[1], bf16),
+        ((PATCH_DIM, width), bf16),
+        ((width, bridge_wide), bf16),
+    ]
+    buffers += kept_shapes + work_shapes(dims)
+    scratch += [pltpu.VMEM(*buffer) for buffer in buffers]
     return pl.pallas_call(
-        encoder_forward_kernel,
-        out_shape=[jax.ShapeDtypeStruct(shape, dtype) for shape, dtype in outs],
-        scratch_shapes=[pltpu.VMEM((count, width), f32)],
-        compiler_params=pltpu.CompilerParams(vmem_limit_bytes=62 * 1024 * 1024),
-        name="encoder_forward",
-    )(kept, images, table, w_in, w_out, embed, bridge, vectors)
+        functools.partial(encode_kernel, ring),
+        out_shape=[jax.ShapeDtypeStruct(shape, kind) for shape, kind in outs],
+        in_specs=in_specs,
+        out_specs=out_specs,
+        scratch_shapes=scratch,
+        compiler_params=pltpu.CompilerParams(vmem_limit_bytes=62 * 1024 * 1024, **params),
+        name="gather_encode" if ring else "encode",
+    )(*operands)
+
+
+def shapes_total(vector_shard):
+    return 8 * vector_shard.shape[1]
 
 
 def encoder_backward_kernel(*refs):
     grad_projected, retained, unit, inverse, low_end = refs[:5]
     saved = list(refs[5:16])
-    w_in, w_out, bridge, vectors = refs[16:20]
-    grad_in, grad_out, grad_bridge, grad_embed, vec_out = refs[20:25]
-    given, spare, low, flow, sums, qkv, mixed = refs[25:]
+    w_in, w_out, bridge, vectors_all, grad_head, dec_sums = refs[16:22]
+    grad_in, grad_out, grad_bridge, grad_pixel, packed = refs[22:27]
+    given, spare, low, flow, sums, qkv, mixed, vec_all = refs[27:35]
     dims = ENC
+    vectors = token_gain(vectors_all, dims)
     count, width = given.shape
     block = dims["block"]
     sums[...] = jnp.zeros_like(sums)
     qkv[...] = saved[3][...]
     mixed[...] = saved[5][...]
     saved[3], saved[5] = qkv, mixed
+    saved += refs[35:]
 
     flat = grad_projected[...].reshape(count, grad_projected.shape[-1])
     grad_bridge[...] = dot_t(low_end[...], flat).astype(bf16)
@@ -1032,7 +1249,8 @@
     layer_backward_rows(
         dims, given, spare, w_in, w_out, vectors, saved, low, flow, grad_in, grad_out, sums
     )
-    grad_embed[...] = dot_t(retained[...], given[...].astype(bf16)).astype(bf16)
+    grad_pixel[:PATCH_DIM] = dot_t(retained[...], given[...].astype(bf16)).astype(bf16)
+    grad_pixel[PATCH_DIM:] = grad_head[...]
 
     def tokens(rows):
         at = lax.broadcasted_iota(jnp.int32, (block, width), 0)
@@ -1040,11 +1258,16 @@
 
     row_loop(count, block, tokens)
     for row in range(7):
-        vec_out[row : row + 1, :] = jnp.sum(sums[row], axis=0, keepdims=True)
-    vec_out[7:8, :] = jnp.zeros((1, width), f32)
-
-
-def encoder_backward(grad_projected, kept_state, w_in, w_out, bridge, vectors):
+        vec_all[row : row + 1, :width] = jnp.sum(sums[row], axis=0, keepdims=True)
+    vec_all[7:8, :width] = jnp.zeros((1, width), f32)
+    vec_all[:, width:] = dec_sums[...]
+    columns = vec_all.shape[1] // 8
+    packed[...] = jnp.zeros_like(packed)
+    for k in range(8):
+        packed[k, :, :columns] = vec_all[:, k * columns : (k + 1) * columns]
+
+
+def encoder_backward(grad_projected, kept_state, w_in, w_out, bridge, vectors, grad_head, dec_sums):
     dims = ENC
     count, width = dims["images"] * dims["block"], dims["width"]
     shapes = saved_shapes(dims)
@@ -1053,8 +1276,8 @@
         jax.ShapeDtypeStruct(w_in.shape, bf16),
         jax.ShapeDtypeStruct(w_out.shape, bf16),
         jax.ShapeDtypeStruct(bridge.shape, bf16),
-        jax.ShapeDtypeStruct((pixels_wide, width), bf16),
-        jax.ShapeDtypeStruct((8, width), f32),
+        jax.ShapeDtypeStruct((pixels_wide + grad_head.shape[0], width), bf16),
+        jax.ShapeDtypeStruct((8, 8, 256), f32),
     ]
     scratch = [
         ((count, width), f32),
@@ -1064,14 +1287,15 @@
         ((7, 8, width), f32),
         shapes[3],
         shapes[5],
-    ]
+        (vectors.shape, f32),
+    ] + work_shapes(dims)
     return pl.pallas_call(
         encoder_backward_kernel,
         out_shape=outs,
         scratch_shapes=[pltpu.VMEM(shape, dtype) for shape, dtype in scratch],
         compiler_params=pltpu.CompilerParams(vmem_limit_bytes=62 * 1024 * 1024),
         name="encoder_backward",
-    )(grad_projected, *kept_state, w_in, w_out, bridge, vectors)
+    )(grad_projected, *kept_state, w_in, w_out, bridge, vectors, grad_head, dec_sums)
 
 
 def gather_grouped(part, groups):
@@ -1088,50 +1312,23 @@
     return tensor_count == 4 and lax.axis_size("dp") == 8
 
 
-def gather_all(masters, counted):
-    tensor_count = lax.axis_size("tensor")
-    columns = masters[6].shape[1]
-    flat = [
-        master.reshape(-1, master.shape[-1]).astype(bf16) for master in masters[:4]
-    ]
-    vectors_low = masters[6].astype(bf16).astype(f32)
-    if ringed(tensor_count):
-        at = lax.axis_index("tensor")
-        quarters = [
-            lax.dynamic_slice_in_dim(
-                master, at * (master.shape[0] // tensor_count), master.shape[0] // tensor_count
-            ).astype(bf16)
-            for master in masters[4:6]
-        ]
-        lanes = 256
-        vec_part = jnp.concatenate(
-            [
-                jnp.pad(vectors_low, ((0, 0), (0, lanes - columns))),
-                jnp.broadcast_to(counted, (1, lanes)),
-            ],
-            axis=0,
-        )
-        wholes = gather_weights([quarters[0], flat[0], flat[1], quarters[1], flat[2], flat[3], vec_part])
-        grouped = [
-            wholes[k].reshape(tensor_count, -1, wholes[k].shape[-1]) for k in (EIN, EOUT, DIN, DOUT)
-        ]
-        pixel_w = wholes[PIX].reshape(-1, wholes[PIX].shape[-1])
-        bridge_w = wholes[BRI].reshape(-1, wholes[BRI].shape[-1])
-        vec_parts = wholes[VEC][0, 0].reshape(8, 8, lanes)
-        vectors_all = vec_parts[:, :7, :columns].transpose(1, 0, 2).reshape(7, -1)
-        patch_total = jnp.sum(vec_parts[:, 7, 0])
-        return grouped, pixel_w, bridge_w, vectors_all, patch_total
-    grouped = [gather_grouped(part, tensor_count) for part in flat]
-    pixel_w = lax.all_gather(masters[4].astype(bf16), "dp", axis=0, tiled=True)
-    bridge_w = lax.all_gather(masters[5].astype(bf16), "dp", axis=0, tiled=True)
-    vectors_all = lax.all_gather(vectors_low, "dp", axis=1, tiled=True)
-    return grouped, pixel_w, bridge_w, vectors_all, lax.psum(counted, "dp")
+def plain_gather(masters, counted):
+    groups = lax.axis_size("tensor")
+    wholes = {}
+    for array, k in ((EIN, 0), (EOUT, 1), (DIN, 2), (DOUT, 3)):
+        flat = masters[k].reshape(-1, masters[k].shape[-1]).astype(bf16)
+        wholes[array] = gather_grouped(flat, groups)
+    for array, k in ((PIX, 4), (BRI, 5)):
+        wholes[array] = lax.all_gather(masters[k].astype(bf16), "dp", axis=0, tiled=True)
+    low = masters[6].astype(bf16).astype(f32)
+    vectors = lax.all_gather(low, "dp", axis=1, tiled=True)
+    eighth = jnp.broadcast_to(lax.psum(counted, "dp") / 8, (1, vectors.shape[1]))
+    return wholes, jnp.concatenate([vectors, eighth], axis=0)
 
 
 def ring_finish(gradients, masters, firsts, seconds):
     grouped, grad_pixel, grad_bridge, packed = gradients
     tensor_count = lax.axis_size("tensor")
-    columns = masters[6].shape[1]
     order = (4, 0, 1, 5, 2, 3, 6)
     sources = (grad_pixel, grouped[0], grouped[1], grad_bridge, grouped[2], grouped[3])
     operands = []
@@ -1141,8 +1338,7 @@
         if array in SHARED:
             rows = rows // tensor_count
         operands.append(source.reshape(whole_shape(array, (rows, wide))))
-    packed = packed.reshape(8, -1, columns).transpose(1, 0, 2)
-    operands.append(jnp.pad(packed, ((0, 0), (0, 0), (0, 256 - columns))))
+    operands.append(packed)
     states = [[members[k] for k in order] for members in (masters, firsts, seconds)]
     *sums, stats = scatter_gradients(operands, *states)
     for array in SHARED:
@@ -1164,6 +1360,8 @@
 
     reduced = [scatter_grouped(gradient) for gradient in grouped]
     reduced += [scatter_shared(grad_pixel), scatter_shared(grad_bridge)]
+    whole = packed.shape[0] * (ENCODER_WIDTH + D_D) // 8
+    packed = packed[:, :, : whole // packed.shape[0]].transpose(1, 0, 2).reshape(8, -1)
     vector_sum = lax.psum(packed, EVERY)
     own = lax.dynamic_slice_in_dim(
         vector_sum[:7], lax.axis_index("dp") * columns, columns, axis=1
@@ -1199,61 +1397,56 @@
     *state,
 ):
     masters, firsts, seconds = state[:7], state[7:14], state[14:21]
-    encoder_in, encoder_out, decoder_in, decoder_out, pixel_maps, bridge_map, vector_pack = masters
     tensor_count = lax.axis_size("tensor")
     tensor_at = lax.axis_index("tensor")
     counted = jnp.sum(masked.astype(f32) * image_valid.astype(f32)[:, None])
-    grouped_w, pixel_w, bridge_w, vectors_all, patch_total = gather_all(masters, counted)
-    enc_in_w, enc_out_w, dec_in_w, dec_out_w = grouped_w
-    enc_vectors = vectors_all[:, :ENCODER_WIDTH]
-    dec_vectors = vectors_all[:, ENCODER_WIDTH:]
     image_count = images.shape[0] // tensor_count
-
-    def own(member):
-        return lax.dynamic_slice_in_dim(member, tensor_at * image_count, image_count, axis=0)
-
-    images, keep_index, unshuffle, masked, image_valid = map(
-        own, (images, keep_index, unshuffle, masked, image_valid)
-    )
-    block = DEC["block"]
-    images = jnp.pad(images, ((0, 0), (0, block - IMAGE_PATCHES), (0, 0)))
     lanes = 256
     codes = jnp.pad(
         jnp.where(masked == 1, MASK_ROW, unshuffle),
         ((0, 0), (0, lanes - IMAGE_PATCHES)),
         constant_values=-1,
     )
-    codes = jnp.where(jnp.arange(lanes) == IMAGE_PATCHES, CLASS_ROW, codes)[:, None, :]
-    kept = jnp.pad(keep_index, ((0, 0), (0, 128 - KEEP)), constant_values=-1)[:, None, :]
-    weight_rows = jnp.broadcast_to(
-        (image_valid.astype(f32) / patch_total)[:, None, None], (image_count, 1, 128)
+    codes = jnp.where(jnp.arange(lanes) == IMAGE_PATCHES, CLASS_ROW, codes)
+    kept = jnp.pad(keep_index, ((0, 0), (0, lanes - KEEP)), constant_values=-1)
+    valid = jnp.broadcast_to(image_valid[:, None], codes.shape)
+    codes = jnp.stack([codes, kept, valid], axis=1)
+    images = lax.dynamic_slice_in_dim(images, tensor_at * image_count, image_count, axis=0)
+    codes = lax.dynamic_slice_in_dim(codes, tensor_at * image_count, image_count, axis=0)
+    enc_table = sinusoid_table(ENCODER_WIDTH, GRID_PATCHES, IMAGE_PATCHES, IMAGE_PATCHES)
+    dec_table = sinusoid_table(D_D, GRID_PATCHES, IMAGE_PATCHES, DEC["block"])
+    if ringed(tensor_count):
+        order = (4, 0, 1, 5, 2, 3, 6)
+        results = encode(
+            images,
+            codes,
+            enc_table,
+            [masters[k] for k in order],
+            jnp.broadcast_to(counted, (1, lanes)),
+        )
+        wholes, vectors, projected, enc_state = results[:7], results[7], results[8], results[9:]
+        wholes = [
+            whole.reshape(-1, whole.shape[-1])
+            if array in SHARED
+            else whole.reshape(tensor_count, -1, whole.shape[-1])
+            for array, whole in enumerate(wholes)
+        ]
+    else:
+        wholes, vectors = plain_gather(masters, counted)
+        projected, *enc_state = encode(images, codes, enc_table, wholes, vectors=vectors)
+    grad_dec_in, grad_dec_out, grad_head, grad_projected, dec_sums = decoder_step(
+        projected, codes, images, dec_table, wholes[DIN], wholes[DOUT], wholes[PIX], vectors
     )
-    enc_state = encoder_forward(
-        kept,
-        images,
-        sinusoid_table(ENCODER_WIDTH, GRID_PATCHES, IMAGE_PATCHES, block),
-        enc_in_w,
-        enc_out_w,
-        pixel_w[:PATCH_DIM],
-        bridge_w,
-        enc_vectors,
+    grad_enc_in, grad_enc_out, grad_bridge, grad_pixel, packed = encoder_backward(
+        grad_projected,
+        enc_state,
+        wholes[EIN],
+        wholes[EOUT],
+        wholes[BRI],
+        vectors,
+        grad_head,
+        dec_sums,
     )
-    grad_dec_in, grad_dec_out, grad_head, grad_projected, dec_sums = decoder_step(
-        enc_state[0],
-        codes,
-        weight_rows,
-        images,
-        sinusoid_table(D_D, GRID_PATCHES, IMAGE_PATCHES, block),
-        dec_in_w,
-        dec_out_w,
-        pixel_w[PATCH_DIM:],
-        dec_vectors,
-    )
-    grad_enc_in, grad_enc_out, grad_bridge, grad_embed, enc_sums = encoder_backward(
-        grad_projected, enc_state[1:], enc_in_w, enc_out_w, bridge_w, enc_vectors
-    )
-    grad_pixel = jnp.concatenate([grad_embed, grad_head.astype(bf16)], axis=0)
-    packed = jnp.concatenate([enc_sums, dec_sums], axis=1)
     finish = ring_finish if ringed(tensor_count) else plain_finish
     return finish(
         ([grad_enc_in, grad_enc_out, grad_dec_in, grad_dec_out], grad_pixel, grad_bridge, packed),

time: 495 us -> 432 us (0.87)
  Pallas kernels: 458 us -> 412 us
  local copies, waits for them, and re-layouts: 27.3 us -> 14.2 us
    pallas_call x3 -> x2, Pallas kernels: 259 us -> 215 us  [the longest x1 138 us: encode(): pl.pallas_call(functools.partial(encode_kernel, ring), out_shape=[jax.Sha...]
    slice x5 -> x0, local copies, waits for them, and re-layouts: 6.54 us -> none  [the longest x1 2.4 us: shards(): pixel_w[:PATCH_DIM]]
    unnamed x76 -> x51, local copies, waits for them, and re-layouts: 10.4 us -> 9.25 us
where the time goes in v4:
time: 432 us; the launch traced here: 431 us
  Pallas kernels  412 us (95%)
  local copies, waits for them, and re-layouts  14.2 us (3%)
    pallas_call x1, Pallas kernels, scatter_gradients(): pl.pallas_call(functools.partial(scatter_kernel, shapes, units), out_shap...  157 us
    pallas_call x1, Pallas kernels, encode(): pl.pallas_call(functools.partial(encode_kernel, ring), out_shape=[jax.Sha...  138 us
    pallas_call x1, Pallas kernels, decoder_step(): pl.pallas_call(decoder_kernel, out_shape=outs, in_specs=[in_vmem, in_vmem...  77.3 us
    pallas_call x1, Pallas kernels, encoder_backward(): pl.pallas_call(encoder_backward_kernel, out_shape=outs, scratch_shapes=[p...  32.9 us
    unnamed x51, local copies, waits for them, and re-layouts  9.25 us

profile of v4, /device:TPU:0, one launch (start us, length us, event | category | flops | bytes accessed | tf_op | source)
XLA Modules:
  0.0 431.0 jit_solution(8493174613717232610)
XLA Ops:
  0.7 0.7 convert_element_type.7
  1.3 1.4 multiply_reduce_fusion
  2.7 1.2 broadcast_in_dim.20.refs_10_
  3.9 0.7 pad.9
  4.6 0.7 compare_select_fusion
  5.4 0.7 stack_broadcast_in_dim.2
  6.2 0.6 fusion.refs_1_
  6.8 2.3 constant_dynamic-slice_fusion
  9.1 1.2 copy.52.refs_0_.refs_2_
  10.3 137.6 %gather_encode.1 = (bf16[4,2,2,2,40,768]{5,4,3,2,1,0:T(8,128)(2,1)}, bf16[2,2,4,2,96,1344]{5,4,3,2,1,0:T(8,128)(2,1)}, bf16[2,2,4,2,120,768]{5,4,3,2,1,0:T(8,128...) custom-call(bf16[4,196,768]{2,1,0:T(8,128)(2,1)} %copy.52.refs_0_.re, ...), custom_call_target="tpu_custom_call" | custom-call | tf_op jit(solution)/shard_map/gather_encode/pallas_call | solution.py:1214
  147.8 77.3 %decoder_step.1 = (bf16[4,512,896]{2,1,0:T(8,128)(2,1)}, bf16[4,640,512]{2,1,0:T(8,128)(2,1)}, bf16[512,768]{1,0:T(8,128)(2,1)}, bf16[4,64,512]{2,1,0:T(8,128)(2,1)}, f32[8,512]{1,0:T(8,128)}) custom-call(f32[4,64,512]{2,1,0:T(8,128)} %get-tuple-element.87.refs_0_, s32[4,3,256]{2,1,0:T(4,128)} %fusion.refs_1_, bf16[4,196,768]{2,1,0:T(8,128)(2,1)} %copy.52.refs_0_.refs_2_, ...), custom_call_target="tpu_custom_call" | custom-call | tf_op jit(solution)/shard_map/decoder_step/pallas_call | solution.py:984
  225.1 32.9 %encoder_backward.1 = (bf16[4,768,1344]{2,1,0:T(8,128)(2,1)}, bf16[4,960,768]{2,1,0:T(8,128)(2,1)}, bf16[768,512]{1,0:T(8,128)(2,1)}, bf16[1280,768]{1,0:T(8,128)(2,1)}, f32[8,8,256]{2,1,0:T(8,128)}) custom-call(bf16[4,64,512]{2,1,0:T(8,128)(2,1)} %get-tuple-element.92.refs_0_, bf16[256,768]{1,0:T(8,128)(2,1)} %get-tuple-element.93.refs_1_, ...), custom_call_target="tpu_custom_call" | custom-call | tf_op jit(solution)/shard_map/encoder_backward/pallas_call | solution.py:1292
  258.0 0.0 copy-start
  258.2 156.6 %scatter_gradients.1 = (f32[4,40,768]{2,1,0:T(8,128)}, f32[96,1344]{1,0:T(8,128)}, f32[120,768]{1,0:T(8,128)}, f32[4,24,512]{2,1,0:T(8,128)}, f32[64,896]{1,0:T(...) custom-call(bf16[4,2,2,2,40,768]{5,4,3,2,1,0:T(8,128)(2,1)} %bitcast.25, ...), custom_call_target="tpu_custom_call" | custom-call | bytes 46530560 | tf_op jit(solution)/shard_map/scatter_gradients/pallas_call | solution.py:509
  415.1 0.9 copy-done.13
  416.0 0.9 copy-done.14
  416.9 1.0 copy-done.15
  417.9 1.0 copy-done.16
  418.9 0.9 copy-done.17
  419.8 0.9 copy-done.18
  420.8 0.9 copy-done.19
  421.7 0.7 copy-done.23
  422.4 0.7 copy-done.24
  423.1 7.8 %apply_update.1 = (f32[160,768]{1,0:T(8,128)}, f32[96,1,1344]{2,1,0:T(1,128)}, f32[1,120,768]{2,1,0:T(8,128)}, f32[96,512]{1,0:T(8,128)}, f32[64,1,896]{2,1,0:T(...) custom-call(f32[160,768]{1,0:T(8,128)S(1)} %bitcast.15, ...), custom_call_target="tpu_custom_call" | custom-call | tf_op jit(solution)/shard_map/apply_update/pallas_call | solution.py:565
  (44 shorter events, 0.2 us)
Async XLA Ops:
  258.0 156.8 %copy-start = (f32[160,768]{1,0:T(8,128)S(1)}, f32[160,768]{1,0:T(8,128)}, u32[]{:S(2)}) copy-start(f32[160,768]{1,0:T(8,128)} %refs_7_.5) | copy-start | bytes 1474564
  258.1 156.8 %copy-start.1 = (f32[1,120,768]{2,1,0:T(8,128)S(1)}, f32[1,120,768]{2,1,0:T(8,128)}, u32[]{:S(2)}) copy-start(f32[1,120,768]{2,1,0:T(8,128)} %refs_9_.5) | copy-start | bytes 1105924
  258.1 156.8 %copy-start.2 = (f32[64,1,896]{2,1,0:T(1,128)S(1)}, f32[64,1,896]{2,1,0:T(1,128)}, u32[]{:S(2)}) copy-start(f32[64,1,896]{2,1,0:T(1,128)} %refs_11_.3) | copy-start | bytes 688132
  258.1 156.8 %copy-start.3 = (f32[160,768]{1,0:T(8,128)S(1)}, f32[160,768]{1,0:T(8,128)}, u32[]{:S(2)}) copy-start(f32[160,768]{1,0:T(8,128)} %refs_14_.3) | copy-start | bytes 1474564
  258.1 156.8 %copy-start.4 = (f32[160,768]{1,0:T(8,128)S(1)}, f32[160,768]{1,0:T(8,128)}, u32[]{:S(2)}) copy-start(f32[160,768]{1,0:T(8,128)} %refs_21_.3) | copy-start | bytes 1474564
  258.1 156.8 %copy-start.5 = (f32[96,512]{1,0:T(8,128)S(1)}, f32[96,512]{1,0:T(8,128)}, u32[]{:S(2)}) copy-start(f32[96,512]{1,0:T(8,128)} %refs_10_.3) | copy-start | bytes 589828
  258.1 156.8 %copy-start.6 = (f32[1,120,768]{2,1,0:T(8,128)S(1)}, f32[1,120,768]{2,1,0:T(8,128)}, u32[]{:S(2)}) copy-start(f32[1,120,768]{2,1,0:T(8,128)} %refs_16_.3) | copy-start | bytes 1105924
  258.1 156.8 %copy-start.7 = (f32[1,120,768]{2,1,0:T(8,128)S(1)}, f32[1,120,768]{2,1,0:T(8,128)}, u32[]{:S(2)}) copy-start(f32[1,120,768]{2,1,0:T(8,128)} %refs_23_.3) | copy-start | bytes 1105924
  258.1 156.8 %copy-start.8 = (f32[1,80,512]{2,1,0:T(8,128)S(1)}, f32[1,80,512]{2,1,0:T(8,128)}, u32[]{:S(2)}) copy-start(f32[1,80,512]{2,1,0:T(8,128)} %refs_12_.3) | copy-start | bytes 491524
  258.2 156.8 %copy-start.9 = (f32[64,1,896]{2,1,0:T(1,128)S(1)}, f32[64,1,896]{2,1,0:T(1,128)}, u32[]{:S(2)}) copy-start(f32[64,1,896]{2,1,0:T(1,128)} %refs_18_.3) | copy-start | bytes 688132
  258.2 156.8 %copy-start.10 = (f32[64,1,896]{2,1,0:T(1,128)S(1)}, f32[64,1,896]{2,1,0:T(1,128)}, u32[]{:S(2)}) copy-start(f32[64,1,896]{2,1,0:T(1,128)} %refs_25_.3) | copy-start | bytes 688132
  258.2 156.8 %copy-start.11 = (f32[96,512]{1,0:T(8,128)S(1)}, f32[96,512]{1,0:T(8,128)}, u32[]{:S(2)}) copy-start(f32[96,512]{1,0:T(8,128)} %refs_17_.3) | copy-start | bytes 589828
  258.2 156.8 %copy-start.12 = (f32[96,512]{1,0:T(8,128)S(1)}, f32[96,512]{1,0:T(8,128)}, u32[]{:S(2)}) copy-start(f32[96,512]{1,0:T(8,128)} %refs_24_.3) | copy-start | bytes 589828
  258.2 156.8 %copy-start.20 = (f32[7,160]{1,0:T(8,128)S(1)}, f32[7,160]{1,0:T(8,128)}, u32[]{:S(2)}) copy-start(f32[7,160]{1,0:T(8,128)} %refs_13_.3) | copy-start | bytes 13444
  258.2 156.8 %copy-start.21 = (f32[7,160]{1,0:T(8,128)S(1)}, f32[7,160]{1,0:T(8,128)}, u32[]{:S(2)}) copy-start(f32[7,160]{1,0:T(8,128)} %refs_20_.3) | copy-start | bytes 13444
  258.2 156.8 %copy-start.22 = (f32[7,160]{1,0:T(8,128)S(1)}, f32[7,160]{1,0:T(8,128)}, u32[]{:S(2)}) copy-start(f32[7,160]{1,0:T(8,128)} %refs_27_.3) | copy-start | bytes 13444
  415.0 0.9 copy-start.13
  416.0 0.9 copy-start.14
  416.9 1.0 copy-start.15
  417.9 1.0 copy-start.16
  418.9 0.9 copy-start.17
  419.8 0.9 copy-start.18
  420.8 0.9 copy-start.19
  421.7 0.7 copy-start.23
  (1 other events, 0.7 us)

commit v5 on v4

--- a/solution.py
+++ b/solution.py
@@ -60,17 +60,19 @@
 
 def greet(z, x, y, c):
     barrier = pltpu.get_barrier_semaphore()
-    peers = [
-        device(z, x, y, 1 - c),
-        device(z, x, 1 - y, c),
-        device(z, 1 - x, y, c),
-        device(flip(z, 1), x, y, c),
-        device(flip(z, 2), x, y, c),
-        device(flip(z, 3), x, y, c),
-    ]
+    peers = [device(flip(z, m), x, y, c) for m in (1, 2, 3)]
+    for m in range(1, 8):
+        peers.append(
+            device(
+                z,
+                1 - x if m // 4 else x,
+                1 - y if (m // 2) % 2 else y,
+                1 - c if m % 2 else c,
+            )
+        )
     for peer in peers:
         pl.semaphore_signal(barrier, inc=1, device_id=peer, device_id_type=MESH_ID)
-    pl.semaphore_wait(barrier, 6)
+    pl.semaphore_wait(barrier, len(peers))
 
 
 SHARED = (PIX, BRI)
@@ -90,13 +92,22 @@
 
 GATHER_STEPS = (
     ((VEC, 0, 8, 0), (PIX, 0, 24, 0), (PIX, 24, 16, 1)),
-    ((EIN, 0, 32, 0), (EIN, 32, 16, 1)),
-    ((EIN, 48, 16, 0), (EIN, 64, 32, 1)),
-    ((EOUT, 0, 32, 0), (EOUT, 32, 32, 1)),
-    ((EOUT, 64, 32, 0), (EOUT, 96, 24, 1), (BRI, 0, 16, 1), (BRI, 16, 8, 0)),
-    ((DIN, 0, 32, 0), (DIN, 32, 32, 1)),
-    ((DOUT, 0, 48, 0), (DOUT, 48, 32, 1)),
+    ((EIN, 0, 16, 0), (EIN, 16, 16, 1)),
+    ((EIN, 32, 16, 0), (EIN, 48, 16, 1)),
+    ((EIN, 64, 16, 0), (EIN, 80, 16, 1)),
+    ((EOUT, 0, 24, 0), (EOUT, 24, 24, 1)),
+    ((EOUT, 48, 24, 0), (EOUT, 72, 24, 1)),
+    ((EOUT, 96, 8, 0), (EOUT, 104, 16, 1), (BRI, 0, 16, 0), (BRI, 16, 8, 1)),
+    ((DIN, 0, 16, 0), (DIN, 16, 16, 1)),
+    ((DIN, 32, 16, 0), (DIN, 48, 16, 1)),
+    ((DOUT, 0, 16, 0), (DOUT, 16, 32, 1)),
+    ((DOUT, 48, 16, 0), (DOUT, 64, 16, 1)),
 )
+DEPTH = 4
+
+
+def last_step(steps, array):
+    return max(at for at, step in enumerate(steps) for unit in step if unit[0] == array)
 
 
 def gather_ticks(parts, outs, send, recv, local):
@@ -185,14 +196,21 @@
 
 
 SCATTER_STEPS = (
-    ((DOUT, 0, 48, 0), (DOUT, 48, 32, 1)),
-    ((BRI, 0, 8, 0), (BRI, 8, 16, 1), (DIN, 0, 32, 0), (DIN, 32, 32, 1)),
+    ((BRI, 0, 8, 0), (BRI, 8, 16, 1)),
     ((PIX, 0, 24, 0), (PIX, 24, 16, 1)),
-    ((EOUT, 0, 32, 0), (EOUT, 32, 32, 1)),
-    ((EOUT, 64, 32, 0), (EOUT, 96, 24, 1)),
-    ((EIN, 0, 32, 0), (EIN, 32, 16, 1)),
-    ((EIN, 48, 16, 0), (EIN, 64, 32, 1)),
+    ((EIN, 0, 16, 0), (EIN, 16, 16, 1)),
+    ((EIN, 32, 16, 0), (EIN, 48, 16, 1)),
+    ((EIN, 64, 16, 0), (EIN, 80, 16, 1)),
+    ((EOUT, 0, 24, 0), (EOUT, 24, 24, 1)),
+    ((EOUT, 48, 24, 0), (EOUT, 72, 24, 1)),
+    ((EOUT, 96, 8, 0), (EOUT, 104, 16, 1)),
+    ((DIN, 0, 16, 0), (DIN, 16, 16, 1)),
+    ((DIN, 32, 16, 0), (DIN, 48, 16, 1)),
+    ((DOUT, 0, 24, 0), (DOUT, 24, 24, 1)),
+    ((DOUT, 48, 16, 0), (DOUT, 64, 16, 1)),
 )
+
+
 STAT_LANES = {EIN: 0, EOUT: 1, DIN: 2, DOUT: 3, PIX: 4, BRI: 5, VEC: 6}
 
 
@@ -232,8 +250,8 @@
     n = len(units)
     own, one, two, three, four = (refs[k * n : (k + 1) * n] for k in range(5))
     vec_one, vec_two, vec_three, vec_four, vec_sum = refs[5 * n : 5 * n + 5]
-    stats, stat_one, stat_two, stat_three, stat_four = refs[5 * n + 5 : 5 * n + 10]
-    send, recv, local, vsend, vrecv, tsend, trecv, ssend, srecv = refs[5 * n + 10 :]
+    stats, stat_one, stat_four = refs[5 * n + 5 : 5 * n + 8]
+    send, recv, local, vsend, vrecv, tsend, trecv, ssend, srecv = refs[5 * n + 8 :]
     z, x, y, c = place()
     every = slice(None)
     copies = {}
@@ -442,19 +460,30 @@
                 tally(array)
             elif array not in SHARED and tick == last + 4:
                 tally(array)
-    stat_peers = (device(z, x, y, 1 - c), device(z, 1 - x, y, c), device(z, x, 1 - y, c))
-    for stage, (held, peer) in enumerate(zip((stat_one, stat_two, stat_three), stat_peers)):
-        remote(stats, held, ("s", stage), ssend.at[stage], srecv.at[stage], peer)
-        copies["s", stage].wait()
-        stats[...] = stats[...] + held[...]
-    stat_four[z] = stats[...]
+    here = (x * 2 + y) * 2 + c
+    stat_one[here] = stats[...]
+    for m in range(1, 8):
+        peer = device(
+            z,
+            1 - x if m // 4 else x,
+            1 - y if (m // 2) % 2 else y,
+            1 - c if m % 2 else c,
+        )
+        remote(stats, stat_one.at[here], ("p", m), ssend.at[m], srecv.at[m], peer)
+    for m in range(1, 8):
+        copies["p", m].wait()
+    total = stat_one[0]
+    for slot in range(1, 8):
+        total = total + stat_one[slot]
+    stats[...] = total
+    stat_four[z] = total
     for m in (1, 2, 3):
         remote(
             stats,
             stat_four.at[z],
             ("s", 2 + m),
-            ssend.at[2 + m],
-            srecv.at[2 + m],
+            ssend.at[7 + m],
+            srecv.at[7 + m],
             device(flip(z, m), x, y, c),
         )
     for m in (1, 2, 3):
@@ -493,7 +522,7 @@
             scratch.append(pltpu.VMEM(lead + (size, shapes[array][5]), bf16))
     vec = grads[6].shape
     scratch += [pltpu.VMEM(vec, f32)] * 3 + [pltpu.VMEM((4,) + vec, f32), pltpu.VMEM(vec, f32)]
-    scratch += [pltpu.VMEM((8, 128), f32)] * 4 + [pltpu.VMEM((4, 8, 128), f32)]
+    scratch += [pltpu.VMEM(lead + (8, 128), f32) for lead in ((), (8,), (4,))]
     scratch += [
         pltpu.SemaphoreType.DMA((n, 6)),
         pltpu.SemaphoreType.DMA((n, 6)),
@@ -502,8 +531,8 @@
         pltpu.SemaphoreType.DMA((6,)),
         pltpu.SemaphoreType.DMA((6,)),
         pltpu.SemaphoreType.DMA((6,)),
-        pltpu.SemaphoreType.DMA((6,)),
-        pltpu.SemaphoreType.DMA((6,)),
+        pltpu.SemaphoreType.DMA((11,)),
+        pltpu.SemaphoreType.DMA((11,)),
     ]
     total = sum(int(grad.size) * grad.dtype.itemsize for grad in grads)
     return pl.pallas_call(
@@ -522,11 +551,27 @@
 
 
 def apply_kernel(*refs):
-    grads, masters, firsts, seconds = (refs[7 * k : 7 * k + 7] for k in range(4))
-    stats = refs[28]
-    next_firsts, next_seconds, news = (refs[29 + 7 * k : 36 + 7 * k] for k in range(3))
-    loss, pairs = refs[50:]
-    for array in range(7):
+    sources, stats = refs[:28], refs[28]
+    targets = refs[29:50]
+    loss, pairs = refs[50:52]
+    held = refs[52:80]
+    results = refs[80:101]
+    loaded, stored = refs[101:]
+    loads = [
+        pltpu.make_async_copy(source, target, loaded.at[at])
+        for at, (source, target) in enumerate(zip(sources, held))
+    ]
+    order = (EIN, EOUT, DIN, DOUT, PIX, BRI, VEC)
+    for array in order:
+        for kind in range(4):
+            loads[7 * kind + array].start()
+    grads, masters, firsts, seconds = (held[7 * k : 7 * k + 7] for k in range(4))
+    next_firsts, next_seconds, news = (results[7 * k : 7 * k + 7] for k in range(3))
+    stores = [
+        pltpu.make_async_copy(source, target, stored.at[at])
+        for at, (source, target) in enumerate(zip(results, targets))
+    ]
+    for array in order:
         lane = STAT_LANES[array]
         norms = [stats[row : row + 1, :][:, lane : lane + 1] for row in range(2)]
         ratio = learn_rate * norms[0] / norms[1]
@@ -552,23 +597,37 @@
             put_rows(next_seconds[array], rows, next_two)
             put_rows(news[array], rows, master - ratio * update)
 
+        for kind in range(4):
+            loads[7 * kind + array].wait()
         if array == VEC:
             body(slice(None))
         else:
             row_loop(count, state_step(count), body)
+        for kind in range(3):
+            stores[7 * kind + array].start()
     pairs[...] = stats[:2, :][:, :7]
     loss[...] = stats[2:3, :][:, :1]
+    for store in stores:
+        store.wait()
 
 
 def apply_update(reduced, masters, firsts, seconds, stats):
     shapes = [jax.ShapeDtypeStruct(master.shape, f32) for master in masters]
+    operands = [*reduced, *masters, *firsts, *seconds]
+    in_vmem = pl.BlockSpec(memory_space=pltpu.VMEM)
+    anywhere = pl.BlockSpec(memory_space=pl.ANY)
     results = pl.pallas_call(
         apply_kernel,
         out_shape=shapes * 3
         + [jax.ShapeDtypeStruct((1, 1), f32), jax.ShapeDtypeStruct((2, 7), f32)],
-        compiler_params=pltpu.CompilerParams(vmem_limit_bytes=48 * 1024 * 1024),
+        in_specs=[anywhere] * 28 + [in_vmem],
+        out_specs=[anywhere] * 21 + [in_vmem] * 2,
+        scratch_shapes=[pltpu.VMEM(member.shape, f32) for member in operands]
+        + [pltpu.VMEM(master.shape, f32) for master in masters] * 3
+        + [pltpu.SemaphoreType.DMA((28,)), pltpu.SemaphoreType.DMA((21,))],
+        compiler_params=pltpu.CompilerParams(vmem_limit_bytes=60 * 1024 * 1024),
         name="apply_update",
-    )(*reduced, *masters, *firsts, *seconds, stats)
+    )(*operands, stats)
     return results[:7], results[7:14], results[14:21], results[21].reshape(()), results[22]
 
 
@@ -689,6 +748,7 @@
 
         body(slice(None))
 
+    yield "projected"
     scale = dims["head"] ** (-0.5)
 
     @pl.loop(0, GROUPS * dims["spans"])
@@ -1088,12 +1148,18 @@
         parts[VEC][7:8, :] = count_row[...]
         ticks = gather_ticks(parts, wholes, send, recv, local)
 
-    def advance(times):
-        if ring:
-            for _ in range(times):
-                next(ticks)
-
-    advance(5)
+    done = [-1]
+
+    def until(tick):
+        while ring and done[0] < tick:
+            next(ticks)
+            done[0] += 1
+
+    at_embed, at_in, at_out = (
+        last_step(GATHER_STEPS, array) + DEPTH for array in (PIX, EIN, EOUT)
+    )
+    at_end = len(GATHER_STEPS) - 1 + DEPTH
+    until(at_embed)
     embed_copy = load(0, PIX, embed)
     if ring:
         vec_copy = pltpu.make_async_copy(wholes[VEC], vec_parts, loaded.at[1])
@@ -1120,21 +1186,24 @@
         stream[rows] = jnp.where(at == CLASS_ROW, vectors[0:1, :], start)
 
     flush(0)
-    advance(2)
+    until(at_in)
     load(2, EIN, w_in).wait()
     layer = layer_forward_rows(dims, stream, w_in, w_out, vectors, saved + work)
     next(layer)
+    until(at_in + 1)
+    next(layer)
     flush(4, 5, 6, 7, 8, 9)
-    advance(2)
+    until(at_out)
     bridge_copy = load(1, BRI, bridge)
     load(3, EOUT, w_out).wait()
     assemble(EOUT, w_out)
     next(layer)
     flush(10, 11, 12)
-    advance(1)
+    until(at_out + 1)
     for _ in layer:
         pass
     flush(13, 14)
+    until(at_out + 2)
     norm_rows(stream, vectors[5:6, :], vectors[6:7, :], unit, inverse, low, dims["step"])
     flush(1, 2, 3)
     bridge_copy.wait()
@@ -1145,7 +1214,7 @@
         rows = pl.ds(pl.multiple_of(b * block, block), block)
         projected[b] = dot(low[rows], bridge[...])
 
-    advance(2)
+    until(at_end + 1)
     for copy in flushes:
         copy.wait()
 

time: 432 us -> 397 us (0.919)
  Pallas kernels: 412 us -> 386 us
  local copies, waits for them, and re-layouts: 14.2 us -> 6.14 us
    pallas_call x1, Pallas kernels: 157 us -> 138 us  [scatter_gradients(): pl.pallas_call(functools.partial(scatter_kernel, shapes, units), out_shap...]
    unnamed x51 -> x1, local copies, waits for them, and re-layouts: 9.25 us -> 1.17 us
    pallas_call x1, Pallas kernels: 138 us -> 130 us  [encode(): pl.pallas_call(functools.partial(encode_kernel, ring), out_shape=[jax.Sha...]
where the time goes in v5:
time: 397 us
  Pallas kernels  386 us (97%)
  local copies, waits for them, and re-layouts  6.14 us (2%)
    pallas_call x1, Pallas kernels, scatter_gradients(): pl.pallas_call(functools.partial(scatter_kernel, shapes, units), out_shap...  138 us
    pallas_call x1, Pallas kernels, encode(): pl.pallas_call(functools.partial(encode_kernel, ring), out_shape=[jax.Sha...  130 us
    pallas_call x1, Pallas kernels, decoder_step(): pl.pallas_call(decoder_kernel, out_shape=outs, in_specs=[in_vmem, in_vmem...  77.3 us
    pallas_call x1, Pallas kernels, encoder_backward(): pl.pallas_call(encoder_backward_kernel, out_shape=outs, scratch_shapes=[p...  33 us

profile of v5, /device:TPU:0, one launch (start us, length us, event | category | flops | bytes accessed | tf_op | source)
XLA Modules:
  0.0 396.8 jit_solution(2955625971770240235)
XLA Ops:
  0.7 0.7 convert_element_type.7
  1.3 1.4 multiply_reduce_fusion
  2.7 1.2 broadcast_in_dim.20.refs_10_
  3.9 0.7 pad.9
  4.6 0.7 compare_select_fusion
  5.4 0.7 stack_broadcast_in_dim.2
  6.2 0.6 fusion.refs_1_
  6.8 2.3 constant_dynamic-slice_fusion
  9.1 1.2 copy.52.refs_0_.refs_2_
  10.3 129.6 %gather_encode.1 = (bf16[4,2,2,2,40,768]{5,4,3,2,1,0:T(8,128)(2,1)}, bf16[2,2,4,2,96,1344]{5,4,3,2,1,0:T(8,128)(2,1)}, bf16[2,2,4,2,120,768]{5,4,3,2,1,0:T(8,128...) custom-call(bf16[4,196,768]{2,1,0:T(8,128)(2,1)} %copy.52.refs_0_.re, ...), custom_call_target="tpu_custom_call" | custom-call | tf_op jit(solution)/shard_map/gather_encode/pallas_call | solution.py:1283
  139.9 77.3 %decoder_step.1 = (bf16[4,512,896]{2,1,0:T(8,128)(2,1)}, bf16[4,640,512]{2,1,0:T(8,128)(2,1)}, bf16[512,768]{1,0:T(8,128)(2,1)}, bf16[4,64,512]{2,1,0:T(8,128)(2,1)}, f32[8,512]{1,0:T(8,128)}) custom-call(f32[4,64,512]{2,1,0:T(8,128)} %get-tuple-element.87.refs_0_, s32[4,3,256]{2,1,0:T(4,128)} %fusion.refs_1_, bf16[4,196,768]{2,1,0:T(8,128)(2,1)} %copy.52.refs_0_.refs_2_, ...), custom_call_target="tpu_custom_call" | custom-call | tf_op jit(solution)/shard_map/decoder_step/pallas_call | solution.py:1044
  217.2 33.0 %encoder_backward.1 = (bf16[4,768,1344]{2,1,0:T(8,128)(2,1)}, bf16[4,960,768]{2,1,0:T(8,128)(2,1)}, bf16[768,512]{1,0:T(8,128)(2,1)}, bf16[1280,768]{1,0:T(8,128)(2,1)}, f32[8,8,256]{2,1,0:T(8,128)}) custom-call(bf16[4,64,512]{2,1,0:T(8,128)(2,1)} %get-tuple-element.92.refs_0_, bf16[256,768]{1,0:T(8,128)(2,1)} %get-tuple-element.93.refs_1_, ...), custom_call_target="tpu_custom_call" | custom-call | tf_op jit(solution)/shard_map/encoder_backward/pallas_call | solution.py:1361
  250.2 138.5 %scatter_gradients.1 = (f32[4,40,768]{2,1,0:T(8,128)}, f32[96,1344]{1,0:T(8,128)}, f32[120,768]{1,0:T(8,128)}, f32[4,24,512]{2,1,0:T(8,128)}, f32[64,896]{1,0:T(...) custom-call(bf16[4,2,2,2,40,768]{5,4,3,2,1,0:T(8,128)(2,1)} %bitcast.23, ...), custom_call_target="tpu_custom_call" | custom-call | bytes 46530560 | tf_op jit(solution)/shard_map/scatter_gradients/pallas_call | solution.py:538
  388.7 7.9 %apply_update.1 = (f32[160,768]{1,0:T(8,128)}, f32[96,1,1344]{2,1,0:T(1,128)}, f32[1,120,768]{2,1,0:T(8,128)}, f32[96,512]{1,0:T(8,128)}, f32[64,1,896]{2,1,0:T(...) custom-call(f32[160,768]{1,0:T(8,128)} %bitcast.27, ...), custom_call_target="tpu_custom_call" | custom-call | tf_op jit(solution)/shard_map/apply_update/pallas_call | solution.py:619
  (4 shorter events, 0.0 us)

commit v6 on v5

--- a/solution.py
+++ b/solution.py
@@ -664,8 +664,14 @@
     return dot(left, right, ((1,), (1,)))
 
 
-def exact_dot(left, right, dims):
-    return dot(left, right, dims, lax.Precision.HIGHEST)
+def exact_pick(choice, values, dims):
+    total = None
+    for _ in range(3):
+        part = values.astype(bf16)
+        values = values - part.astype(f32)
+        product = dot(choice, part, dims)
+        total = product if total is None else total + product
+    return total
 
 
 def row_loop(count, step, body):
@@ -810,7 +816,9 @@
         pl.loop(half, GROUPS)(feed)
 
 
-def layer_backward_rows(dims, given, spare, w_in, w_out, vectors, saved, low, flow, grad_in, grad_out, sums):
+def layer_backward_rows(
+    dims, given, spare, w_in, w_out, vectors, saved, low, flow, turned, grad_in, grad_out, sums, need, ready
+):
     unit_one, inv_one, low_one, qkv, probs, mixed, unit_two, inv_two, low_two, active, slope, work, low_work, low_more = saved
     count, width = given.shape
     inner = dims["heads"] * dims["head"]
@@ -822,6 +830,8 @@
         spare[rows] = jnp.zeros_like(spare[rows])
 
     row_loop(count, 32, lower)
+    need("low_two", "active", "slope", "w_out", "w_in")
+    turned[...] = low_two[...].T
 
     @pl.loop(0, GROUPS)
     def _(t):
@@ -834,12 +844,13 @@
             spare[rows] = spare[rows] + dot_nt(flow[rows], up)
 
         body(slice(None))
-        grad_up = dot_t(low_two[...], flow[...]).astype(bf16)
+        grad_up = dot(turned[...], flow[...]).astype(bf16)
         if aligned:
             grad_in[t, :, 3 * inner :] = grad_up
         else:
             grad_in[t] = jnp.concatenate([jnp.zeros((width, 3 * inner), bf16), grad_up], axis=1)
 
+    need("unit_two", "inv_two", "mixed")
     norm_back_rows(spare, unit_two, inv_two, vectors[3:4, :], given, given, sums, 3, dims["step"])
     row_loop(count, 32, lower)
 
@@ -848,10 +859,10 @@
         weights = w_out[t, :inner]
         grad_out[t, :inner] = dot_t(mixed[t], low[...]).astype(bf16)
 
-        def body(rows):
-            mixed[t, rows] = dot_nt(low[rows], weights).astype(bf16)
-
-        body(slice(None))
+        mixed[t] = dot_nt(low[...], weights).astype(bf16)
+        ready("out", t)
+
+    need("qkv", "probs")
 
     scale = dims["head"] ** (-0.5)
 
@@ -883,19 +894,20 @@
         grad_query = jnp.concatenate(parts[0], axis=0).T
         qkv[t, rows] = jnp.concatenate([grad_query] + parts[1] + parts[2], axis=1).astype(bf16)
 
+    need("low_one", "unit_one", "inv_one")
+    turned[...] = low_one[...].T
+
     @pl.loop(0, GROUPS)
     def _(t):
         weights = w_in[t, :, : 3 * inner] if aligned else w_in[t][:, : 3 * inner]
-        grad_triple = dot_t(low_one[...], qkv[t]).astype(bf16)
+        grad_triple = dot(turned[...], qkv[t]).astype(bf16)
         if aligned:
             grad_in[t, :, : 3 * inner] = grad_triple
         else:
             grad_in[t] = jnp.concatenate([grad_triple, grad_in[t][:, 3 * inner :]], axis=1)
 
-        def body(rows):
-            spare[rows] = spare[rows] + dot_nt(qkv[t, rows], weights)
-
-        body(slice(None))
+        ready("in", t)
+        spare[...] = spare[...] + dot_nt(qkv[t], weights)
 
     norm_back_rows(spare, unit_one, inv_one, vectors[1:2, :], given, given, sums, 1, dims["step"])
 
@@ -925,35 +937,66 @@
     return [(shape, f32), (shape, bf16), (shape, bf16)]
 
 
+SAVED = (
+    "unit_one", "inv_one", "low_one", "qkv", "probs", "mixed",
+    "unit_two", "inv_two", "low_two", "active", "slope",
+)
+
+
+def loader(names, sources, targets, semaphores):
+    copies = {}
+    for at, (name, source, target) in enumerate(zip(names, sources, targets)):
+        copies[name] = pltpu.make_async_copy(source, target, semaphores.at[at])
+        copies[name].start()
+
+    def need(*wanted):
+        for name in wanted:
+            if name in copies:
+                copies.pop(name).wait()
+
+    return need
+
+
+def storer(held, outs, semaphores):
+    def ready(kind, t):
+        at = ("in", "out").index(kind)
+        pltpu.make_async_copy(held[at].at[t], outs[at].at[t], semaphores.at[at]).start()
+
+    def finish():
+        for at in range(2):
+            pltpu.make_async_copy(held[at], outs[at], semaphores.at[at]).wait()
+
+    return ready, finish
+
+
 def token_gain(vectors, dims):
     return vectors.at[:, pl.ds(dims["first"], dims["width"])]
 
 
 def decoder_kernel(*refs):
-    projected, codes, images, table, w_in, w_out, pixel_w, vectors_all = refs[:8]
-    grad_in, grad_out, grad_head, grad_projected, vec_out = refs[8:13]
-    stream, given, unit, inverse, low, flow, sums, loss, head, pixels_here, head_sum, loaded = refs[13:25]
-    saved = refs[25:]
+    projected, codes, images, table, w_in_all, w_out_all, pixel_w, vectors_all = refs[:8]
+    grad_in_all, grad_out_all, grad_head, grad_projected, vec_out = refs[8:13]
+    stream, given, unit, inverse, low, flow, sums, loss, head, pixels_here, head_sum = refs[13:24]
+    w_in, w_out, grad_in, grad_out, turned, loaded, stored = refs[24:31]
+    saved = refs[31:]
     dims = DEC
     vectors = token_gain(vectors_all, dims)
     count, width = stream.shape
     block = dims["block"]
-    copies = [pltpu.make_async_copy(pixel_w.at[pl.ds(PATCH_DIM, width)], head, loaded.at[0])]
-    for b in range(dims["images"]):
-        copies.append(
-            pltpu.make_async_copy(
-                images.at[b], pixels_here.at[b], loaded.at[1 + b]
-            )
-        )
-    for copy in copies:
-        copy.start()
+    need = loader(
+        ("w_in", "w_out", "head", "images"),
+        (w_in_all, w_out_all, pixel_w.at[pl.ds(PATCH_DIM, width)], images),
+        (w_in, w_out, head, pixels_here),
+        loaded,
+    )
+    ready, finish = storer((grad_in, grad_out), (grad_in_all, grad_out_all), stored)
     sums[...] = jnp.zeros_like(sums)
     loss[...] = jnp.zeros_like(loss)
 
     def placer(b):
         return (
             lax.broadcasted_iota(jnp.int32, (64, block), 0) == codes[b][:1, :block]
-        ).astype(f32)
+        ).astype(bf16)
 
     def block_rows(b):
         return pl.ds(pl.multiple_of(b * block, block), block)
@@ -963,13 +1006,13 @@
         at = lax.broadcasted_iota(jnp.int32, (64, width), 0)
         source = jnp.where(at == MASK_ROW, vectors[0:1, :], projected[b])
         source = jnp.where(at > MASK_ROW, 0.0, source)
-        stream[block_rows(b)] = exact_dot(placer(b), source, ((0,), (0,))) + table[...]
-
+        stream[block_rows(b)] = exact_pick(placer(b), source, ((0,), (0,))) + table[...]
+
+    need("w_in", "w_out")
     for _ in layer_forward_rows(dims, stream, w_in, w_out, vectors, saved):
         pass
     norm_rows(stream, vectors[5:6, :], vectors[6:7, :], unit, inverse, low, dims["step"])
-    for copy in copies:
-        copy.wait()
+    need("head", "images")
     head_sum[...] = jnp.zeros_like(head_sum)
     pixels_wide = pixels_here.shape[-1]
     counted = vectors_all[7:8, :]
@@ -979,16 +1022,13 @@
     def _(b):
         rows = block_rows(b)
         predicted = dot(low[rows], head[...])
-        pixels = jnp.concatenate(
-            [pixels_here[b], jnp.zeros((block - IMAGE_PATCHES, pixels_wide), bf16)], axis=0
-        ).astype(f32)
+        pixels = pixels_here[b].astype(f32)
         centred = pixels - jnp.mean(pixels, axis=-1, keepdims=True)
         variance = jnp.sum(centred * centred, axis=-1, keepdims=True) / (pixels_wide - 1)
         errors = predicted - centred * lax.rsqrt(variance + eps_norm)
         at = lax.broadcasted_iota(jnp.int32, (64, 128), 0)
-        share = codes[b][2:3, :128].astype(f32) / patch_total
-        spread = jnp.where(at == MASK_ROW, share, 0.0)
-        weight = exact_dot(placer(b), spread, ((0,), (0,)))[:, :1]
+        spread = jnp.where(at == MASK_ROW, codes[b][2:3, :128].astype(f32), 0.0)
+        weight = dot_t(placer(b), spread.astype(bf16))[:, :1] / patch_total
         loss[...] = loss[...] + fold(errors * errors * weight)
         grad_low = (errors * (2.0 / pixels_wide) * weight).astype(bf16)
         head_sum[...] = head_sum[...] + dot_t(low[rows], grad_low)
@@ -997,12 +1037,12 @@
     grad_head[...] = head_sum[...].astype(bf16)
     norm_back_rows(given, unit, inverse, vectors[5:6, :], given, None, sums, 5, dims["step"])
     layer_backward_rows(
-        dims, given, stream, w_in, w_out, vectors, saved, low, flow, grad_in, grad_out, sums
+        dims, given, stream, w_in, w_out, vectors, saved, low, flow, turned, grad_in, grad_out, sums, need, ready
     )
 
     @pl.loop(0, dims["images"])
     def _(b):
-        back = exact_dot(placer(b), given[block_rows(b)], ((1,), (0,)))
+        back = exact_pick(placer(b), given[block_rows(b)], ((1,), (0,)))
         at = lax.broadcasted_iota(jnp.int32, (64, width), 0)
         grad_projected[b] = jnp.where(at < MASK_ROW, back, 0.0).astype(bf16)
         sums[0] = sums[0] + fold(jnp.where(at == MASK_ROW, back, 0.0))
@@ -1011,6 +1051,7 @@
         vec_out[row : row + 1, :] = jnp.sum(sums[row], axis=0, keepdims=True)
     total = jnp.sum(jnp.sum(loss[...], axis=0, keepdims=True), axis=1, keepdims=True)
     vec_out[7:8, :] = jnp.broadcast_to(total / pixels_wide, (1, width))
+    finish()
 
 
 def decoder_step(projected, codes, images, table, w_in, w_out, pixel_w, vectors):
@@ -1034,9 +1075,15 @@
         ((7, 8, width), f32),
         ((8, wide), f32),
         ((width, wide), bf16),
-        ((dims["images"],) + images.shape[1:], bf16),
+        (images.shape, bf16),
         ((width, wide), f32),
-        None,
+        (w_in.shape, bf16),
+        (w_out.shape, bf16),
+        (w_in.shape, bf16),
+        (w_out.shape, bf16),
+        ((width, count), bf16),
+        4,
+        2,
     ]
     scratch += saved_shapes(dims) + work_shapes(dims)
     in_vmem = pl.BlockSpec(memory_space=pltpu.VMEM)
@@ -1044,9 +1091,10 @@
     return pl.pallas_call(
         decoder_kernel,
         out_shape=outs,
-        in_specs=[in_vmem, in_vmem, anywhere, in_vmem, in_vmem, in_vmem, anywhere, in_vmem],
+        in_specs=[in_vmem, in_vmem, anywhere, in_vmem, anywhere, anywhere, anywhere, in_vmem],
+        out_specs=[anywhere, anywhere, in_vmem, in_vmem, in_vmem],
         scratch_shapes=[
-            pltpu.SemaphoreType.DMA((5,)) if shape is None else pltpu.VMEM(*shape)
+            pltpu.SemaphoreType.DMA((shape,)) if isinstance(shape, int) else pltpu.VMEM(*shape)
             for shape in scratch
         ],
         compiler_params=pltpu.CompilerParams(vmem_limit_bytes=62 * 1024 * 1024),
@@ -1056,39 +1104,48 @@
 
 def encode_kernel(ring, *refs):
     dims = ENC
-    images, codes, table = refs[:3]
-    refs = refs[3:]
+    images, keep_index, unshuffle, masked, image_valid, table = refs[:6]
+    refs = refs[6:]
     group = lax.axis_index("tensor")
     if ring:
-        masters, count_row, refs = refs[:7], refs[7], refs[8:]
-        wholes, vectors_all, projected, kept_state = refs[:7], refs[7], refs[8], refs[9:24]
-        refs = refs[24:]
+        masters, refs = refs[:7], refs[7:]
+        wholes, vectors_all, codes, pictures, projected = refs[:7], *refs[7:11]
+        kept_state, refs = refs[11:26], refs[26:]
         parts, send, recv, local, vec_parts = refs[:7], *refs[7:11]
         raw = dict(zip((PIX, EOUT, BRI), refs[11:14]))
         refs = refs[14:]
     else:
         wholes, vectors_all = refs[:4], refs[4]
-        projected, kept_state = refs[5], refs[6:21]
-        refs = refs[21:]
+        codes, pictures, projected, kept_state = refs[5], refs[6], refs[7], refs[8:23]
+        refs = refs[23:]
         wholes = dict(zip((PIX, EIN, EOUT, BRI), wholes))
     loaded, flushed = refs[:2]
-    pixels_here, stream, w_in, w_out, embed, bridge = refs[2:8]
-    retained, unit, inverse, low = refs[8:12]
-    saved = refs[12:23]
-    work = refs[23:]
+    eight, pixels_here, stream, w_in, w_out, embed, bridge = refs[2:9]
+    retained, unit, inverse, low = refs[9:13]
+    saved = refs[13:24]
+    work = refs[24:]
     held = (retained, unit, inverse, low) + tuple(saved)
     vectors = token_gain(vectors_all, dims)
     count, width = stream.shape
     block = dims["block"]
 
-    picture_copies = [
-        pltpu.make_async_copy(
-            images.at[b], pixels_here.at[b], loaded.at[4 + b]
+    first = pl.multiple_of((group // 2) * 8, 8)
+    eight_copy = pltpu.make_async_copy(images.at[:, pl.ds(first, 8)], eight, loaded.at[4])
+    eight_copy.start()
+    lane = lax.broadcasted_iota(jnp.int32, (1, codes.shape[2]), 1)
+    valid = image_valid[...]
+    image_at = lax.broadcasted_iota(jnp.int32, valid.shape, 1)
+    codes[...] = jnp.full(codes.shape, -1, jnp.int32)
+    for b in range(dims["images"]):
+        mine = group * dims["images"] + b
+        row = pl.ds(mine, 1)
+        codes[b, 0:1, :] = jnp.where(lane == IMAGE_PATCHES, CLASS_ROW, -1)
+        codes[b, 0:1, :IMAGE_PATCHES] = jnp.where(masked[row] == 1, MASK_ROW, unshuffle[row])
+        codes[b, 1:2, :KEEP] = keep_index[row]
+        own_valid = jnp.sum(
+            jnp.where(image_at == mine, valid, 0).astype(f32), axis=1, keepdims=True
         )
-        for b in range(dims["images"])
-    ]
-    for copy in picture_copies:
-        copy.start()
+        codes[b, 2:3, :] = jnp.broadcast_to(own_valid, (1, codes.shape[2])).astype(jnp.int32)
 
     def load(slot, array, target):
         if not ring:
@@ -1145,7 +1202,9 @@
         columns = masters[VEC].shape[1]
         parts[VEC][...] = jnp.zeros_like(parts[VEC])
         parts[VEC][:7, :columns] = masters[VEC][...].astype(bf16).astype(f32)
-        parts[VEC][7:8, :] = count_row[...]
+        counts = dot(valid.astype(bf16), masked[...].astype(f32).astype(bf16))
+        counted = jnp.sum(counts, axis=1, keepdims=True)
+        parts[VEC][7:8, :] = jnp.broadcast_to(counted, (1, parts[VEC].shape[1]))
         ticks = gather_ticks(parts, wholes, send, recv, local)
 
     done = [-1]
@@ -1159,6 +1218,22 @@
         last_step(GATHER_STEPS, array) + DEPTH for array in (PIX, EIN, EOUT)
     )
     at_end = len(GATHER_STEPS) - 1 + DEPTH
+    until(0)
+    eight_copy.wait()
+    pixels_wide = eight.shape[2]
+
+    @pl.loop(0, dims["images"])
+    def _(b):
+        size = (pixels_here.shape[1], IMAGE_PATCHES * 8)
+        patch = lax.broadcasted_iota(jnp.int32, size, 0)
+        at = lax.broadcasted_iota(jnp.int32, size, 1)
+        wanted = patch * 8 + (group % 2) * dims["images"] + b
+        choice = (at == wanted) & (patch < IMAGE_PATCHES)
+        flat = eight[...].reshape(IMAGE_PATCHES * 8, pixels_wide)
+        pixels_here[b] = dot(choice.astype(f32).astype(bf16), flat).astype(bf16)
+
+    picture_copy = pltpu.make_async_copy(pixels_here, pictures, loaded.at[5])
+    picture_copy.start()
     until(at_embed)
     embed_copy = load(0, PIX, embed)
     if ring:
@@ -1168,8 +1243,6 @@
         vectors_all[...] = jnp.concatenate(
             [vec_parts[0, 0, k // 2, k % 2][:, :columns] for k in range(8)], axis=1
         )
-    for copy in picture_copies:
-        copy.wait()
     embed_copy.wait()
     assemble(PIX, embed)
 
@@ -1177,10 +1250,10 @@
     def _(b):
         rows = pl.ds(pl.multiple_of(b * block, block), block)
         choice = (
-            lax.broadcasted_iota(jnp.int32, (IMAGE_PATCHES, block), 0) == codes[b][1:2, :block]
+            lax.broadcasted_iota(jnp.int32, (table.shape[0], block), 0) == codes[b][1:2, :block]
         )
         retained[rows] = dot_t(choice.astype(bf16), pixels_here[b]).astype(bf16)
-        places = exact_dot(choice.astype(f32), table[...], ((0,), (0,)))
+        places = exact_pick(choice.astype(bf16), table[...], ((0,), (0,)))
         at = lax.broadcasted_iota(jnp.int32, (block, width), 0)
         start = dot(retained[rows], embed[...]) + places
         stream[rows] = jnp.where(at == CLASS_ROW, vectors[0:1, :], start)
@@ -1215,11 +1288,12 @@
         projected[b] = dot(low[rows], bridge[...])
 
     until(at_end + 1)
+    picture_copy.wait()
     for copy in flushes:
         copy.wait()
 
 
-def encode(images, codes, table, weights, count_row=None, vectors=None):
+def encode(images, indices, table, weights, vectors=None):
     dims = ENC
     ring = vectors is None
     count, width = dims["images"] * dims["block"], dims["width"]
@@ -1227,14 +1301,16 @@
     in_vmem = pl.BlockSpec(memory_space=pltpu.VMEM)
     anywhere = pl.BlockSpec(memory_space=pl.ANY)
     kept_shapes = [
-        ((count, images.shape[-1]), bf16),
+        ((count, images.shape[2]), bf16),
         ((count, width), f32),
         ((count, 1), f32),
         ((count, width), bf16),
     ] + saved_shapes(dims)
-    outs = [((dims["images"], dims["block"], bridge_wide), f32)] + kept_shapes
-    out_specs = [in_vmem] + [anywhere] * len(kept_shapes)
-    in_specs = [anywhere, in_vmem, in_vmem]
+    picture_shape = (dims["images"], DEC["block"], images.shape[2])
+    outs = [((dims["images"], 8, 256), jnp.int32), (picture_shape, bf16)]
+    outs += [((dims["images"], dims["block"], bridge_wide), f32)] + kept_shapes
+    out_specs = [in_vmem, anywhere, in_vmem] + [anywhere] * len(kept_shapes)
+    in_specs = [anywhere] + [in_vmem] * 5
     scratch = []
     if ring:
         shapes = []
@@ -1243,8 +1319,8 @@
             shapes.append((rows // 4 if array in SHARED else rows, wide))
         shapes.append((8, 256))
         types = [bf16] * 6 + [f32]
-        operands = [images, codes, table, *weights, count_row]
-        in_specs += [in_vmem] * 8
+        operands = [images, *indices, table, *weights]
+        in_specs += [in_vmem] * 7
         gathered = [(whole_shape(k, shape), types[k]) for k, shape in enumerate(shapes)]
         outs = gathered + [((8, shapes_total(weights[VEC])), f32)] + outs
         out_specs = [anywhere] * 7 + [in_vmem] + out_specs
@@ -1265,13 +1341,14 @@
             (GROUPS, 8 * shapes[EOUT][0], shapes[EOUT][1]),
         ]
     else:
-        operands = [images, codes, table] + [weights[k] for k in (PIX, EIN, EOUT, BRI)] + [vectors]
+        operands = [images, *indices, table] + [weights[k] for k in (PIX, EIN, EOUT, BRI)] + [vectors]
         in_specs += [anywhere] * 4 + [in_vmem]
         params = {}
         w_shapes = [weights[EIN].shape, weights[EOUT].shape]
     scratch += [pltpu.SemaphoreType.DMA((8,)), pltpu.SemaphoreType.DMA((15,))]
     buffers = [
-        ((dims["images"],) + images.shape[1:], bf16),
+        ((images.shape[0], 8, images.shape[2]), bf16),
+        (picture_shape, bf16),
         ((count, width), f32),
         (w_shapes[0], bf16),
         (w_shapes[1], bf16),
@@ -1296,28 +1373,37 @@
 
 
 def encoder_backward_kernel(*refs):
-    grad_projected, retained, unit, inverse, low_end = refs[:5]
-    saved = list(refs[5:16])
-    w_in, w_out, bridge, vectors_all, grad_head, dec_sums = refs[16:22]
-    grad_in, grad_out, grad_bridge, grad_pixel, packed = refs[22:27]
-    given, spare, low, flow, sums, qkv, mixed, vec_all = refs[27:35]
+    grad_projected = refs[0]
+    sources = refs[1:18]
+    bridge, vectors_all, grad_head, dec_sums = refs[18:22]
+    grad_in_all, grad_out_all, grad_bridge, grad_pixel, packed = refs[22:27]
+    given, spare, low, flow, sums, vec_all, turned = refs[27:34]
+    held = refs[34:51]
+    grad_in, grad_out, loaded, stored = refs[51:55]
+    names = ("retained", "unit", "inverse", "low_end") + SAVED + ("w_in", "w_out")
+    order = (3, 1, 2, 12, 13, 14, 16, 15, 10, 11, 9, 7, 8, 6, 4, 5, 0)
+    need = loader(
+        [names[k] for k in order], [sources[k] for k in order], [held[k] for k in order], loaded
+    )
+    ready, finish = storer((grad_in, grad_out), (grad_in_all, grad_out_all), stored)
+    retained, unit, inverse, low_end = held[:4]
+    saved = held[4:15] + refs[55:]
+    w_in, w_out = held[15:17]
     dims = ENC
     vectors = token_gain(vectors_all, dims)
     count, width = given.shape
     block = dims["block"]
     sums[...] = jnp.zeros_like(sums)
-    qkv[...] = saved[3][...]
-    mixed[...] = saved[5][...]
-    saved[3], saved[5] = qkv, mixed
-    saved += refs[35:]
-
+
+    need("low_end", "unit", "inverse")
     flat = grad_projected[...].reshape(count, grad_projected.shape[-1])
     grad_bridge[...] = dot_t(low_end[...], flat).astype(bf16)
     given[...] = dot_nt(flat, bridge[...])
     norm_back_rows(given, unit, inverse, vectors[5:6, :], given, None, sums, 5, dims["step"])
     layer_backward_rows(
-        dims, given, spare, w_in, w_out, vectors, saved, low, flow, grad_in, grad_out, sums
+        dims, given, spare, w_in, w_out, vectors, saved, low, flow, turned, grad_in, grad_out, sums, need, ready
     )
+    need("retained")
     grad_pixel[:PATCH_DIM] = dot_t(retained[...], given[...].astype(bf16)).astype(bf16)
     grad_pixel[PATCH_DIM:] = grad_head[...]
 
@@ -1334,12 +1420,12 @@
     packed[...] = jnp.zeros_like(packed)
     for k in range(8):
         packed[k, :, :columns] = vec_all[:, k * columns : (k + 1) * columns]
+    finish()
 
 
 def encoder_backward(grad_projected, kept_state, w_in, w_out, bridge, vectors, grad_head, dec_sums):
     dims = ENC
     count, width = dims["images"] * dims["block"], dims["width"]
-    shapes = saved_shapes(dims)
     pixels_wide = kept_state[0].shape[1]
     outs = [
         jax.ShapeDtypeStruct(w_in.shape, bf16),
@@ -1354,14 +1440,23 @@
         ((count, width), bf16),
         ((count, dims["hidden"]), bf16),
         ((7, 8, width), f32),
-        shapes[3],
-        shapes[5],
         (vectors.shape, f32),
-    ] + work_shapes(dims)
+        ((width, count), bf16),
+    ]
+    kept_shapes = [(member.shape, member.dtype) for member in kept_state]
+    scratch += kept_shapes + [(w_in.shape, bf16), (w_out.shape, bf16)]
+    scratch += [(w_in.shape, bf16), (w_out.shape, bf16), 17, 2] + work_shapes(dims)
+    in_vmem = pl.BlockSpec(memory_space=pltpu.VMEM)
+    anywhere = pl.BlockSpec(memory_space=pl.ANY)
     return pl.pallas_call(
         encoder_backward_kernel,
         out_shape=outs,
-        scratch_shapes=[pltpu.VMEM(shape, dtype) for shape, dtype in scratch],
+        in_specs=[in_vmem] + [anywhere] * 17 + [in_vmem] * 4,
+        out_specs=[anywhere] * 2 + [in_vmem] * 3,
+        scratch_shapes=[
+            pltpu.SemaphoreType.DMA((shape,)) if isinstance(shape, int) else pltpu.VMEM(*shape)
+            for shape in scratch
+        ],
         compiler_params=pltpu.CompilerParams(vmem_limit_bytes=62 * 1024 * 1024),
         name="encoder_backward",
     )(grad_projected, *kept_state, w_in, w_out, bridge, vectors, grad_head, dec_sums)
@@ -1467,33 +1562,17 @@
 ):
     masters, firsts, seconds = state[:7], state[7:14], state[14:21]
     tensor_count = lax.axis_size("tensor")
-    tensor_at = lax.axis_index("tensor")
-    counted = jnp.sum(masked.astype(f32) * image_valid.astype(f32)[:, None])
-    image_count = images.shape[0] // tensor_count
-    lanes = 256
-    codes = jnp.pad(
-        jnp.where(masked == 1, MASK_ROW, unshuffle),
-        ((0, 0), (0, lanes - IMAGE_PATCHES)),
-        constant_values=-1,
+    enc_table, dec_table = (
+        sinusoid_table(width, GRID_PATCHES, IMAGE_PATCHES, DEC["block"])
+        for width in (ENCODER_WIDTH, D_D)
     )
-    codes = jnp.where(jnp.arange(lanes) == IMAGE_PATCHES, CLASS_ROW, codes)
-    kept = jnp.pad(keep_index, ((0, 0), (0, lanes - KEEP)), constant_values=-1)
-    valid = jnp.broadcast_to(image_valid[:, None], codes.shape)
-    codes = jnp.stack([codes, kept, valid], axis=1)
-    images = lax.dynamic_slice_in_dim(images, tensor_at * image_count, image_count, axis=0)
-    codes = lax.dynamic_slice_in_dim(codes, tensor_at * image_count, image_count, axis=0)
-    enc_table = sinusoid_table(ENCODER_WIDTH, GRID_PATCHES, IMAGE_PATCHES, IMAGE_PATCHES)
-    dec_table = sinusoid_table(D_D, GRID_PATCHES, IMAGE_PATCHES, DEC["block"])
+    indices = (keep_index, unshuffle, masked, image_valid[None, :])
+    by_patch = images.transpose(1, 0, 2)
     if ringed(tensor_count):
         order = (4, 0, 1, 5, 2, 3, 6)
-        results = encode(
-            images,
-            codes,
-            enc_table,
-            [masters[k] for k in order],
-            jnp.broadcast_to(counted, (1, lanes)),
-        )
-        wholes, vectors, projected, enc_state = results[:7], results[7], results[8], results[9:]
+        results = encode(by_patch, indices, enc_table, [masters[k] for k in order])
+        wholes, results = results[:7], results[7:]
+        vectors, codes, pictures, projected, *enc_state = results
         wholes = [
             whole.reshape(-1, whole.shape[-1])
             if array in SHARED
@@ -1501,10 +1580,13 @@
             for array, whole in enumerate(wholes)
         ]
     else:
+        counted = jnp.sum(masked.astype(f32) * image_valid.astype(f32)[:, None])
         wholes, vectors = plain_gather(masters, counted)
-        projected, *enc_state = encode(images, codes, enc_table, wholes, vectors=vectors)
+        codes, pictures, projected, *enc_state = encode(
+            by_patch, indices, enc_table, wholes, vectors=vectors
+        )
     grad_dec_in, grad_dec_out, grad_head, grad_projected, dec_sums = decoder_step(
-        projected, codes, images, dec_table, wholes[DIN], wholes[DOUT], wholes[PIX], vectors
+        projected, codes, pictures, dec_table, wholes[DIN], wholes[DOUT], wholes[PIX], vectors
     )
     grad_enc_in, grad_enc_out, grad_bridge, grad_pixel, packed = encoder_backward(
         grad_projected,

time: 397 us -> 378 us (0.952)
  Pallas kernels: 386 us -> 376 us
  local copies, waits for them, and re-layouts: 6.14 us -> 0 us
    pallas_call x1, Pallas kernels: 33 us -> 26.5 us  [encoder_backward(): pl.pallas_call(encoder_backward_kernel, out_shape=outs, in_specs=[in_vmem...]
where the time goes in v6:
time: 378 us; the launch traced here: 377 us
  Pallas kernels  376 us (99%)
    pallas_call x1, Pallas kernels, scatter_gradients(): pl.pallas_call(functools.partial(scatter_kernel, shapes, units), out_shap...  138 us
    pallas_call x1, Pallas kernels, encode(): pl.pallas_call(functools.partial(encode_kernel, ring), out_shape=[jax.Sha...  131 us
    pallas_call x1, Pallas kernels, decoder_step(): pl.pallas_call(decoder_kernel, out_shape=outs, in_specs=[in_vmem, in_vmem...  73.6 us
    pallas_call x1, Pallas kernels, encoder_backward(): pl.pallas_call(encoder_backward_kernel, out_shape=outs, in_specs=[in_vmem...  26.5 us
    pallas_call x1, Pallas kernels, apply_update(): pl.pallas_call(apply_kernel, out_shape=shapes * 3 + [jax.ShapeDtypeStruct...  7.91 us

profile of v6, /device:TPU:0, one launch (start us, length us, event | category | flops | bytes accessed | tf_op | source)
XLA Modules:
  0.0 377.3 jit_solution(10609653889120055618)
XLA Ops:
  0.7 130.6 %gather_encode.1 = (bf16[4,2,2,2,40,768]{5,4,3,2,1,0:T(8,128)(2,1)}, bf16[2,2,4,2,96,1344]{5,4,3,2,1,0:T(8,128)(2,1)}, bf16[2,2,4,2,120,768]{5,4,3,2,1,0:T(8,128...) custom-call(bf16[196,16,768]{2,1,0:T(8,128)(2,1)} %bitcast.21, ...), custom_call_target="tpu_custom_call" | custom-call | tf_op jit(solution)/shard_map/gather_encode/pallas_call | solution.py:1360
  131.3 73.6 %decoder_step.1 = (bf16[4,512,896]{2,1,0:T(8,128)(2,1)}, bf16[4,640,512]{2,1,0:T(8,128)(2,1)}, bf16[512,768]{1,0:T(8,128)(2,1)}, bf16[4,64,512]{2,1,0:T(8,128)(2,1)}, f32[8,512]{1,0:T(8,128)}) custom-call(f32[4,64,512]{2,1,0:T(8,128)} %get-tuple-element.89.refs_0_, s32[4,8,256]{2,1,0:T(8,128)} %get-tuple-element.90.refs_1_, ...), custom_call_target="tpu_custom_call" | custom-call | tf_op jit(solution)/shard_map/decoder_step/pallas_call | solution.py:1091
  204.8 26.5 %encoder_backward.1 = (bf16[4,768,1344]{2,1,0:T(8,128)(2,1)}, bf16[4,960,768]{2,1,0:T(8,128)(2,1)}, bf16[768,512]{1,0:T(8,128)(2,1)}, bf16[1280,768]{1,0:T(8,128)(2,1)}, f32[8,8,256]{2,1,0:T(8,128)}) custom-call(bf16[4,64,512]{2,1,0:T(8,128)(2,1)} %get-tuple-element.96.refs_0_, bf16[256,768]{1,0:T(8,128)(2,1)} %get-tuple-element.97.refs_1_, ...), custom_call_target="tpu_custom_call" | custom-call | tf_op jit(solution)/shard_map/encoder_backward/pallas_call | solution.py:1451
  231.3 137.9 %scatter_gradients.1 = (f32[4,40,768]{2,1,0:T(8,128)}, f32[96,1344]{1,0:T(8,128)}, f32[120,768]{1,0:T(8,128)}, f32[4,24,512]{2,1,0:T(8,128)}, f32[64,896]{1,0:T(...) custom-call(bf16[4,2,2,2,40,768]{5,4,3,2,1,0:T(8,128)(2,1)} %bitcast.26, ...), custom_call_target="tpu_custom_call" | custom-call | bytes 46530560 | tf_op jit(solution)/shard_map/scatter_gradients/pallas_call | solution.py:538
  369.2 7.9 %apply_update.1 = (f32[160,768]{1,0:T(8,128)}, f32[96,1,1344]{2,1,0:T(1,128)}, f32[1,120,768]{2,1,0:T(8,128)}, f32[96,512]{1,0:T(8,128)}, f32[64,1,896]{2,1,0:T(...) custom-call(f32[160,768]{1,0:T(8,128)} %bitcast.30, ...), custom_call_target="tpu_custom_call" | custom-call | tf_op jit(solution)/shard_map/apply_update/pallas_call | solution.py:619

commit v7 on v6

--- a/solution.py
+++ b/solution.py
@@ -244,14 +244,23 @@
 
 def scatter_kernel(shapes, units, *refs):
     grads = refs[:7]
-    masters, firsts, seconds = refs[7:14], refs[14:21], refs[21:28]
-    outs = refs[28:36]
+    sources, results = refs[7:28], refs[28:36]
     refs = refs[36:]
     n = len(units)
     own, one, two, three, four = (refs[k * n : (k + 1) * n] for k in range(5))
     vec_one, vec_two, vec_three, vec_four, vec_sum = refs[5 * n : 5 * n + 5]
     stats, stat_one, stat_four = refs[5 * n + 5 : 5 * n + 8]
-    send, recv, local, vsend, vrecv, tsend, trecv, ssend, srecv = refs[5 * n + 8 :]
+    send, recv, local, vsend, vrecv, tsend, trecv, ssend, srecv = refs[5 * n + 8 : 5 * n + 17]
+    refs = refs[5 * n + 17 :]
+    held, outs, loaded, stored = refs[:21], refs[21:28] + results[7:], *refs[28:]
+    masters, firsts, seconds = held[:7], held[7:14], held[14:]
+    state_copies = [
+        pltpu.make_async_copy(source, target, loaded.at[at])
+        for at, (source, target) in enumerate(zip(sources, held))
+    ]
+    for copy in state_copies:
+        copy.start()
+    stores = []
     z, x, y, c = place()
     every = slice(None)
     copies = {}
@@ -259,6 +268,10 @@
     stat_lane = lax.broadcasted_iota(jnp.int32, (8, 128), 1)
 
     def tally(array):
+        stores.append(pltpu.make_async_copy(outs[array], results[array], stored.at[array]))
+        stores[-1].start()
+        for kind in range(3):
+            state_copies[7 * kind + array].wait()
         if array == VEC:
             gradient = outs[VEC][:7, : masters[VEC].shape[1]]
             update = moments(
@@ -423,19 +436,19 @@
             for stage in (3, 4, 5):
                 copies[number, stage].wait()
             add(number, 3)
-        if tick < 4:
-            if tick == 0:
-                vec_sum[...] = grads[6][...]
-            if tick < 3:
-                remote(vec_sum.at[...], vec_dst[tick], ("v", tick), vsend.at[tick], vrecv.at[tick], vec_peer[tick])
-            else:
-                vec_four[z] = vec_sum[...]
-                for m in (1, 2, 3):
-                    remote(vec_sum.at[...], vec_four.at[z], ("v", 2 + m), vsend.at[2 + m], vrecv.at[2 + m], device(flip(z, m), x, y, c))
+        if tick == 0:
+            vec_sum[...] = grads[6][...]
+        if 1 <= tick <= 3:
+            copies["v", tick - 1].wait()
+            vec_sum[...] = vec_sum[...] + vec_dst[tick - 1][...]
         if tick < 3:
-            copies["v", tick].wait()
-            vec_sum[...] = vec_sum[...] + vec_dst[tick][...]
-        if tick == 4:
+            remote(vec_sum, vec_dst[tick], ("v", tick), vsend.at[tick], vrecv.at[tick], vec_peer[tick])
+        elif tick == 3:
+            vec_four[z] = vec_sum[...]
+            for m in (1, 2, 3):
+                peer = device(flip(z, m), x, y, c)
+                remote(vec_sum, vec_four.at[z], ("v", 2 + m), vsend.at[2 + m], vrecv.at[2 + m], peer)
+        elif tick == 4:
             for m in (1, 2, 3):
                 copies["v", 2 + m].wait()
             vec_sum[...] = (vec_four[0] + vec_four[1]) + (vec_four[2] + vec_four[3])
@@ -493,6 +506,8 @@
     outs[7][...] = jnp.where(stat_row == 2, loss, norms)
     for number in range(n):
         copies[number, 0].wait_send()
+    for store in stores:
+        store.wait()
 
 
 def scatter_gradients(grads, masters, firsts, seconds):
@@ -534,13 +549,17 @@
         pltpu.SemaphoreType.DMA((11,)),
         pltpu.SemaphoreType.DMA((11,)),
     ]
+    states = [*masters, *firsts, *seconds]
+    scratch += [pltpu.VMEM(member.shape, f32) for member in states + outs[:7]]
+    scratch += [pltpu.SemaphoreType.DMA((21,)), pltpu.SemaphoreType.DMA((7,))]
+    in_vmem = pl.BlockSpec(memory_space=pltpu.VMEM)
+    anywhere = pl.BlockSpec(memory_space=pl.ANY)
     total = sum(int(grad.size) * grad.dtype.itemsize for grad in grads)
     return pl.pallas_call(
         functools.partial(scatter_kernel, shapes, units),
         out_shape=outs,
-        in_specs=[pl.BlockSpec(memory_space=pl.ANY)] * 6
-        + [pl.BlockSpec(memory_space=pltpu.VMEM)] * 22,
-        out_specs=[pl.BlockSpec(memory_space=pltpu.VMEM)] * 8,
+        in_specs=[anywhere] * 6 + [in_vmem] + [anywhere] * 21,
+        out_specs=[anywhere] * 7 + [in_vmem],
         scratch_shapes=scratch,
         compiler_params=pltpu.CompilerParams(
             collective_id=1, has_side_effects=True, vmem_limit_bytes=60 * 1024 * 1024
@@ -1120,6 +1139,13 @@
         refs = refs[23:]
         wholes = dict(zip((PIX, EIN, EOUT, BRI), wholes))
     loaded, flushed = refs[:2]
+    first_copies = []
+    if ring:
+        shards, states_loaded, refs = refs[2:9], refs[9], refs[:2] + refs[10:]
+        for at, (source, target) in enumerate(zip(masters, shards)):
+            first_copies.append(pltpu.make_async_copy(source, target, states_loaded.at[at]))
+            first_copies[-1].start()
+        masters = shards
     eight, pixels_here, stream, w_in, w_out, embed, bridge = refs[2:9]
     retained, unit, inverse, low = refs[9:13]
     saved = refs[13:24]
@@ -1191,6 +1217,8 @@
             copy.start()
             flushes.append(copy)
 
+    for copy in first_copies:
+        copy.wait()
     if ring:
         for array in range(6):
             if array in SHARED:
@@ -1320,7 +1348,7 @@
         shapes.append((8, 256))
         types = [bf16] * 6 + [f32]
         operands = [images, *indices, table, *weights]
-        in_specs += [in_vmem] * 7
+        in_specs += [anywhere] * 7
         gathered = [(whole_shape(k, shape), types[k]) for k, shape in enumerate(shapes)]
         outs = gathered + [((8, shapes_total(weights[VEC])), f32)] + outs
         out_specs = [anywhere] * 7 + [in_vmem] + out_specs
@@ -1346,6 +1374,9 @@
         params = {}
         w_shapes = [weights[EIN].shape, weights[EOUT].shape]
     scratch += [pltpu.SemaphoreType.DMA((8,)), pltpu.SemaphoreType.DMA((15,))]
+    if ring:
+        scratch += [pltpu.VMEM(member.shape, f32) for member in weights]
+        scratch += [pltpu.SemaphoreType.DMA((7,))]
     buffers = [
         ((images.shape[0], 8, images.shape[2]), bf16),
         (picture_shape, bf16),

time: 378 us -> 372 us (0.984)
  Pallas kernels: 376 us -> 371 us
    pallas_call x1, Pallas kernels: 138 us -> 132 us  [scatter_gradients(): pl.pallas_call(functools.partial(scatter_kernel, shapes, units), out_shap...]
where the time goes in v7:
time: 372 us
  Pallas kernels  371 us (100%)
    pallas_call x1, Pallas kernels, scatter_gradients(): pl.pallas_call(functools.partial(scatter_kernel, shapes, units), out_shap...  132 us
    pallas_call x1, Pallas kernels, encode(): pl.pallas_call(functools.partial(encode_kernel, ring), out_shape=[jax.Sha...  131 us
    pallas_call x1, Pallas kernels, decoder_step(): pl.pallas_call(decoder_kernel, out_shape=outs, in_specs=[in_vmem, in_vmem...  73.6 us
    pallas_call x1, Pallas kernels, encoder_backward(): pl.pallas_call(encoder_backward_kernel, out_shape=outs, in_specs=[in_vmem...  26.5 us
    pallas_call x1, Pallas kernels, apply_update(): pl.pallas_call(apply_kernel, out_shape=shapes * 3 + [jax.ShapeDtypeStruct...  7.91 us

profile of v7, /device:TPU:0, one launch (start us, length us, event | category | flops | bytes accessed | tf_op | source)
XLA Modules:
  0.0 371.9 jit_solution(1095220710649800079)
XLA Ops:
  0.7 131.0 %gather_encode.1 = (bf16[4,2,2,2,40,768]{5,4,3,2,1,0:T(8,128)(2,1)}, bf16[2,2,4,2,96,1344]{5,4,3,2,1,0:T(8,128)(2,1)}, bf16[2,2,4,2,120,768]{5,4,3,2,1,0:T(8,128...) custom-call(bf16[196,16,768]{2,1,0:T(8,128)(2,1)} %bitcast.21, ...), custom_call_target="tpu_custom_call" | custom-call | tf_op jit(solution)/shard_map/gather_encode/pallas_call | solution.py:1391
  131.7 73.6 %decoder_step.1 = (bf16[4,512,896]{2,1,0:T(8,128)(2,1)}, bf16[4,640,512]{2,1,0:T(8,128)(2,1)}, bf16[512,768]{1,0:T(8,128)(2,1)}, bf16[4,64,512]{2,1,0:T(8,128)(2,1)}, f32[8,512]{1,0:T(8,128)}) custom-call(f32[4,64,512]{2,1,0:T(8,128)} %get-tuple-element.89.refs_0_, s32[4,8,256]{2,1,0:T(8,128)} %get-tuple-element.90.refs_1_, ...), custom_call_target="tpu_custom_call" | custom-call | tf_op jit(solution)/shard_map/decoder_step/pallas_call | solution.py:1110
  205.3 26.5 %encoder_backward.1 = (bf16[4,768,1344]{2,1,0:T(8,128)(2,1)}, bf16[4,960,768]{2,1,0:T(8,128)(2,1)}, bf16[768,512]{1,0:T(8,128)(2,1)}, bf16[1280,768]{1,0:T(8,128)(2,1)}, f32[8,8,256]{2,1,0:T(8,128)}) custom-call(bf16[4,64,512]{2,1,0:T(8,128)(2,1)} %get-tuple-element.96.refs_0_, bf16[256,768]{1,0:T(8,128)(2,1)} %get-tuple-element.97.refs_1_, ...), custom_call_target="tpu_custom_call" | custom-call | tf_op jit(solution)/shard_map/encoder_backward/pallas_call | solution.py:1482
  231.8 132.0 %scatter_gradients.1 = (f32[4,40,768]{2,1,0:T(8,128)}, f32[96,1344]{1,0:T(8,128)}, f32[120,768]{1,0:T(8,128)}, f32[4,24,512]{2,1,0:T(8,128)}, f32[64,896]{1,0:T(...) custom-call(bf16[4,2,2,2,40,768]{5,4,3,2,1,0:T(8,128)(2,1)} %bitcast.26, ...), custom_call_target="tpu_custom_call" | custom-call | bytes 46530560 | tf_op jit(solution)/shard_map/scatter_gradients/pallas_call | solution.py:558
  363.8 7.9 %apply_update.1 = (f32[160,768]{1,0:T(8,128)}, f32[96,1,1344]{2,1,0:T(1,128)}, f32[1,120,768]{2,1,0:T(8,128)}, f32[96,512]{1,0:T(8,128)}, f32[64,1,896]{2,1,0:T(...) custom-call(f32[160,768]{1,0:T(8,128)} %bitcast.30, ...), custom_call_target="tpu_custom_call" | custom-call | tf_op jit(solution)/shard_map/apply_update/pallas_call | solution.py:638

commit v8 on v7

--- a/solution.py
+++ b/solution.py
@@ -430,7 +430,7 @@
         for number in step_units(tick - 3):
             copies[number, 2].wait()
             add(number, 2)
-            for stage in (3, 4, 5):
+            for stage in (5, 4, 3):
                 start(number, stage)
         for number in step_units(tick - 4):
             for stage in (3, 4, 5):
@@ -825,7 +825,7 @@
                 jnp.exp(-0.5 * hidden * hidden) * (0.5 / np.pi) ** 0.5
             )
 
-        row_loop(count, 32, bend)
+        row_loop(count, 64, bend)
         stream[...] = stream[...] + dot(active[t], down)
 
     half = GROUPS // 2 if dims["spans"] == 1 else GROUPS

time: 372 us -> 372 us (level)
  no operation moved by 1% of the time
where the time goes in v8:
time: 372 us; the launch traced here: 371 us
  Pallas kernels  371 us (100%)
    pallas_call x1, Pallas kernels, scatter_gradients(): pl.pallas_call(functools.partial(scatter_kernel, shapes, units), out_shap...  132 us
    pallas_call x1, Pallas kernels, encode(): pl.pallas_call(functools.partial(encode_kernel, ring), out_shape=[jax.Sha...  131 us
    pallas_call x1, Pallas kernels, decoder_step(): pl.pallas_call(decoder_kernel, out_shape=outs, in_specs=[in_vmem, in_vmem...  72.9 us
    pallas_call x1, Pallas kernels, encoder_backward(): pl.pallas_call(encoder_backward_kernel, out_shape=outs, in_specs=[in_vmem...  26.5 us
    pallas_call x1, Pallas kernels, apply_update(): pl.pallas_call(apply_kernel, out_shape=shapes * 3 + [jax.ShapeDtypeStruct...  7.91 us

profile of v8, /device:TPU:0, one launch (start us, length us, event | category | flops | bytes accessed | tf_op | source)
XLA Modules:
  0.0 371.4 jit_solution(461591560097103135)
XLA Ops:
  0.7 131.0 %gather_encode.1 = (bf16[4,2,2,2,40,768]{5,4,3,2,1,0:T(8,128)(2,1)}, bf16[2,2,4,2,96,1344]{5,4,3,2,1,0:T(8,128)(2,1)}, bf16[2,2,4,2,120,768]{5,4,3,2,1,0:T(8,128...) custom-call(bf16[196,16,768]{2,1,0:T(8,128)(2,1)} %bitcast.21, ...), custom_call_target="tpu_custom_call" | custom-call | tf_op jit(solution)/shard_map/gather_encode/pallas_call | solution.py:1391
  131.6 72.9 %decoder_step.1 = (bf16[4,512,896]{2,1,0:T(8,128)(2,1)}, bf16[4,640,512]{2,1,0:T(8,128)(2,1)}, bf16[512,768]{1,0:T(8,128)(2,1)}, bf16[4,64,512]{2,1,0:T(8,128)(2,1)}, f32[8,512]{1,0:T(8,128)}) custom-call(f32[4,64,512]{2,1,0:T(8,128)} %get-tuple-element.89.refs_0_, s32[4,8,256]{2,1,0:T(8,128)} %get-tuple-element.90.refs_1_, ...), custom_call_target="tpu_custom_call" | custom-call | tf_op jit(solution)/shard_map/decoder_step/pallas_call | solution.py:1110
  204.6 26.5 %encoder_backward.1 = (bf16[4,768,1344]{2,1,0:T(8,128)(2,1)}, bf16[4,960,768]{2,1,0:T(8,128)(2,1)}, bf16[768,512]{1,0:T(8,128)(2,1)}, bf16[1280,768]{1,0:T(8,128)(2,1)}, f32[8,8,256]{2,1,0:T(8,128)}) custom-call(bf16[4,64,512]{2,1,0:T(8,128)(2,1)} %get-tuple-element.96.refs_0_, bf16[256,768]{1,0:T(8,128)(2,1)} %get-tuple-element.97.refs_1_, ...), custom_call_target="tpu_custom_call" | custom-call | tf_op jit(solution)/shard_map/encoder_backward/pallas_call | solution.py:1482
  231.1 132.2 %scatter_gradients.1 = (f32[4,40,768]{2,1,0:T(8,128)}, f32[96,1344]{1,0:T(8,128)}, f32[120,768]{1,0:T(8,128)}, f32[4,24,512]{2,1,0:T(8,128)}, f32[64,896]{1,0:T(...) custom-call(bf16[4,2,2,2,40,768]{5,4,3,2,1,0:T(8,128)(2,1)} %bitcast.26, ...), custom_call_target="tpu_custom_call" | custom-call | bytes 46530560 | tf_op jit(solution)/shard_map/scatter_gradients/pallas_call | solution.py:558
  363.3 7.9 %apply_update.1 = (f32[160,768]{1,0:T(8,128)}, f32[96,1,1344]{2,1,0:T(1,128)}, f32[1,120,768]{2,1,0:T(8,128)}, f32[96,512]{1,0:T(8,128)}, f32[64,1,896]{2,1,0:T(...) custom-call(f32[160,768]{1,0:T(8,128)} %bitcast.30, ...), custom_call_target="tpu_custom_call" | custom-call | tf_op jit(solution)/shard_map/apply_update/pallas_call | solution.py:638

commit v9 on v7

--- a/solution.py
+++ b/solution.py
@@ -664,7 +664,7 @@
 
 GROUPS = 4
 ENC = dict(step=128, first=0, images=4, block=64, tokens=50, width=768, heads=3, head=64, hidden=768, spans=1)
-DEC = dict(step=208, first=768, images=4, block=208, tokens=197, width=512, heads=4, head=32, hidden=512, spans=4)
+DEC = dict(step=416, first=768, images=4, block=208, tokens=197, width=512, heads=4, head=32, hidden=512, spans=4)
 CLASS_ROW = 49
 MASK_ROW = 50
 

time: 372 us -> 371 us (level)
  no operation moved by 1% of the time
where the time goes in v9:
time: 371 us
  Pallas kernels  370 us (100%)
    pallas_call x1, Pallas kernels, scatter_gradients(): pl.pallas_call(functools.partial(scatter_kernel, shapes, units), out_shap...  132 us
    pallas_call x1, Pallas kernels, encode(): pl.pallas_call(functools.partial(encode_kernel, ring), out_shape=[jax.Sha...  131 us
    pallas_call x1, Pallas kernels, decoder_step(): pl.pallas_call(decoder_kernel, out_shape=outs, in_specs=[in_vmem, in_vmem...  72.4 us
    pallas_call x1, Pallas kernels, encoder_backward(): pl.pallas_call(encoder_backward_kernel, out_shape=outs, in_specs=[in_vmem...  26.5 us
    pallas_call x1, Pallas kernels, apply_update(): pl.pallas_call(apply_kernel, out_shape=shapes * 3 + [jax.ShapeDtypeStruct...  7.91 us

profile of v9, /device:TPU:0, one launch (start us, length us, event | category | flops | bytes accessed | tf_op | source)
XLA Modules:
  0.0 370.7 jit_solution(14343075667647591894)
XLA Ops:
  0.7 131.0 %gather_encode.1 = (bf16[4,2,2,2,40,768]{5,4,3,2,1,0:T(8,128)(2,1)}, bf16[2,2,4,2,96,1344]{5,4,3,2,1,0:T(8,128)(2,1)}, bf16[2,2,4,2,120,768]{5,4,3,2,1,0:T(8,128...) custom-call(bf16[196,16,768]{2,1,0:T(8,128)(2,1)} %bitcast.21, ...), custom_call_target="tpu_custom_call" | custom-call | tf_op jit(solution)/shard_map/gather_encode/pallas_call | solution.py:1391
  131.7 72.4 %decoder_step.1 = (bf16[4,512,896]{2,1,0:T(8,128)(2,1)}, bf16[4,640,512]{2,1,0:T(8,128)(2,1)}, bf16[512,768]{1,0:T(8,128)(2,1)}, bf16[4,64,512]{2,1,0:T(8,128)(2,1)}, f32[8,512]{1,0:T(8,128)}) custom-call(f32[4,64,512]{2,1,0:T(8,128)} %get-tuple-element.89.refs_0_, s32[4,8,256]{2,1,0:T(8,128)} %get-tuple-element.90.refs_1_, ...), custom_call_target="tpu_custom_call" | custom-call | tf_op jit(solution)/shard_map/decoder_step/pallas_call | solution.py:1110
  204.2 26.5 %encoder_backward.1 = (bf16[4,768,1344]{2,1,0:T(8,128)(2,1)}, bf16[4,960,768]{2,1,0:T(8,128)(2,1)}, bf16[768,512]{1,0:T(8,128)(2,1)}, bf16[1280,768]{1,0:T(8,128)(2,1)}, f32[8,8,256]{2,1,0:T(8,128)}) custom-call(bf16[4,64,512]{2,1,0:T(8,128)(2,1)} %get-tuple-element.96.refs_0_, bf16[256,768]{1,0:T(8,128)(2,1)} %get-tuple-element.97.refs_1_, ...), custom_call_target="tpu_custom_call" | custom-call | tf_op jit(solution)/shard_map/encoder_backward/pallas_call | solution.py:1482
  230.7 131.9 %scatter_gradients.1 = (f32[4,40,768]{2,1,0:T(8,128)}, f32[96,1344]{1,0:T(8,128)}, f32[120,768]{1,0:T(8,128)}, f32[4,24,512]{2,1,0:T(8,128)}, f32[64,896]{1,0:T(...) custom-call(bf16[4,2,2,2,40,768]{5,4,3,2,1,0:T(8,128)(2,1)} %bitcast.26, ...), custom_call_target="tpu_custom_call" | custom-call | bytes 46530560 | tf_op jit(solution)/shard_map/scatter_gradients/pallas_call | solution.py:558
  362.6 7.9 %apply_update.1 = (f32[160,768]{1,0:T(8,128)}, f32[96,1,1344]{2,1,0:T(1,128)}, f32[1,120,768]{2,1,0:T(8,128)}, f32[96,512]{1,0:T(8,128)}, f32[64,1,896]{2,1,0:T(...) custom-call(f32[160,768]{1,0:T(8,128)} %bitcast.30, ...), custom_call_target="tpu_custom_call" | custom-call | tf_op jit(solution)/shard_map/apply_update/pallas_call | solution.py:638
